TPU v7x, 32 devices: a whole 2x2x4 slice. The times are simulated.
32 devices in a mesh: tm: 4 (over y, x), beam: 8 (over z, core).
Axes of the slice: x: 2, y: 2, z: 4, core: 2. Of those that a mesh axis runs over, the one named last changes fastest.
Arguments:
- element_signals: bfloat16 [2, 2048, 4096], P(None, None, ('tm', 'beam')), may hold values from -6 to 6
- beam_weights: bfloat16 [2, 1024, 2048], P(None, ('tm', 'beam')), may hold values from -0.09375 to 0.09375
- beam_order: int32 [1024], replicated, may hold values from 0 to 1023, as said below
- neighbours: int32 [1024, 6], replicated, may hold values from 0 to 1024, as said below
- leakage: bfloat16 [2, 1024, 6], replicated, may hold values from -1.5 to 1.5
- noise_var: float32 [1024], replicated, may hold values from 0.5 to 2
- bit_labels: int32 [16], replicated, may hold values from 0 to 15, each once
Outputs:
- llr: bfloat16 [4, 1024, 4096], P(None, 'beam', 'tm')
Inputs may be any that keep to these rules, and one draw needn't show every extreme that they name: `beam_order`: A permutation of the 1024 beams. Position p lies in row p // 16 and column p % 16 of a hexagonal grid of 64 rows in which odd rows sit half a cell to the right. `neighbours`: row b lists the beams in the grid cells adjacent to beam b's cell (up to six, each once) and 1024 in the remaining slots. `bit_labels`: each label once.
All inputs are finite; a program needn't handle non-finite values.
Results may differ from a plain program's by a relative error of at most 0.0063.
Values may be sent and summed in bfloat16 or wider, within the bound.
No kernel may reach another device: no remote copies, remote signals or barrier semaphores. Data moves between devices by JAX's collectives and lax.ppermute only.
A program may use at most 128 MiB of HBM per device.

v0:
```python
import math

import jax
import jax.numpy as jnp
from jax import lax
from jax.sharding import PartitionSpec as P

COLS = 16


LEVEL = 0.31622776601683794
HUGE = 1e30


def as_sent(value):
    return jax.tree.map(lambda a: a.astype(jnp.bfloat16) if a.dtype == jnp.float32 else a, value)


def with_halo(value, sides, width):
    for axis, dim in sides:
        devices, length = (lax.axis_size(axis), value.shape[dim])
        up = [(i, (i + 1) % devices) for i in range(devices - 1)]
        down = [(j, i) for i, j in up]
        last = lax.slice_in_dim(value, length - width, length, axis=dim)
        leading = lax.slice_in_dim(value, 0, width, axis=dim)
        before = lax.ppermute(last, axis, up)
        after = lax.ppermute(leading, axis, down)
        value = jnp.concatenate([before, value, after], axis=dim)
    return value


def label_table(bit_labels):
    powers = jnp.array([1, 2, 4, 8], jnp.int32)
    return bit_labels[:, None] // powers[None, :] % 2 == 1


def point_arrays():
    points = jnp.arange(16, dtype=jnp.int32)
    real_values = (2 * (points // 4) - 3).astype(jnp.float32) * LEVEL
    imaginary_values = (2 * (points % 4) - 3).astype(jnp.float32) * LEVEL
    return (real_values, imaginary_values)


def metric_block(field_real, field_imaginary, variance, table):
    real_values, imaginary_values = point_arrays()
    distance = (field_real[None] - real_values[:, None, None]) ** 2 + (
        field_imaginary[None] - imaginary_values[:, None, None]
    ) ** 2
    result = []
    for bit in range(4):
        chosen = table[:, bit][:, None, None]
        lowest_one = jnp.min(jnp.where(chosen, distance, HUGE), axis=0)
        lowest_zero = jnp.min(jnp.where(chosen, HUGE, distance), axis=0)
        result.append((lowest_one - lowest_zero) / variance)
    return jnp.stack(result)


def soft_block(field_real, field_imaginary, variance, table):
    real_values, imaginary_values = point_arrays()
    chance = jax.nn.sigmoid(metric_block(field_real, field_imaginary, variance, table))
    factors = jnp.where(table[:, :, None, None], 1.0 - chance[None], chance[None])
    weight = jnp.prod(factors, axis=1)
    total_real = jnp.sum(real_values[:, None, None] * weight, axis=0)
    total_imaginary = jnp.sum(imaginary_values[:, None, None] * weight, axis=0)
    return jnp.stack([total_real, total_imaginary]).astype(jnp.bfloat16)


def by_columns(method, field_real, field_imaginary, variance, table):
    rows, columns = field_real.shape
    size = math.gcd(columns, 2048)
    count = columns // size
    split_real = jnp.transpose(field_real.reshape(rows, count, size), (1, 0, 2))
    split_imaginary = jnp.transpose(field_imaginary.reshape(rows, count, size), (1, 0, 2))
    result = lax.map(
        lambda pair: method(pair[0], pair[1], variance, table), (split_real, split_imaginary)
    )
    return jnp.transpose(result, (1, 2, 0, 3)).reshape(result.shape[1], rows, columns)


def soft_symbols(field_real, field_imaginary, variance, table):
    return by_columns(soft_block, field_real, field_imaginary, variance, table)


def cross_terms(matrix, soft):
    cross_real = jnp.dot(matrix[0], soft[0], preferred_element_type=jnp.float32) - jnp.dot(
        matrix[1], soft[1], preferred_element_type=jnp.float32
    )
    cross_imaginary = jnp.dot(matrix[0], soft[1], preferred_element_type=jnp.float32) + jnp.dot(
        matrix[1], soft[0], preferred_element_type=jnp.float32
    )
    return (cross_real, cross_imaginary)


def on_device(
    element_signals, beam_weights, beam_order, neighbours, leakage, noise_var, bit_labels
):
    count_beams = beam_order.shape[0]
    tile_rows = count_beams // lax.axis_size("beam")
    margin = COLS
    table = label_table(bit_labels)
    group_rows = lax.all_gather(beam_weights, "beam", axis=1, tiled=True)
    piece = lax.all_gather(group_rows, "tm", axis=1, tiled=True)
    real_part = jnp.dot(piece[0], element_signals[0], preferred_element_type=jnp.float32) - jnp.dot(
        piece[1], element_signals[1], preferred_element_type=jnp.float32
    )
    imaginary_part = jnp.dot(
        piece[0], element_signals[1], preferred_element_type=jnp.float32
    ) + jnp.dot(piece[1], element_signals[0], preferred_element_type=jnp.float32)
    beams = jnp.stack([real_part, imaginary_part]).astype(jnp.bfloat16)
    ordered = jnp.take(beams, beam_order, axis=1)
    tiled = lax.all_to_all(ordered, "beam", split_axis=1, concat_axis=2, tiled=True)
    first = lax.axis_index("beam") * tile_rows
    position_of = (
        jnp.zeros((count_beams,), jnp.int32)
        .at[beam_order]
        .set(jnp.arange(count_beams, dtype=jnp.int32))
    )
    rows = first + jnp.arange(tile_rows, dtype=jnp.int32)
    inside = (rows >= 0) & (rows < count_beams)
    beam_ids = jnp.take(beam_order, jnp.clip(rows, 0, count_beams - 1))
    near = jnp.take(neighbours, beam_ids, axis=0)
    present = (near < count_beams) & inside[:, None]
    column = jnp.take(position_of, jnp.clip(near, 0, count_beams - 1)) - (first - margin)
    hits = (
        column[:, :, None] == jnp.arange(tile_rows + 2 * margin, dtype=jnp.int32)[None, None, :]
    ) & present[:, :, None]
    weights_near = jnp.take(leakage, beam_ids, axis=1).astype(jnp.float32)
    matrix = jnp.sum(jnp.where(hits[None], weights_near[:, :, :, None], 0.0), axis=2)
    own_matrix = matrix.astype(jnp.bfloat16)
    own_variance = jnp.take(noise_var, beam_ids)[:, None]
    field_real = tiled[0].astype(jnp.float32)
    field_imaginary = tiled[1].astype(jnp.float32)
    for section in range(2):
        soft = soft_symbols(field_real, field_imaginary, own_variance, table)
        padded = with_halo(as_sent(soft), (("beam", 1),), margin).astype(soft.dtype)
        cross_real, cross_imaginary = cross_terms(own_matrix, padded)
        field_real = tiled[0].astype(jnp.float32) - cross_real
        field_imaginary = tiled[1].astype(jnp.float32) - cross_imaginary
    metrics = by_columns(metric_block, field_real, field_imaginary, own_variance, table)
    return metrics.astype(jnp.bfloat16)


def solution(mesh):
    in_specs = (
        P(None, None, ("tm", "beam")),
        P(None, ("tm", "beam"), None),
        P(),
        P(),
        P(),
        P(),
        P(),
    )
    out_specs = P(None, "beam", "tm")
    return jax.shard_map(
        on_device, mesh=mesh, in_specs=in_specs, out_specs=out_specs, check_vma=False
    )
```

profile of v0, /device:TPU:0, one launch (start us, length us, event | category | flops | bytes accessed | tf_op | source)
XLA Modules:
  0.0 237.0 jit_solution(5661304931235452964)
XLA Ops:
  7.3 33.5 %all-gather.3.cloned.1.call-done = bf16[2,256,2048]{2,1,0:T(8,128)(2,1)} async-done(((bf16[2,32,2048]{2,1,0:T(8,128)(2,1)}), bf16[2,256,2048]{2,1,0:T(8,128)(2,1)}) %all-gather.3.cloned.1.call-update) | async-done | bytes 2097168 | tf_op jit(solution)/shard_map/all_gather | solution.py:101
  40.8 1.0 copy.30
  41.8 1.6 gather_fusion.1
  43.5 1.0 gather_fusion.5
  45.4 1.2 copy.33
  48.0 0.9 fusion.40
  50.5 79.3 %all-gather.5.cloned.1.call-done = bf16[2,1024,2048]{2,1,0:T(8,128)(2,1)} async-done(((bf16[2,256,2048]{2,1,0:T(8,128)(2,1)}), bf16[2,1024,2048]{2,1,0:T(8,128)(2,1)}) %all-gather.5.cloned.1.call-update) | async-done | bytes 8388624 | tf_op jit(solution)/shard_map/all_gather | solution.py:102
  129.8 3.7 %fusion = f32[1024,128]{1,0:T(8,128)S(1)} fusion(bf16[2,1024,2048]{2,1,0:T(8,128)(2,1)} %all-gather.5.cloned.1.call-done, bf16[2,2048,128]{2,1,0:T(8,128)(2,1)} %param.8), kind=kOutput, calls=%fused_computation.42 | convolution fusion | flops 536870912 | bytes 5242880 | tf_op jit(solution)/shard_map/dot_general | solution.py:106
  133.5 1.1 copy-done.2
  134.6 1.2 fusion.1
  135.8 1.3 fusion.19
  137.1 1.3 fusion.18
  139.0 3.7 %gather_fusion = bf16[1024,2,128]{2,1,0:T(2,128)(2,1)S(1)} fusion(bf16[2,1024,128]{2,0,1:T(2,128)(2,1)S(1)} %copy.28, s32[1024]{0:T(1024)S(1)} %get-tuple-element.118), kind=kCustom, calls=%fused_computation | custom fusion | bytes 1052672 | tf_op jit(solution)/shard_map/jit(_take)/gather | solution.py:110
  142.7 4.4 %fusion.28 = bf16[2,1024,128]{2,0,1:T(2,128)(2,1)} fusion(bf16[1024,2,128]{2,1,0:T(2,128)(2,1)S(1)} %gather_fusion, pred[1024]{0:T(1024)(128)(4,1)S(1)} %compare_and_fusion.1), kind=kLoop, calls=%fused_computation.99 | loop fusion | flops 262144 | bytes 1049600 | tf_op jit(solution)/shard_map/jit(_take)/select_n | solution.py:110
  147.1 4.6 %all-to-all-start = ((bf16[2,1024,128]{2,0,1:T(2,128)(2,1)}), bf16[2,1024,128]{2,0,1:T(2,128)(2,1)S(1)}, u32[]{:S(2)}, u32[]{:S(2)}) async-start(bf16[2,1024,128]{2,0,1:T(2,128)(2,1)} %fusion.28), calls=%async_computation | async-start | bytes 1048576 | tf_op jit(solution)/shard_map/all_to_all | solution.py:111
  151.9 4.5 %scatter_custom_fusion = s32[1024]{0:T(1024)S(1)} fusion(s32[1024]{0:T(1024)S(1)} %get-tuple-element.117, s32[1024]{0:T(1024)S(1)} %iota.55, s32[]{:T(128)} %constant.228.clone.1), kind=kCustom, calls=%fused_computation.150 | custom fusion | bytes 4100 | tf_op jit(solution)/shard_map/scatter | solution.py:116
  156.4 3.2 %gather_fusion.3 = s32[768]{0:T(1024)S(1)} fusion(s32[1024]{0:T(1024)S(1)} %scatter_custom_fusion, s32[1024]{0:T(1024)S(1)} %pad_clamp_fusion), kind=kCustom, calls=%fused_computation.3 | custom fusion | bytes 9216 | tf_op jit(solution)/shard_map/jit(_take)/gather | solution.py:123
  160.1 7.0 %all-to-all-done = bf16[2,1024,128]{2,0,1:T(2,128)(2,1)S(1)} async-done(((bf16[2,1024,128]{2,0,1:T(2,128)(2,1)}), bf16[2,1024,128]{2,0,1:T(2,128)(2,1)S(1)}, u32[]{:S(2)}, u32[]{:S(2)}) %all-to-all-start) | async-done | bytes 524320 | tf_op jit(solution)/shard_map/all_to_all | solution.py:111
  167.7 9.0 %select_reduce_fusion.24 = (f32[128,1024]{1,0:T(8,128)S(1)}, f32[128,1024]{1,0:T(8,128)S(1)}, f32[128,1024]{1,0:T(8,128)S(1)}, f32[128,1024]{1,0:T(8,128)S(1)}, ...) fusion(f32[16]{0:T(128)S(1)} %get-tuple-element.137, ...), kind=kLoop, calls=%fused_computation.37 | loop fusion | flops 42991616 | bytes 5243072 | tf_op jit(solution)/shard_map/while/body/eval_jaxpr/reduce_min | solution.py:53
  178.1 7.0 %select_reduce_fusion.1 = f32[16,128,1024]{2,1,0:T(8,128)S(1)} fusion(f32[4,128,1024]{2,1,0:T(8,128)S(1)} %get-tuple-element.108, f32[4,128,1024]{2,1,0:T(8,128)S(1)} %get-tuple-element.107, pred[16,4]{1,0:T(8,128)(4,1)S(1)} %copy.35), kind=kLoop, calls=%fused_computation.8 | loop fusion | flops 14680064 | bytes 12582976 | tf_op jit(solution)/shard_map/while/body/eval_jaxpr/reduce_prod | solution.py:62
  185.1 1.2 multiply_reduce_fusion.3
  186.3 1.5 collective-permute-start
  187.9 1.5 collective-permute-start.1
  189.5 1.5 collective-permute-done.1
  192.1 9.0 %select_reduce_fusion.16 = (f32[128,1024]{1,0:T(8,128)S(1)}, f32[128,1024]{1,0:T(8,128)S(1)}, f32[128,1024]{1,0:T(8,128)S(1)}, f32[128,1024]{1,0:T(8,128)S(1)}, ...) fusion(f32[128,1024]{1,0:T(8,128)S(1)} %fusion.12, ...), kind=kLoop, calls=%fused_computation.26 | loop fusion | flops 42991616 | bytes 5243072 | tf_op jit(solution)/shard_map/while/body/eval_jaxpr/reduce_min | solution.py:53
  202.5 7.0 %select_reduce_fusion = f32[16,128,1024]{2,1,0:T(8,128)S(1)} fusion(f32[4,128,1024]{2,1,0:T(8,128)S(1)} %get-tuple-element.106, f32[4,128,1024]{2,1,0:T(8,128)S(1)} %get-tuple-element.105, pred[16,4]{1,0:T(8,128)(4,1)S(1)} %copy.35), kind=kLoop, calls=%fused_computation.7 | loop fusion | flops 14680064 | bytes 12582976 | tf_op jit(solution)/shard_map/while/body/eval_jaxpr/reduce_prod | solution.py:62
  209.6 1.2 multiply_reduce_fusion.1
  210.8 4.4 %collective-permute-start.2 = (bf16[2,16,1024]{2,1,0:T(8,128)(2,1)S(1)}, bf16[2,16,1024]{2,1,0:T(8,128)(2,1)S(1)}, u32[]{:S(2)}, u32[]{:S(2)}) collective-permute-start(bf16[2,16,1024]{2,1,0:T(8,128)(2,1)S(1)} %get-tuple-element.111), channel_id=1, source_target_pairs={{0,1},{1,2},{2,3},{3,4},{4,5},{5,6},{6,7},{8,9},{9,10},{10,11},{11... | collective-permute-start | bytes 196616 | tf_op jit(solution)/shard_map/ppermute | solution.py:26
  215.1 1.3 collective-permute-start.3
  216.4 1.8 collective-permute-done.3
  219.4 9.0 %select_reduce_fusion.8 = (f32[128,1024]{1,0:T(8,128)S(1)}, f32[128,1024]{1,0:T(8,128)S(1)}, f32[128,1024]{1,0:T(8,128)S(1)}, f32[128,1024]{1,0:T(8,128)S(1)}, f...) fusion(f32[128,1024]{1,0:T(8,128)S(1)} %fusion.10, ...), kind=kLoop, calls=%fused_computation.15 | loop fusion | flops 42991616 | bytes 5243072 | tf_op jit(solution)/shard_map/while/body/eval_jaxpr/reduce_min | solution.py:53
  229.0 1.1 pad_maximum_fusion
  (62 shorter events, 12.0 us)
Async XLA Ops:
  6.5 37.0 %copy-start = (f32[1024]{0:T(1024)S(1)}, f32[1024]{0:T(1024)}, u32[]{:S(2)}) copy-start(f32[1024]{0:T(1024)} %param.13) | copy-start | bytes 12292
  6.5 126.9 %copy-start.3 = (bf16[2,2048,128]{2,1,0:T(8,128)(2,1)S(1)}, bf16[2,2048,128]{2,1,0:T(8,128)(2,1)}, u32[]{:S(2)}) copy-start(bf16[2,2048,128]{2,1,0:T(8,128)(2,1)} %param.8) | copy-start | bytes 3145732
  6.5 34.3 %all-gather.3.cloned.1.call-start = ((), (), s32[]{:S(2)}) async-start(), calls=%async_computation.1 | async-start | bytes 2359296 | tf_op jit(solution)/shard_map/all_gather | solution.py:101
  7.3 122.5 %all-gather.5.cloned.1.call-start = ((), (), s32[]{:S(2)}) async-start(), calls=%async_computation.2 | async-start | bytes 10485760 | tf_op jit(solution)/shard_map/all_gather | solution.py:102
  129.8 4.8 %copy-start.2 = (bf16[2,1024,2048]{2,1,0:T(8,128)(2,1)S(1)}, bf16[2,1024,2048]{2,1,0:T(8,128)(2,1)}, u32[]{:S(2)}) copy-start(bf16[2,1024,2048]{2,1,0:T(8,128)(2,1)} %all-gather.5.cloned.1.call-done) | copy-start | bytes 25165828
  147.1 20.0 %all-to-all-start = ((bf16[2,1024,128]{2,0,1:T(2,128)(2,1)}), bf16[2,1024,128]{2,0,1:T(2,128)(2,1)S(1)}, u32[]{:S(2)}, u32[]{:S(2)}) async-start(bf16[2,1024,128]{2,0,1:T(2,128)(2,1)} %fusion.28), calls=%async_computation | async-start | bytes 1048576 | tf_op jit(solution)/shard_map/all_to_all | solution.py:111
  186.3 3.2 %collective-permute-start = (bf16[2,16,1024]{2,1,0:T(8,128)(2,1)S(1)}, bf16[2,16,1024]{2,1,0:T(8,128)(2,1)S(1)}, u32[]{:S(2)}, u32[]{:S(2)}) collective-permute-start(bf16[2,16,1024]{2,1,0:T(8,128)(2,1)S(1)} %get-tuple-element.113), channel_id=1, source_target_pairs={{0,1},{1,2},{2,3},{3,4},{4,5},{5,6},{6,7},{8,9},{9,10},{10,11},{11... | collective-permute-start | bytes 196616 | tf_op jit(solution)/shard_map/ppermute | solution.py:26
  187.9 3.1 %collective-permute-start.1 = (bf16[2,16,1024]{2,1,0:T(8,128)(2,1)S(1)}, bf16[2,16,1024]{2,1,0:T(8,128)(2,1)S(1)}, u32[]{:S(2)}, u32[]{:S(2)}) collective-permute-start(bf16[2,16,1024]{2,1,0:T(8,128)(2,1)S(1)} %get-tuple-element.114), channel_id=1, source_target_pairs={{1,0},{2,1},{3,2},{4,3},{5,4},{6,5},{7,6},{9,8},{10,9},{11,10},{12... | collective-permute-start | bytes 196616 | tf_op jit(solution)/shard_map/ppermute | solution.py:27
  210.8 5.7 %collective-permute-start.2 = (bf16[2,16,1024]{2,1,0:T(8,128)(2,1)S(1)}, bf16[2,16,1024]{2,1,0:T(8,128)(2,1)S(1)}, u32[]{:S(2)}, u32[]{:S(2)}) collective-permute-start(bf16[2,16,1024]{2,1,0:T(8,128)(2,1)S(1)} %get-tuple-element.111), channel_id=1, source_target_pairs={{0,1},{1,2},{2,3},{3,4},{4,5},{5,6},{6,7},{8,9},{9,10},{10,11},{11... | collective-permute-start | bytes 196616 | tf_op jit(solution)/shard_map/ppermute | solution.py:26
  215.1 3.1 %collective-permute-start.3 = (bf16[2,16,1024]{2,1,0:T(8,128)(2,1)S(1)}, bf16[2,16,1024]{2,1,0:T(8,128)(2,1)S(1)}, u32[]{:S(2)}, u32[]{:S(2)}) collective-permute-start(bf16[2,16,1024]{2,1,0:T(8,128)(2,1)S(1)} %get-tuple-element.112), channel_id=1, source_target_pairs={{1,0},{2,1},{3,2},{4,3},{5,4},{6,5},{7,6},{9,8},{10,9},{11,10},{12... | collective-permute-start | bytes 196616 | tf_op jit(solution)/shard_map/ppermute | solution.py:27
  218.6 11.6 %copy-start.1 = (f32[1024]{0:T(1024)S(1)}, f32[1024]{0:T(1024)}, u32[]{:S(2)}) copy-start(f32[1024]{0:T(1024)} %param.13) | copy-start | bytes 12292
Sparse Core Ops, SparseCore 0:
  9.0 31.7 all-gather.2
  42.6 87.0 all-gather.4
where the time goes:
time: 239 us; the launch traced here: 237 us
  waiting for transfers between devices  124 us (52%)
  other arithmetic  56 us (23%)
  local copies, waits for them, and re-layouts  20.3 us (8%)
  between operations  13.9 us (6%)
  starting transfers between devices  13.4 us (6%)
  matrix products  9.57 us (4%)
    all_gather x1, waiting for transfers between devices, on_device(): piece = lax.all_gather(group_rows, 'tm', axis=1, tiled=True)  79.3 us
    all_gather x1, waiting for transfers between devices, on_device(): group_rows = lax.all_gather(beam_weights, 'beam', axis=1, tiled=True)  33.5 us
    reduce_min x3, other arithmetic, metric_block(): lowest_zero = jnp.min(jnp.where(chosen, HUGE, distance), axis=0)  27.1 us
    reduce_prod x2, other arithmetic, soft_block(): weight = jnp.prod(factors, axis=1)  14.1 us
    all_to_all x1, waiting for transfers between devices, on_device(): lax.all_to_all(ordered, 'beam', split_axis=1, concat_axis=2, tiled=True)  7.02 us
    ppermute x2, starting transfers between devices, with_halo(): before = lax.ppermute(last, axis, up)  5.9 us
    select_n x2, other arithmetic, on_device(): ordered = jnp.take(beams, beam_order, axis=1)  5.11 us
  transfers between devices with their start and end apart: 7, of which 5 were waited for; matrix products, arithmetic and copies ran while one was open for 8% of the time, Pallas kernels for 0%

commit v1 on v0

v1 whole, which is shorter than its diff:
```python
import functools

import jax
import jax.numpy as jnp
import numpy as np
from jax import lax
from jax.experimental import pallas as pl
from jax.experimental.pallas import tpu as pltpu
from jax.sharding import PartitionSpec as P

COLS = 16
HALO = 2 * COLS
LEVEL = 0.31622776601683794
LANES = 128
MEBI = 1 << 20


def beams_kernel(pieces, groups, steps, *refs):
    weights = refs[:pieces]
    signals = refs[pieces : pieces + groups]
    outs = refs[pieces + groups : pieces + 2 * groups]
    total = refs[-1]
    step = pl.program_id(0)

    @pl.when(step == 0)
    def _():
        total[...] = jnp.zeros_like(total)

    w_real = jnp.concatenate([w[0] for w in weights], axis=0)
    w_imag = jnp.concatenate([w[1] for w in weights], axis=0)
    x_real = jnp.concatenate([x[0] for x in signals], axis=1)
    x_imag = jnp.concatenate([x[1] for x in signals], axis=1)
    dot = functools.partial(jnp.dot, preferred_element_type=jnp.float32)
    total[0] += dot(w_real, x_real) - dot(w_imag, x_imag)
    total[1] += dot(w_real, x_imag) + dot(w_imag, x_real)

    @pl.when(step == steps - 1)
    def _():
        for g in range(groups):
            outs[g][...] = total[:, :, g * LANES : (g + 1) * LANES].astype(jnp.bfloat16)


def form_beams(weights, signals):
    pieces, groups = len(weights), len(signals)
    rows, elements = weights[0].shape[1:]
    samples = signals[0].shape[2]
    depth = min(512, elements)
    steps = elements // depth
    all_rows = pieces * rows
    return pl.pallas_call(
        functools.partial(beams_kernel, pieces, groups, steps),
        grid=(steps,),
        in_specs=[pl.BlockSpec((2, rows, depth), lambda k: (0, 0, k))] * pieces
        + [pl.BlockSpec((2, depth, samples), lambda k: (0, k, 0))] * groups,
        out_specs=[pl.BlockSpec((2, all_rows, samples), lambda k: (0, 0, 0))] * groups,
        out_shape=[jax.ShapeDtypeStruct((2, all_rows, samples), jnp.bfloat16)] * groups,
        scratch_shapes=[pltpu.VMEM((2, all_rows, groups * samples), jnp.float32)],
        compiler_params=pltpu.CompilerParams(vmem_limit_bytes=40 * MEBI),
        cost_estimate=pl.CostEstimate(
            flops=8 * all_rows * elements * groups * samples,
            bytes_accessed=4 * elements * (all_rows + groups * samples),
            transcendentals=0,
        ),
        name="form_beams",
    )(*weights, *signals)


def order_kernel(parts, *refs):
    select, beams, out = refs[0], refs[1 : 1 + parts], refs[-1]
    real = jnp.concatenate([b[0] for b in beams], axis=0)
    imag = jnp.concatenate([b[1] for b in beams], axis=0)
    both = jnp.concatenate([real, imag], axis=1)
    picked = jnp.dot(select[0], both, preferred_element_type=jnp.float32).astype(jnp.bfloat16)
    samples = real.shape[1]
    out[0, 0] = picked[:, :samples]
    out[0, 1] = picked[:, samples:]


def order_beams(select, beams):
    tiles, rows, count = select.shape
    part_rows, samples = beams[0].shape[1:]
    return pl.pallas_call(
        functools.partial(order_kernel, len(beams)),
        grid=(tiles,),
        in_specs=[pl.BlockSpec((1, rows, count), lambda d: (d, 0, 0))]
        + [pl.BlockSpec((2, part_rows, samples), lambda d: (0, 0, 0))] * len(beams),
        out_specs=pl.BlockSpec((1, 2, rows, samples), lambda d: (d, 0, 0, 0)),
        out_shape=jax.ShapeDtypeStruct((tiles, 2, rows, samples), jnp.bfloat16),
        compiler_params=pltpu.CompilerParams(vmem_limit_bytes=40 * MEBI),
        cost_estimate=pl.CostEstimate(
            flops=4 * tiles * rows * count * samples,
            bytes_accessed=2 * tiles * rows * (count + 2 * samples),
            transcendentals=0,
        ),
        name="order_beams",
    )(select, *beams)


def bit_gaps(real, imag, index, scratch):
    shift = 8.0 * LEVEL * LEVEL
    for axis, field in ((0, real), (1, imag)):
        step = field * (2.0 * LEVEL)
        triple = field * (6.0 * LEVEL)
        scratch[axis * 4] = shift + triple
        scratch[axis * 4 + 1] = step
        scratch[axis * 4 + 2] = -step
        scratch[axis * 4 + 3] = shift - triple
    far = [scratch[index[label]] + scratch[index[16 + label]] for label in range(16)]
    least = jnp.minimum
    low = [
        least(least(far[b], far[b + 4]), least(far[b + 8], far[b + 12])) for b in range(4)
    ]
    high = [
        least(least(far[4 * b], far[4 * b + 1]), least(far[4 * b + 2], far[4 * b + 3]))
        for b in range(4)
    ]
    gaps = []
    for part in (low, high):
        gaps.append(least(part[1], part[3]) - least(part[0], part[2]))
        gaps.append(least(part[2], part[3]) - least(part[0], part[1]))
    return gaps


def expand(signs, coefs, base):
    terms = [coefs[base + t] + signs[3] * coefs[base + t + 8] for t in range(8)]
    terms = [terms[t] + signs[2] * terms[t + 4] for t in range(4)]
    terms = [terms[t] + signs[1] * terms[t + 2] for t in range(2)]
    return terms[0] + signs[0] * terms[1]


def soft_kernel(shape, index, field, first, second, scale, coefs, out, s_one, s_two, rest, scratch):
    blocks, rows, inner, tile = shape
    margin = (rows - inner) // 2
    dot = functools.partial(jnp.dot, preferred_element_type=jnp.float32)
    chunk = 16

    def tiles(value):
        return value.reshape(chunk // 8, 8, LANES)

    def soften(real, imag, start, slot):
        gaps = bit_gaps(real, imag, index, scratch.at[slot])
        half = tiles(scale[pl.ds(start, chunk), :])
        signs = [jnp.tanh(gap * half) for gap in gaps]
        return [
            expand(signs, coefs, base).reshape(chunk, LANES).astype(jnp.bfloat16)
            for base in (0, 16)
        ]

    count = 0
    for block in range(blocks):
        lanes = pl.ds(block * LANES, LANES)
        for start in range(0, rows, chunk):
            real = tiles(field[block, 0, start : start + chunk, :].astype(jnp.float32))
            imag = tiles(field[block, 1, start : start + chunk, :].astype(jnp.float32))
            a, b = soften(real, imag, start, count % 2)
            s_one[start : start + chunk, lanes] = a
            s_one[rows + start : rows + start + chunk, lanes] = b
            count += 1
    rest[...] = dot(first[...], s_one[...])
    for block in range(blocks):
        lanes = pl.ds(block * LANES, LANES)
        for start in range(0, inner, chunk):
            away = start + margin
            real = field[block, 0, away : away + chunk, :].astype(jnp.float32) - rest[
                start : start + chunk, lanes
            ]
            imag = field[block, 1, away : away + chunk, :].astype(jnp.float32) - rest[
                inner + start : inner + start + chunk, lanes
            ]
            a, b = soften(tiles(real), tiles(imag), away, count % 2)
            s_two[start : start + chunk, lanes] = a
            s_two[inner + start : inner + start + chunk, lanes] = b
            count += 1
    rest[0 : 2 * tile, :] = dot(second[...], s_two[...])
    for block in range(blocks):
        lanes = pl.ds(block * LANES, LANES)
        for start in range(0, tile, chunk):
            away = start + 2 * margin
            real = field[block, 0, away : away + chunk, :].astype(jnp.float32) - rest[
                start : start + chunk, lanes
            ]
            imag = field[block, 1, away : away + chunk, :].astype(jnp.float32) - rest[
                tile + start : tile + start + chunk, lanes
            ]
            gaps = bit_gaps(tiles(real), tiles(imag), index, scratch.at[count % 2])
            whole = 2.0 * tiles(scale[away : away + chunk, :])
            for bit in range(4):
                out[bit, start : start + chunk, lanes] = (
                    (gaps[bit] * whole).reshape(chunk, LANES).astype(jnp.bfloat16)
                )
            count += 1


def cancel(index, field, first, second, scale, coefs):
    sources, _, rows, samples = field.shape
    inner, tile = first.shape[0] // 2, second.shape[0] // 2
    blocks = 2
    wide = blocks * samples
    elements = sources * samples
    return pl.pallas_call(
        functools.partial(soft_kernel, (blocks, rows, inner, tile)),
        grid=(sources // blocks,),
        in_specs=[
            pl.BlockSpec(memory_space=pltpu.SMEM),
            pl.BlockSpec((blocks, 2, rows, samples), lambda s: (s, 0, 0, 0)),
            pl.BlockSpec(first.shape, lambda s: (0, 0)),
            pl.BlockSpec(second.shape, lambda s: (0, 0)),
            pl.BlockSpec(scale.shape, lambda s: (0, 0)),
            pl.BlockSpec(coefs.shape, lambda s: (0, 0, 0)),
        ],
        out_specs=pl.BlockSpec((4, tile, wide), lambda s: (0, 0, s)),
        out_shape=jax.ShapeDtypeStruct((4, tile, elements), jnp.bfloat16),
        scratch_shapes=[
            pltpu.VMEM((2 * rows, wide), jnp.bfloat16),
            pltpu.VMEM((2 * inner, wide), jnp.bfloat16),
            pltpu.VMEM((2 * inner, wide), jnp.float32),
            pltpu.VMEM((2, 8, 2, 8, LANES), jnp.float32),
        ],
        compiler_params=pltpu.CompilerParams(vmem_limit_bytes=40 * MEBI),
        cost_estimate=pl.CostEstimate(
            flops=130 * (rows + inner + tile) * elements,
            bytes_accessed=4 * rows * elements + 8 * tile * elements,
            transcendentals=4 * (rows + inner) * elements,
        ),
        name="cancel",
    )(index, field, first, second, scale, coefs)


class Places:
    def __init__(self, mesh):
        self.tm, self.beam = mesh.shape["tm"], mesh.shape["beam"]
        self.ny, self.nz = self.tm // 2, self.beam // 2

    def flat(self, y, x, z, core):
        return (y * 2 + x) * self.beam + z * 2 + core

    def permute(self, value, move):
        pairs = []
        for y in range(self.ny):
            for x in range(2):
                for z in range(self.nz):
                    for core in range(2):
                        pairs.append(
                            (self.flat(y, x, z, core), self.flat(*move(y, x, z, core)))
                        )
        return lax.ppermute(value, ("tm", "beam"), pairs)

    def across_core(self, value):
        return self.permute(value, lambda y, x, z, core: (y, x, z, 1 - core))

    def across_x(self, value):
        return self.permute(value, lambda y, x, z, core: (y, 1 - x, z, core))

    def across_y(self, value):
        return self.permute(value, lambda y, x, z, core: (1 - y, x, z, core))

    def along_z(self, value, k):
        return self.permute(value, lambda y, x, z, core: (y, x, (z + k) % self.nz, core))


def all_beams(places, element_signals, beam_weights):
    rows = beam_weights.shape[1]
    near = jnp.arange(rows, dtype=jnp.int32)
    if places.ny != 2 or places.nz != 4:
        gathered = lax.all_gather(beam_weights, ("tm", "beam"), axis=1, tiled=True)
        beams = form_beams([gathered], [element_signals])
        return beams, jnp.arange(gathered.shape[1], dtype=jnp.int32)
    half = element_signals.shape[1] // 2
    x_parts = [
        places.across_x(element_signals[:, i * half : (i + 1) * half]) for i in range(2)
    ]
    shifts = (0, 1, 3, 2)
    column = [beam_weights] + [places.along_z(beam_weights, k) for k in shifts[1:]]
    other = [places.across_y(piece) for piece in column]
    from_core = places.across_core(element_signals)
    from_x = jnp.concatenate(x_parts, axis=1)
    from_both = jnp.concatenate([places.across_core(part) for part in x_parts], axis=1)
    made = form_beams(column + other, [element_signals, from_core, from_x, from_both])
    beams = [
        made[0],
        places.across_core(made[1]),
        places.across_x(made[2]),
        places.permute(made[3], lambda y, x, z, core: (y, 1 - x, z, 1 - core)),
    ]
    kinds = [
        (mx, mc, a, k)
        for mx, mc in ((0, 0), (0, 1), (1, 0), (1, 1))
        for a in range(2)
        for k in shifts
    ]
    mx, mc, a, k = (np.array(v, np.int32) for v in zip(*kinds))
    tm, beam = lax.axis_index("tm"), lax.axis_index("beam")
    source = places.flat(
        (tm // 2) ^ a, (tm % 2) ^ mx, (beam // 2 - k) % places.nz, (beam % 2) ^ mc
    )
    return beams, (source[:, None] * rows + near[None, :]).reshape(-1)


def constellation(bit_labels):
    points = jnp.arange(16, dtype=jnp.int32)
    holds = bit_labels[None, :] == points[:, None]
    point = jnp.sum(jnp.where(holds, points[None, :], 0), axis=1)
    index = jnp.concatenate([point // 4, 4 + point % 4])
    walsh = np.array(
        [[(-1.0) ** bin(t & m).count("1") for m in range(16)] for t in range(16)], np.float32
    )
    values = jnp.stack([point // 4, point % 4])
    values = (2 * values - 3).astype(jnp.float32) * LEVEL
    coefs = jnp.sum(values[:, None, :] * walsh[None], axis=2) / 16.0
    return index, jnp.broadcast_to(coefs.reshape(32, 1, 1), (32, 8, LANES))


def on_device(places, element_signals, beam_weights, beam_order, neighbours, leakage, noise_var, bit_labels):
    count = beam_order.shape[0]
    tile = count // places.beam
    rows = tile + 2 * HALO
    slots = neighbours.shape[1]
    starts = np.arange(places.beam)[:, None] * tile - HALO + np.arange(rows)[None, :]
    windows = jnp.where(
        (starts >= 0) & (starts < count), beam_order[np.clip(starts, 0, count - 1)], -1
    )
    mine = lax.axis_index("beam")
    own = windows[mine]
    table = jnp.concatenate(
        [
            neighbours.astype(jnp.float32),
            leakage[0].astype(jnp.float32),
            leakage[1].astype(jnp.float32),
            noise_var[:, None],
        ],
        axis=1,
    )
    taken = jnp.take(table, own, axis=0, mode="clip")
    near, noise = taken[:, :slots], taken[:, 3 * slots]
    hits = near[:, :, None] == own.astype(jnp.float32)[None, None, :]
    real, imag = (
        jnp.sum(jnp.where(hits, taken[:, i * slots : (i + 1) * slots, None], 0.0), axis=1)
        for i in (1, 2)
    )
    scale = jnp.broadcast_to(0.5 / noise[:, None], (rows, LANES))

    def crossing(out, cols):
        r, i = real[out:-out, cols : rows - cols], imag[out:-out, cols : rows - cols]
        top, bottom = jnp.concatenate([r, -i], axis=1), jnp.concatenate([i, r], axis=1)
        return jnp.concatenate([top, bottom], axis=0).astype(jnp.bfloat16)

    index, coefs = constellation(bit_labels)
    beams, held = all_beams(places, element_signals, beam_weights)
    select = (windows[:, :, None] == held[None, None, :]).astype(jnp.bfloat16)
    ordered = order_beams(select, beams)
    field = lax.all_to_all(ordered, "beam", split_axis=0, concat_axis=0, tiled=True)
    return cancel(index, field, crossing(COLS, 0), crossing(2 * COLS, COLS), scale, coefs)


def solution(mesh):
    in_specs = (
        P(None, None, ("tm", "beam")),
        P(None, ("tm", "beam"), None),
        P(),
        P(),
        P(),
        P(),
        P(),
    )
    return jax.shard_map(
        functools.partial(on_device, Places(mesh)),
        mesh=mesh,
        in_specs=in_specs,
        out_specs=P(None, "beam", "tm"),
        check_vma=False,
    )
```

time: 239 us -> 123 us (0.51)
  waiting for transfers between devices: 124 us -> 60.8 us
  other arithmetic: 56 us -> 5.56 us
  Pallas kernels: 0 us -> 21 us
  between operations: 13.9 us -> 0.39 us
  matrix products: 9.57 us -> 0 us
  starting transfers between devices: 13.4 us -> 18.9 us
  local copies, waits for them, and re-layouts: 20.3 us -> 16.2 us
    all_gather x2 -> x0, waiting for transfers between devices: 113 us -> none  [the longest x1 79.3 us: on_device(): piece = lax.all_gather(group_rows, 'tm', axis=1, tiled=True)]
    ppermute x4 -> x15, waiting for transfers between devices: 3.36 us -> 41.5 us  [permute(): return lax.ppermute(value, ('tm', 'beam'), pairs)]
    reduce_min x3 -> x0, other arithmetic: 27.1 us -> none  [metric_block(): lowest_zero = jnp.min(jnp.where(chosen, HUGE, distance), axis=0)]
    pallas_call x0 -> x3, Pallas kernels: none -> 21 us  [the longest x1 14.2 us: cancel(): pl.pallas_call(functools.partial(soft_kernel, (blocks, rows, inner, tile)...]
    reduce_prod x2 -> x0, other arithmetic: 14.1 us -> none  [soft_block(): weight = jnp.prod(factors, axis=1)]
    all_to_all x1, waiting for transfers between devices: 7.02 us -> 19.2 us  [on_device(): lax.all_to_all(ordered, 'beam', split_axis=0, concat_axis=0, tiled=True)]
    dot_general x12 -> x0, matrix products: 9.57 us -> none  [the longest x1 3.69 us: on_device(): jnp.dot(piece[0], element_signals[1], preferred_element_type=jnp.float32)]
    slice x0 -> x10, local copies, waits for them, and re-layouts: none -> 8.07 us  [the longest x3 2.75 us: on_device(): taken[:, i * slots:(i + 1) * slots, None]]
  transfers between devices with their start and end apart: 7 -> 16, of which waited for: 5 -> 9; matrix products, arithmetic and copies ran while one was open for 8% -> 17% of each run, Pallas kernels for 0% -> 0%
where the time goes in v1:
time: 123 us
  waiting for transfers between devices  60.8 us (49%)
  Pallas kernels  21 us (17%)
  starting transfers between devices  18.9 us (15%)
  local copies, waits for them, and re-layouts  16.2 us (13%)
  other arithmetic  5.56 us (5%)
    ppermute x15, waiting for transfers between devices, permute(): return lax.ppermute(value, ('tm', 'beam'), pairs)  41.5 us
    all_to_all x1, waiting for transfers between devices, on_device(): lax.all_to_all(ordered, 'beam', split_axis=0, concat_axis=0, tiled=True)  19.2 us
    ppermute x15, starting transfers between devices, permute(): return lax.ppermute(value, ('tm', 'beam'), pairs)  15.2 us
    pallas_call x1, Pallas kernels, cancel(): pl.pallas_call(functools.partial(soft_kernel, (blocks, rows, inner, tile)...  14.2 us
    gather x1, local copies, waits for them, and re-layouts, on_device(): beam_order[np.clip(starts, 0, count - 1)]  5.85 us
    pallas_call x1, Pallas kernels, form_beams(): pl.pallas_call(functools.partial(beams_kernel, pieces, groups, steps), gr...  4.58 us
    all_to_all x1, starting transfers between devices, on_device(): lax.all_to_all(ordered, 'beam', split_axis=0, concat_axis=0, tiled=True)  3.68 us
    slice x3, local copies, waits for them, and re-layouts, on_device(): taken[:, i * slots:(i + 1) * slots, None]  2.75 us
  transfers between devices with their start and end apart: 16, of which 9 were waited for; matrix products, arithmetic and copies ran while one was open for 17% of the time, Pallas kernels for 0%

profile of v1, /device:TPU:0, one launch (start us, length us, event | category | flops | bytes accessed | tf_op | source)
XLA Modules:
  0.0 122.8 jit_solution(10093551542084979510)
XLA Ops:
  0.0 4.0 %collective-permute-start.2 = (bf16[2,32,2048]{2,1,0:T(8,128)(2,1)}, bf16[2,32,2048]{2,1,0:T(8,128)(2,1)}, u32[]{:S(2)}, u32[]{:S(2)}) collective-permute-start(bf16[2,32,2048]{2,1,0:T(8,128)(2,1)} %refs_0_.1), channel_id=1, source_target_pairs={{0,4},{1,5},{2,6},{3,7},{4,0},{5,1},{6,2},{7,3},{8,12},{9,13},{10,... | collective-permute-start | bytes 786440 | tf_op jit(solution)/shard_map/ppermute | solution.py:246
  4.0 1.3 %collective-permute-start.1 = (bf16[2,32,2048]{2,1,0:T(8,128)(2,1)}, bf16[2,32,2048]{2,1,0:T(8,128)(2,1)}, u32[]{:S(2)}, u32[]{:S(2)}) collective-permute-start(bf16[2,32,2048]{2,1,0:T(8,128)(2,1)} %refs_0_.1), channel_id=1, source_target_pairs={{0,6},{1,7},{2,0},{3,1},{4,2},{5,3},{6,4},{7,5},{8,14},{9,15},{10,... | collective-permute-start | bytes 786440 | tf_op jit(solution)/shard_map/ppermute | solution.py:246
  5.4 2.2 %fusion.15 = (bf16[2,1024,128]{2,1,0:T(8,128)(2,1)}, bf16[2,1024,128]{2,1,0:T(8,128)(2,1)}) fusion(bf16[2,2048,128]{2,1,0:T(8,128)(2,1)} %refs_8_.1), kind=kLoop, calls=%fused_computation.59 | loop fusion | bytes 2097152 | tf_op jit(solution)/shard_map/slice | solution.py:270
  7.6 1.5 %collective-permute-start.8 = (bf16[2,1024,128]{2,1,0:T(8,128)(2,1)}, bf16[2,1024,128]{2,1,0:T(8,128)(2,1)}, u32[]{:S(2)}, u32[]{:S(2)}) collective-permute-start(bf16[2,1024,128]{2,1,0:T(8,128)(2,1)} %get-tuple-element.17), channel_id=1, source_target_pairs={{0,8},{1,9},{2,10},{3,11},{4,12},{5,13},{6,14},{7,15},{8,0},{9,1},... | collective-permute-start | bytes 1572872 | tf_op jit(solution)/shard_map/ppermute | solution.py:246
  9.8 5.9 %gather_fusion = s32[1536]{0:T(1024)S(1)} fusion(s32[1024]{0:T(1024)S(1)} %copy-done, s32[2048]{0:T(1024)S(1)} %pad_clamp_fusion), kind=kCustom, calls=%fused_computation | custom fusion | bytes 18432 | tf_op jit(solution)/shard_map/gather | solution.py:320
  17.6 5.1 %collective-permute-done.8 = bf16[2,1024,128]{2,1,0:T(8,128)(2,1)} collective-permute-done((bf16[2,1024,128]{2,1,0:T(8,128)(2,1)}, bf16[2,1024,128]{2,1,0:T(8,128)(2,1)}, u32[]{:S(2)}, u32[]{:S(2)}) %collective-permute-start.8) | collective-permute-done | bytes 524320 | tf_op jit(solution)/shard_map/ppermute | solution.py:246
  22.7 10.8 %collective-permute-done.9 = bf16[2,1024,128]{2,1,0:T(8,128)(2,1)} collective-permute-done((bf16[2,1024,128]{2,1,0:T(8,128)(2,1)}, bf16[2,1024,128]{2,1,0:T(8,128)(2,1)}, u32[]{:S(2)}, u32[]{:S(2)}) %collective-permute-start.9) | collective-permute-done | bytes 524320 | tf_op jit(solution)/shard_map/ppermute | solution.py:246
  33.5 0.8 fusion.16
  34.3 1.0 copy.30
  35.3 1.0 copy.31
  36.3 1.0 copy.29
  37.8 0.7 collective-permute-start
  38.7 1.6 %collective-permute-start.3 = (bf16[2,32,2048]{2,1,0:T(8,128)(2,1)S(1)}, bf16[2,32,2048]{2,1,0:T(8,128)(2,1)S(1)}, u32[]{:S(2)}, u32[]{:S(2)}) collective-permute-start(bf16[2,32,2048]{2,1,0:T(8,128)(2,1)S(1)} %copy-done.3), channel_id=1, source_target_pairs={{0,16},{1,17},{2,18},{3,19},{4,20},{5,21},{6,22},{7,23},{8,24},{9,... | collective-permute-start | bytes 786440 | tf_op jit(solution)/shard_map/ppermute | solution.py:246
  40.3 8.1 %collective-permute-done.refs_1_ = bf16[2,32,2048]{2,1,0:T(8,128)(2,1)S(1)} collective-permute-done((bf16[2,32,2048]{2,1,0:T(8,128)(2,1)S(1)}, bf16[2,32,2048]{2,1,0:T(8,128)(2,1)S(1)}, u32[]{:S(2)}, u32[]{:S(2)}) %collective-permute-start) | collective-permute-done | bytes 262176 | tf_op jit(solution)/shard_map/ppermute | solution.py:246
  48.4 1.5 %collective-permute-start.6 = (bf16[2,32,2048]{2,1,0:T(8,128)(2,1)}, bf16[2,32,2048]{2,1,0:T(8,128)(2,1)S(1)}, u32[]{:S(2)}, u32[]{:S(2)}) collective-permute-start(bf16[2,32,2048]{2,1,0:T(8,128)(2,1)} %collective-permute-done.2.refs_3_), channel_id=1, source_target_pairs={{0,16},{1,17},{2,18},{3,19},{4,20},{5,21},{6,22},{7,23},{8,24},{9,... | collective-permute-start | bytes 786440 | tf_op jit(solution)/shard_map/ppermute | solution.py:246
  50.4 1.5 %collective-permute-start.4 = (bf16[2,32,2048]{2,1,0:T(8,128)(2,1)S(1)}, bf16[2,32,2048]{2,1,0:T(8,128)(2,1)S(1)}, u32[]{:S(2)}, u32[]{:S(2)}) collective-permute-start(bf16[2,32,2048]{2,1,0:T(8,128)(2,1)S(1)} %collective-permute-done.refs_1_), channel_id=1, source_target_pairs={{0,16},{1,17},{2,18},{3,19},{4,20},{5,21},{6,22},{7,23},{8,24},{9,... | collective-permute-start | bytes 786440 | tf_op jit(solution)/shard_map/ppermute | solution.py:246
  51.9 1.3 %pad_maximum_fusion.refs_10_ = bf16[2,2048,128]{2,1,0:T(8,128)(2,1)S(1)} fusion(bf16[2,1024,128]{2,1,0:T(8,128)(2,1)} %collective-permute-done.9, bf16[2,1024,128]{2,1,0:T(8,128)(2,1)} %collective-permute-done.8), kind=kLoop, calls=%fused_computation.7 | loop fusion | flops 2097152 | bytes 2097152 | tf_op jit(solution)/shard_map/concatenate | solution.py:276
  53.2 1.3 %pad_maximum_fusion.1.refs_11_ = bf16[2,2048,128]{2,1,0:T(8,128)(2,1)S(1)} fusion(bf16[2,1024,128]{2,1,0:T(8,128)(2,1)} %collective-permute-done.11, bf16[2,1024,128]{2,1,0:T(8,128)(2,1)} %collective-permute-done.10), kind=kLoop, calls=%fused_computation.8 | loop fusion | flops 2097152 | bytes 2097152 | tf_op jit(solution)/shard_map/concatenate | solution.py:277
  54.5 3.3 %collective-permute-done.6.refs_7_ = bf16[2,32,2048]{2,1,0:T(8,128)(2,1)S(1)} collective-permute-done((bf16[2,32,2048]{2,1,0:T(8,128)(2,1)}, bf16[2,32,2048]{2,1,0:T(8,128)(2,1)S(1)}, u32[]{:S(2)}, u32[]{:S(2)}) %collective-permute-start.6) | collective-permute-done | bytes 262176 | tf_op jit(solution)/shard_map/ppermute | solution.py:246
  57.8 5.6 %collective-permute-done.5.refs_6_ = bf16[2,32,2048]{2,1,0:T(8,128)(2,1)S(1)} collective-permute-done((bf16[2,32,2048]{2,1,0:T(8,128)(2,1)}, bf16[2,32,2048]{2,1,0:T(8,128)(2,1)S(1)}, u32[]{:S(2)}, u32[]{:S(2)}) %collective-permute-start.5) | collective-permute-done | bytes 262176 | tf_op jit(solution)/shard_map/ppermute | solution.py:246
  63.4 4.3 %collective-permute-done.4.refs_5_ = bf16[2,32,2048]{2,1,0:T(8,128)(2,1)S(1)} collective-permute-done((bf16[2,32,2048]{2,1,0:T(8,128)(2,1)S(1)}, bf16[2,32,2048]{2,1,0:T(8,128)(2,1)S(1)}, u32[]{:S(2)}, u32[]{:S(2)}) %collective-permute-start.4) | collective-permute-done | bytes 262176 | tf_op jit(solution)/shard_map/ppermute | solution.py:246
  67.8 4.6 %form_beams.1 = (bf16[2,256,128]{2,1,0:T(8,128)(2,1)S(1)}, bf16[2,256,128]{2,1,0:T(8,128)(2,1)S(1)}, bf16[2,256,128]{2,1,0:T(8,128)(2,1)S(1)}, bf16[2,256,128]{2,1,0:T(8,128)(2,1)S(1)}) custom-call(bf16[2,32,2048]{2,1,0:T(8,128)(2,1)S(1)} %copy-done.3, bf16[2,32,2048]{2,1,0:T(8,128)(2,1)S(1)} %collective-permute-done.refs_1_, ...), custom_call_target="tpu_custom_call" | custom-call | flops 2147483648 | bytes 6291456 | tf_op jit(solution)/shard_map/form_beams/pallas_call | solution.py:50
  72.4 1.6 %collective-permute-start.13 = (bf16[2,256,128]{2,1,0:T(8,128)(2,1)S(1)}, bf16[2,256,128]{2,1,0:T(8,128)(2,1)S(1)}, u32[]{:S(2)}, u32[]{:S(2)}) collective-permute-start(bf16[2,256,128]{2,1,0:T(8,128)(2,1)S(1)} %get-tuple-element.11), channel_id=1, source_target_pairs={{0,8},{1,9},{2,10},{3,11},{4,12},{5,13},{6,14},{7,15},{8,0},{9,1},... | collective-permute-start | bytes 393224 | tf_op jit(solution)/shard_map/ppermute | solution.py:246
  75.0 0.7 slice.72
  76.5 2.3 %collective-permute-done.13.refs_3_ = bf16[2,256,128]{2,1,0:T(8,128)(2,1)S(1)} collective-permute-done((bf16[2,256,128]{2,1,0:T(8,128)(2,1)S(1)}, bf16[2,256,128]{2,1,0:T(8,128)(2,1)S(1)}, u32[]{:S(2)}, u32[]{:S(2)}) %collective-permute-start.13) | collective-permute-done | bytes 131104 | tf_op jit(solution)/shard_map/ppermute | solution.py:246
  78.8 1.9 %collective-permute-done.14.refs_4_ = bf16[2,256,128]{2,1,0:T(8,128)(2,1)S(1)} collective-permute-done((bf16[2,256,128]{2,1,0:T(8,128)(2,1)S(1)}, bf16[2,256,128]{2,1,0:T(8,128)(2,1)S(1)}, u32[]{:S(2)}, u32[]{:S(2)}) %collective-permute-start.14) | collective-permute-done | bytes 131104 | tf_op jit(solution)/shard_map/ppermute | solution.py:246
  80.7 2.2 %order_beams.1 = bf16[8,2,192,128]{3,2,1,0:T(8,128)(2,1)S(1)} custom-call(bf16[8,192,1024]{2,1,0:T(8,128)(2,1)S(1)} %compare_convert_fusion.refs_0_, bf16[2,256,128]{2,1,0:T(8,128)(2,1)S(1)} %get-tuple-element.9.refs_1_, bf16[2,256,128]{2,1,0:T(8,128)(2,1)S(1)} %collective-permute-done.12.refs_2_, bf16[2,256,128]{2,1,0:T(8,128)(2,1)S(1)} %collective-permute-done.13.refs_3_, ...), custom_call_target="tpu_custom_call" | custom-call | flops 805306368 | bytes 3932160 | tf_op jit(solution)/shard_map/order_beams/pallas_call | solution.py:82
  82.9 0.9 copy-done.1
  83.8 3.7 %all-to-all-start = ((bf16[8,2,192,128]{3,2,1,0:T(8,128)(2,1)}), bf16[8,2,192,128]{3,2,1,0:T(8,128)(2,1)S(1)}, u32[]{:S(2)}, u32[]{:S(2)}) async-start(bf16[8,2,192,128]{3,2,1,0:T(8,128)(2,1)} %copy-done.1), calls=%async_computation | async-start | bytes 1572864 | tf_op jit(solution)/shard_map/all_to_all | solution.py:351
  87.8 1.0 maximum_maximum_fusion.1.second
  89.2 19.2 %all-to-all-done.field = bf16[8,2,192,128]{3,2,1,0:T(8,128)(2,1)S(1)} async-done(((bf16[8,2,192,128]{3,2,1,0:T(8,128)(2,1)}), bf16[8,2,192,128]{3,2,1,0:T(8,128)(2,1)S(1)}, u32[]{:S(2)}, u32[]{:S(2)}) %all-to-all-start) | async-done | bytes 786464 | tf_op jit(solution)/shard_map/all_to_all | solution.py:351
  108.6 14.2 %cancel.1 = bf16[4,128,1024]{2,1,0:T(8,128)(2,1)} custom-call(s32[32]{0:T(128)S(1)} %pad_add_fusion.index, bf16[8,2,192,128]{3,2,1,0:T(8,128)(2,1)S(1)} %all-to-all-done.field, bf16[320,384]{1,0:T(8,128)(2,1)S(1)} %maximum_maximum_fusion.first, bf16[256,320]{1,0:T(8,128)(2,1)S(1)} %maximum_maximum_fusion.1.second, f32[192,128]{1,0:T(8,128)S(1)} %broadcast_in_dim.77.scale, ...), custom_call_target="tpu_custom_call" | custom-call | flops 63897600 | bytes 1835008 | tf_op jit(solution)/shard_map/cancel/pallas_call | solution.py:200
  (82 shorter events, 6.2 us)
Async XLA Ops:
  0.0 9.7 %copy-start = (s32[1024]{0:T(1024)S(1)}, s32[1024]{0:T(1024)}, u32[]{:S(2)}) copy-start(s32[1024]{0:T(1024)} %param.17) | copy-start | bytes 12292
  0.0 9.7 %copy-start.10 = (s32[1536]{0:T(1024)S(1)}, s32[1536]{0:T(1024)}, u32[]{:S(2)}) copy-start(s32[1536]{0:T(1024)} %constant.133) | copy-start | bytes 18436
  0.0 37.8 %collective-permute-start.2 = (bf16[2,32,2048]{2,1,0:T(8,128)(2,1)}, bf16[2,32,2048]{2,1,0:T(8,128)(2,1)}, u32[]{:S(2)}, u32[]{:S(2)}) collective-permute-start(bf16[2,32,2048]{2,1,0:T(8,128)(2,1)} %refs_0_.1), channel_id=1, source_target_pairs={{0,4},{1,5},{2,6},{3,7},{4,0},{5,1},{6,2},{7,3},{8,12},{9,13},{10,... | collective-permute-start | bytes 786440 | tf_op jit(solution)/shard_map/ppermute | solution.py:246
  4.0 34.7 %collective-permute-start.1 = (bf16[2,32,2048]{2,1,0:T(8,128)(2,1)}, bf16[2,32,2048]{2,1,0:T(8,128)(2,1)}, u32[]{:S(2)}, u32[]{:S(2)}) collective-permute-start(bf16[2,32,2048]{2,1,0:T(8,128)(2,1)} %refs_0_.1), channel_id=1, source_target_pairs={{0,6},{1,7},{2,0},{3,1},{4,2},{5,3},{6,4},{7,5},{8,14},{9,15},{10,... | collective-permute-start | bytes 786440 | tf_op jit(solution)/shard_map/ppermute | solution.py:246
  5.4 62.4 %collective-permute-start.7 = (bf16[2,2048,128]{2,1,0:T(8,128)(2,1)}, bf16[2,2048,128]{2,1,0:T(8,128)(2,1)}, u32[]{:S(2)}, u32[]{:S(2)}) collective-permute-start(bf16[2,2048,128]{2,1,0:T(8,128)(2,1)} %refs_8_.1), channel_id=1, source_target_pairs={{0,1},{1,0},{2,3},{3,2},{4,5},{5,4},{6,7},{7,6},{8,9},{9,8},{10,11... | collective-permute-start | bytes 3145736 | tf_op jit(solution)/shard_map/ppermute | solution.py:246
  7.6 15.0 %collective-permute-start.8 = (bf16[2,1024,128]{2,1,0:T(8,128)(2,1)}, bf16[2,1024,128]{2,1,0:T(8,128)(2,1)}, u32[]{:S(2)}, u32[]{:S(2)}) collective-permute-start(bf16[2,1024,128]{2,1,0:T(8,128)(2,1)} %get-tuple-element.17), channel_id=1, source_target_pairs={{0,8},{1,9},{2,10},{3,11},{4,12},{5,13},{6,14},{7,15},{8,0},{9,1},... | collective-permute-start | bytes 1572872 | tf_op jit(solution)/shard_map/ppermute | solution.py:246
  9.1 24.4 %collective-permute-start.9 = (bf16[2,1024,128]{2,1,0:T(8,128)(2,1)}, bf16[2,1024,128]{2,1,0:T(8,128)(2,1)}, u32[]{:S(2)}, u32[]{:S(2)}) collective-permute-start(bf16[2,1024,128]{2,1,0:T(8,128)(2,1)} %get-tuple-element.18), channel_id=1, source_target_pairs={{0,8},{1,9},{2,10},{3,11},{4,12},{5,13},{6,14},{7,15},{8,0},{9,1},... | collective-permute-start | bytes 1572872 | tf_op jit(solution)/shard_map/ppermute | solution.py:246
  9.7 6.0 %copy-start.12 = (pred[1536]{0:T(1024)(128)(4,1)S(1)}, pred[1536]{0:T(1024)(128)(4,1)}, u32[]{:S(2)}) copy-start(pred[1536]{0:T(1024)(128)(4,1)} %constant.134) | copy-start | bytes 4612
  9.7 6.0 %copy-start.13 = (s32[32]{0:T(128)S(1)}, s32[32]{0:T(128)}, u32[]{:S(2)}) copy-start(s32[32]{0:T(128)} %constant.131) | copy-start | bytes 388
  9.7 6.0 %copy-start.14 = (s32[32]{0:T(128)S(1)}, s32[32]{0:T(128)}, u32[]{:S(2)}) copy-start(s32[32]{0:T(128)} %constant.129.clone) | copy-start | bytes 388
  9.7 6.0 %copy-start.15 = (s32[32]{0:T(128)S(1)}, s32[32]{0:T(128)}, u32[]{:S(2)}) copy-start(s32[32]{0:T(128)} %constant.127.clone) | copy-start | bytes 388
  9.7 6.0 %copy-start.16 = (s32[32]{0:T(128)S(1)}, s32[32]{0:T(128)}, u32[]{:S(2)}) copy-start(s32[32]{0:T(128)} %constant.126.clone) | copy-start | bytes 388
  9.7 6.2 %copy-start.8 = (s32[1024,6]{0,1:T(8,128)S(1)}, s32[1024,6]{0,1:T(8,128)}, u32[]{:S(2)}) copy-start(s32[1024,6]{0,1:T(8,128)} %param.18) | copy-start | bytes 73732
  9.8 6.2 %copy-start.7 = (bf16[2,1024,6]{1,0,2:T(2,128)(2,1)S(1)}, bf16[2,1024,6]{1,0,2:T(2,128)(2,1)}, u32[]{:S(2)}) copy-start(bf16[2,1024,6]{1,0,2:T(2,128)(2,1)} %param.19) | copy-start | bytes 73732
  9.8 6.2 %copy-start.11 = (f32[1024]{0:T(1024)S(1)}, f32[1024]{0:T(1024)}, u32[]{:S(2)}) copy-start(f32[1024]{0:T(1024)} %param.20) | copy-start | bytes 12292
  17.0 20.8 %copy-start.3 = (bf16[2,32,2048]{2,1,0:T(8,128)(2,1)S(1)}, bf16[2,32,2048]{2,1,0:T(8,128)(2,1)}, u32[]{:S(2)}) copy-start(bf16[2,32,2048]{2,1,0:T(8,128)(2,1)} %refs_0_.1) | copy-start | bytes 786436
  17.0 21.6 %copy-start.17 = (s32[16]{0:T(128)S(1)}, s32[16]{0:T(128)}, u32[]{:S(2)}) copy-start(s32[16]{0:T(128)} %param.21) | copy-start | bytes 196
  22.7 27.3 %collective-permute-start.10 = (bf16[2,1024,128]{2,1,0:T(8,128)(2,1)}, bf16[2,1024,128]{2,1,0:T(8,128)(2,1)}, u32[]{:S(2)}, u32[]{:S(2)}) collective-permute-start(bf16[2,1024,128]{2,1,0:T(8,128)(2,1)} %collective-permute-done.8), channel_id=1, source_target_pairs={{0,1},{1,0},{2,3},{3,2},{4,5},{5,4},{6,7},{7,6},{8,9},{9,8},{10,11... | collective-permute-start | bytes 1572872 | tf_op jit(solution)/shard_map/ppermute | solution.py:246
  33.5 16.9 %collective-permute-start.11 = (bf16[2,1024,128]{2,1,0:T(8,128)(2,1)}, bf16[2,1024,128]{2,1,0:T(8,128)(2,1)}, u32[]{:S(2)}, u32[]{:S(2)}) collective-permute-start(bf16[2,1024,128]{2,1,0:T(8,128)(2,1)} %collective-permute-done.9), channel_id=1, source_target_pairs={{0,1},{1,0},{2,3},{3,2},{4,5},{5,4},{6,7},{7,6},{8,9},{9,8},{10,11... | collective-permute-start | bytes 1572872 | tf_op jit(solution)/shard_map/ppermute | solution.py:246
  37.8 38.0 %copy-start.4 = (f32[192,192]{1,0:T(8,128)}, f32[192,192]{1,0:T(8,128)S(1)}, u32[]{:S(2)}) copy-start(f32[192,192]{1,0:T(8,128)S(1)} %get-tuple-element.13) | copy-start | bytes 442372
  37.8 10.6 %collective-permute-start = (bf16[2,32,2048]{2,1,0:T(8,128)(2,1)S(1)}, bf16[2,32,2048]{2,1,0:T(8,128)(2,1)S(1)}, u32[]{:S(2)}, u32[]{:S(2)}) collective-permute-start(bf16[2,32,2048]{2,1,0:T(8,128)(2,1)S(1)} %copy-done.3), channel_id=1, source_target_pairs={{0,2},{1,3},{2,4},{3,5},{4,6},{5,7},{6,0},{7,1},{8,10},{9,11},{10,... | collective-permute-start | bytes 786440 | tf_op jit(solution)/shard_map/ppermute | solution.py:246
  38.7 29.1 %copy-start.2 = (bf16[2,2048,128]{2,1,0:T(8,128)(2,1)S(1)}, bf16[2,2048,128]{2,1,0:T(8,128)(2,1)}, u32[]{:S(2)}) copy-start(bf16[2,2048,128]{2,1,0:T(8,128)(2,1)} %refs_8_.1) | copy-start | bytes 3145732
  38.7 15.8 %collective-permute-start.3 = (bf16[2,32,2048]{2,1,0:T(8,128)(2,1)S(1)}, bf16[2,32,2048]{2,1,0:T(8,128)(2,1)S(1)}, u32[]{:S(2)}, u32[]{:S(2)}) collective-permute-start(bf16[2,32,2048]{2,1,0:T(8,128)(2,1)S(1)} %copy-done.3), channel_id=1, source_target_pairs={{0,16},{1,17},{2,18},{3,19},{4,20},{5,21},{6,22},{7,23},{8,24},{9,... | collective-permute-start | bytes 786440 | tf_op jit(solution)/shard_map/ppermute | solution.py:246
  48.4 9.4 %collective-permute-start.6 = (bf16[2,32,2048]{2,1,0:T(8,128)(2,1)}, bf16[2,32,2048]{2,1,0:T(8,128)(2,1)S(1)}, u32[]{:S(2)}, u32[]{:S(2)}) collective-permute-start(bf16[2,32,2048]{2,1,0:T(8,128)(2,1)} %collective-permute-done.2.refs_3_), channel_id=1, source_target_pairs={{0,16},{1,17},{2,18},{3,19},{4,20},{5,21},{6,22},{7,23},{8,24},{9,... | collective-permute-start | bytes 786440 | tf_op jit(solution)/shard_map/ppermute | solution.py:246
  49.9 13.5 %collective-permute-start.5 = (bf16[2,32,2048]{2,1,0:T(8,128)(2,1)}, bf16[2,32,2048]{2,1,0:T(8,128)(2,1)S(1)}, u32[]{:S(2)}, u32[]{:S(2)}) collective-permute-start(bf16[2,32,2048]{2,1,0:T(8,128)(2,1)} %collective-permute-done.1.refs_2_), channel_id=1, source_target_pairs={{0,16},{1,17},{2,18},{3,19},{4,20},{5,21},{6,22},{7,23},{8,24},{9,... | collective-permute-start | bytes 786440 | tf_op jit(solution)/shard_map/ppermute | solution.py:246
  50.4 17.3 %collective-permute-start.4 = (bf16[2,32,2048]{2,1,0:T(8,128)(2,1)S(1)}, bf16[2,32,2048]{2,1,0:T(8,128)(2,1)S(1)}, u32[]{:S(2)}, u32[]{:S(2)}) collective-permute-start(bf16[2,32,2048]{2,1,0:T(8,128)(2,1)S(1)} %collective-permute-done.refs_1_), channel_id=1, source_target_pairs={{0,16},{1,17},{2,18},{3,19},{4,20},{5,21},{6,22},{7,23},{8,24},{9,... | collective-permute-start | bytes 786440 | tf_op jit(solution)/shard_map/ppermute | solution.py:246
  54.5 21.9 %copy-start.9 = (f32[16,16]{1,0:T(8,128)S(1)}, f32[16,16]{1,0:T(8,128)}, u32[]{:S(2)}) copy-start(f32[16,16]{1,0:T(8,128)} %constant.132) | copy-start | bytes 3076
  72.4 4.1 %collective-permute-start.12 = (bf16[2,256,128]{2,1,0:T(8,128)(2,1)S(1)}, bf16[2,256,128]{2,1,0:T(8,128)(2,1)S(1)}, u32[]{:S(2)}, u32[]{:S(2)}) collective-permute-start(bf16[2,256,128]{2,1,0:T(8,128)(2,1)S(1)} %get-tuple-element.10), channel_id=1, source_target_pairs={{0,1},{1,0},{2,3},{3,2},{4,5},{5,4},{6,7},{7,6},{8,9},{9,8},{10,11... | collective-permute-start | bytes 393224 | tf_op jit(solution)/shard_map/ppermute | solution.py:246
  72.4 6.4 %collective-permute-start.13 = (bf16[2,256,128]{2,1,0:T(8,128)(2,1)S(1)}, bf16[2,256,128]{2,1,0:T(8,128)(2,1)S(1)}, u32[]{:S(2)}, u32[]{:S(2)}) collective-permute-start(bf16[2,256,128]{2,1,0:T(8,128)(2,1)S(1)} %get-tuple-element.11), channel_id=1, source_target_pairs={{0,8},{1,9},{2,10},{3,11},{4,12},{5,13},{6,14},{7,15},{8,0},{9,1},... | collective-permute-start | bytes 393224 | tf_op jit(solution)/shard_map/ppermute | solution.py:246
  74.0 6.7 %collective-permute-start.14 = (bf16[2,256,128]{2,1,0:T(8,128)(2,1)S(1)}, bf16[2,256,128]{2,1,0:T(8,128)(2,1)S(1)}, u32[]{:S(2)}, u32[]{:S(2)}) collective-permute-start(bf16[2,256,128]{2,1,0:T(8,128)(2,1)S(1)} %get-tuple-element.12), channel_id=1, source_target_pairs={{0,9},{1,8},{2,11},{3,10},{4,13},{5,12},{6,15},{7,14},{8,1},{9,0},... | collective-permute-start | bytes 393224 | tf_op jit(solution)/shard_map/ppermute | solution.py:246
  80.7 7.0 %copy-start.5 = (f32[192,192]{1,0:T(8,128)S(1)}, f32[192,192]{1,0:T(8,128)}, u32[]{:S(2)}) copy-start(f32[192,192]{1,0:T(8,128)} %copy-done.4) | copy-start | bytes 442372
  83.8 24.6 %all-to-all-start = ((bf16[8,2,192,128]{3,2,1,0:T(8,128)(2,1)}), bf16[8,2,192,128]{3,2,1,0:T(8,128)(2,1)S(1)}, u32[]{:S(2)}, u32[]{:S(2)}) async-start(bf16[8,2,192,128]{3,2,1,0:T(8,128)(2,1)} %copy-done.1), calls=%async_computation | async-start | bytes 1572864 | tf_op jit(solution)/shard_map/all_to_all | solution.py:351
  (2 other events, 5.9 us)

commit v2 on v1

v2 whole, which is shorter than its diff:
```python
import functools
import math

import jax
import jax.numpy as jnp
import numpy as np
from jax import lax
from jax.experimental import pallas as pl
from jax.experimental.pallas import tpu as pltpu
from jax.sharding import PartitionSpec as P

COLS = 16
HALO = 2 * COLS
LEVEL = 0.31622776601683794
LANES = 128
MEBI = 1 << 20


def beams_kernel(pieces, *refs):
    weights, signals, out, total = refs[:pieces], *refs[pieces:]
    elements = weights[0].shape[2]
    depth = math.gcd(elements, 512)
    for start in range(0, elements, depth):
        part = slice(start, start + depth)
        stack = jnp.concatenate(
            [w[0, :, part] for w in weights] + [w[1, :, part] for w in weights], axis=0
        )
        wide = jnp.concatenate([signals[0, part, :], signals[1, part, :]], axis=1)
        product = jnp.dot(stack, wide, preferred_element_type=jnp.float32)
        if start:
            total[...] += product
        else:
            total[...] = product
    rows, samples = total.shape[0] // 2, signals.shape[2]
    out[0] = (total[:rows, :samples] - total[rows:, samples:]).astype(jnp.bfloat16)
    out[1] = (total[:rows, samples:] + total[rows:, :samples]).astype(jnp.bfloat16)


def form_beams(weights, signals):
    pieces = len(weights)
    rows, elements = weights[0].shape[1:]
    samples = signals.shape[2]
    all_rows = pieces * rows
    whole = pl.BlockSpec(memory_space=pltpu.VMEM)
    return pl.pallas_call(
        functools.partial(beams_kernel, pieces),
        in_specs=[whole] * (pieces + 1),
        out_specs=whole,
        out_shape=jax.ShapeDtypeStruct((2, all_rows, samples), jnp.bfloat16),
        scratch_shapes=[pltpu.VMEM((2 * all_rows, 2 * samples), jnp.float32)],
        compiler_params=pltpu.CompilerParams(vmem_limit_bytes=24 * MEBI),
        cost_estimate=pl.CostEstimate(
            flops=8 * all_rows * elements * samples,
            bytes_accessed=4 * elements * (all_rows + samples),
            transcendentals=0,
        ),
        name="form_beams",
    )(*weights, signals)


def order_kernel(parts, *refs):
    select, beams, out = refs[0], refs[1 : 1 + parts], refs[-1]
    real = jnp.concatenate([b[0] for b in beams], axis=0)
    imag = jnp.concatenate([b[1] for b in beams], axis=0)
    both = jnp.concatenate([real, imag], axis=1)
    samples = real.shape[1]
    for d in range(select.shape[0]):
        picked = jnp.dot(select[d], both, preferred_element_type=jnp.float32)
        out[d, 0] = picked[:, :samples].astype(jnp.bfloat16)
        out[d, 1] = picked[:, samples:].astype(jnp.bfloat16)


def order_beams(select, beams):
    tiles, rows, count = select.shape
    samples = beams[0].shape[2]
    whole = pl.BlockSpec(memory_space=pltpu.VMEM)
    return pl.pallas_call(
        functools.partial(order_kernel, len(beams)),
        in_specs=[whole] * (1 + len(beams)),
        out_specs=whole,
        out_shape=jax.ShapeDtypeStruct((tiles, 2, rows, samples), jnp.bfloat16),
        compiler_params=pltpu.CompilerParams(vmem_limit_bytes=24 * MEBI),
        cost_estimate=pl.CostEstimate(
            flops=4 * tiles * rows * count * samples,
            bytes_accessed=2 * tiles * rows * (count + 2 * samples),
            transcendentals=0,
        ),
        name="order_beams",
    )(select, *beams)


def bit_gaps(real, imag, index, scratch):
    shift = 8.0 * LEVEL * LEVEL
    for axis, field in ((0, real), (1, imag)):
        step = field * (2.0 * LEVEL)
        triple = field * (6.0 * LEVEL)
        scratch[axis * 4] = shift + triple
        scratch[axis * 4 + 1] = step
        scratch[axis * 4 + 2] = -step
        scratch[axis * 4 + 3] = shift - triple
    far = [scratch[index[label]] + scratch[index[16 + label]] for label in range(16)]
    least = jnp.minimum
    low = [
        least(least(far[b], far[b + 4]), least(far[b + 8], far[b + 12])) for b in range(4)
    ]
    high = [
        least(least(far[4 * b], far[4 * b + 1]), least(far[4 * b + 2], far[4 * b + 3]))
        for b in range(4)
    ]
    gaps = []
    for part in (low, high):
        gaps.append(least(part[1], part[3]) - least(part[0], part[2]))
        gaps.append(least(part[2], part[3]) - least(part[0], part[1]))
    return gaps


def expand(signs, coefs, base):
    terms = [coefs[base + t] + signs[3] * coefs[base + t + 8] for t in range(8)]
    terms = [terms[t] + signs[2] * terms[t + 4] for t in range(4)]
    terms = [terms[t] + signs[1] * terms[t + 2] for t in range(2)]
    return terms[0] + signs[0] * terms[1]


def soft_kernel(shape, index, field, first, second, scale, coefs, out, s_one, s_two, rest, scratch):
    blocks, rows, inner, tile = shape
    margin = (rows - inner) // 2
    dot = functools.partial(jnp.dot, preferred_element_type=jnp.float32)
    chunk = 16

    def tiles(value):
        return value.reshape(chunk // 8, 8, LANES)

    def soften(real, imag, start, slot):
        gaps = bit_gaps(real, imag, index, scratch.at[slot])
        half = tiles(scale[pl.ds(start, chunk), :])
        signs = [jnp.tanh(gap * half) for gap in gaps]
        return [
            expand(signs, coefs, base).reshape(chunk, LANES).astype(jnp.bfloat16)
            for base in (0, 16)
        ]

    width = first.shape[1] // 2

    @pl.when(pl.program_id(0) == 0)
    def _():
        s_one[...] = jnp.zeros_like(s_one)
        s_two[...] = jnp.zeros_like(s_two)

    count = 0
    for block in range(blocks):
        lanes = pl.ds(block * LANES, LANES)
        for start in range(0, rows, chunk):
            real = tiles(field[block, 0, start : start + chunk, :].astype(jnp.float32))
            imag = tiles(field[block, 1, start : start + chunk, :].astype(jnp.float32))
            a, b = soften(real, imag, start, count % 2)
            s_one[start : start + chunk, lanes] = a
            s_one[width + start : width + start + chunk, lanes] = b
            count += 1
    rest[...] = dot(first[...], s_one[...])
    for block in range(blocks):
        lanes = pl.ds(block * LANES, LANES)
        for start in range(0, inner, chunk):
            away = start + margin
            real = field[block, 0, away : away + chunk, :].astype(jnp.float32) - rest[
                start : start + chunk, lanes
            ]
            imag = field[block, 1, away : away + chunk, :].astype(jnp.float32) - rest[
                inner + start : inner + start + chunk, lanes
            ]
            a, b = soften(tiles(real), tiles(imag), away, count % 2)
            s_two[start : start + chunk, lanes] = a
            s_two[width + start : width + start + chunk, lanes] = b
            count += 1
    rest[0 : 2 * tile, :] = dot(second[...], s_two[...])
    for block in range(blocks):
        lanes = pl.ds(block * LANES, LANES)
        for start in range(0, tile, chunk):
            away = start + 2 * margin
            real = field[block, 0, away : away + chunk, :].astype(jnp.float32) - rest[
                start : start + chunk, lanes
            ]
            imag = field[block, 1, away : away + chunk, :].astype(jnp.float32) - rest[
                tile + start : tile + start + chunk, lanes
            ]
            gaps = bit_gaps(tiles(real), tiles(imag), index, scratch.at[count % 2])
            whole = 2.0 * tiles(scale[away : away + chunk, :])
            for bit in range(4):
                out[bit, start : start + chunk, lanes] = (
                    (gaps[bit] * whole).reshape(chunk, LANES).astype(jnp.bfloat16)
                )
            count += 1


def cancel(index, field, first, second, scale, coefs):
    sources, _, rows, samples = field.shape
    inner, tile = first.shape[0] // 2, second.shape[0] // 2
    blocks = 2
    wide = blocks * samples
    elements = sources * samples
    return pl.pallas_call(
        functools.partial(soft_kernel, (blocks, rows, inner, tile)),
        grid=(sources // blocks,),
        in_specs=[
            pl.BlockSpec(memory_space=pltpu.SMEM),
            pl.BlockSpec((blocks, 2, rows, samples), lambda s: (s, 0, 0, 0)),
            pl.BlockSpec(first.shape, lambda s: (0, 0)),
            pl.BlockSpec(second.shape, lambda s: (0, 0)),
            pl.BlockSpec(scale.shape, lambda s: (0, 0)),
            pl.BlockSpec(coefs.shape, lambda s: (0, 0, 0)),
        ],
        out_specs=pl.BlockSpec((4, tile, wide), lambda s: (0, 0, s)),
        out_shape=jax.ShapeDtypeStruct((4, tile, elements), jnp.bfloat16),
        scratch_shapes=[
            pltpu.VMEM((first.shape[1], wide), jnp.bfloat16),
            pltpu.VMEM((second.shape[1], wide), jnp.bfloat16),
            pltpu.VMEM((2 * inner, wide), jnp.float32),
            pltpu.VMEM((2, 8, 2, 8, LANES), jnp.float32),
        ],
        compiler_params=pltpu.CompilerParams(vmem_limit_bytes=24 * MEBI),
        cost_estimate=pl.CostEstimate(
            flops=130 * (rows + inner + tile) * elements,
            bytes_accessed=4 * rows * elements + 8 * tile * elements,
            transcendentals=4 * (rows + inner) * elements,
        ),
        name="cancel",
    )(index, field, first, second, scale, coefs)


class Places:
    def __init__(self, mesh):
        self.tm, self.beam = mesh.shape["tm"], mesh.shape["beam"]
        self.square = self.tm == 4 and self.beam == 8

    def flat(self, y, x, z, core):
        return (y * 2 + x) * self.beam + z * 2 + core

    def swap(self, value, y=0, x=0, z=0, core=0):
        mask = self.flat(y, x, z, core)
        pairs = [(i, i ^ mask) for i in range(self.tm * self.beam)]
        return lax.ppermute(value, ("tm", "beam"), pairs)


def after(value, *others):
    return lax.optimization_barrier((value, *others))[0]


MASKS = [(y, x, z, core) for z in (0, 2) for y in range(2) for x in range(2) for core in range(2)]


def rows_held(places, rows):
    if not places.square:
        return jnp.arange(places.tm * places.beam * rows, dtype=jnp.int32)
    masks = [places.flat(y, x, z ^ near, core) for near in (0, 1) for y, x, z, core in MASKS]
    me = lax.axis_index("tm") * places.beam + lax.axis_index("beam")
    source = me ^ np.array(masks, np.int32)
    held = source[:, None] * rows + jnp.arange(rows, dtype=jnp.int32)[None, :]
    return held.reshape(-1)


def all_beams(places, element_signals, beam_weights, ready):
    if not places.square:
        gathered = lax.all_gather(beam_weights, ("tm", "beam"), axis=1, tiled=True)
        return [form_beams([gathered], element_signals)]
    swap, w = places.swap, beam_weights
    w_z, w_x, w_y = swap(w, z=2), swap(w, x=1), swap(w, y=1)
    far = swap(after(element_signals, *ready), z=1)
    w_xy = swap(after(w_x, w_y), y=1)
    w_xz, w_yz = swap(after(w_z, w_y), x=1), swap(after(w_z, w_y), y=1)
    w_c, w_xc = swap(after(w, w_z), core=1), swap(after(w_x, w_z), core=1)
    w_yc, w_zc = swap(after(w_y, w_xy), core=1), swap(after(w_z, w_xy), core=1)
    w_xyc = swap(after(w_xy, w_zc), core=1)
    w_xyz = swap(after(w_yz, w_xz), x=1)
    w_xzc = swap(after(w_xz, w_xyc), core=1)
    w_yzc = swap(after(w_yz, w_xyc), core=1)
    w_xyzc = swap(w_xyz, core=1)
    pieces = [w, w_c, w_x, w_xc, w_y, w_yc, w_xy, w_xyc]
    pieces += [w_z, w_zc, w_xz, w_xzc, w_yz, w_yzc, w_xyz, w_xyzc]
    mine = form_beams(pieces, element_signals)
    other = form_beams(pieces, after(far, mine))
    return [mine, swap(other, z=1)]


def tables_kernel(shape, labels, taken, own, index, coefs, first, second, scale):
    slots, rows, inner, tile = shape
    margin = (rows - inner) // 2
    term = lax.broadcasted_iota(jnp.int32, (16, LANES), 0)
    sums = [jnp.zeros((16, LANES), jnp.float32) for _ in range(2)]
    for point in range(16):
        label = labels[point]
        index[label] = point // 4
        index[16 + label] = 4 + point % 4
        odd = term & label
        odd = odd ^ (odd >> 2)
        odd = (odd ^ (odd >> 1)) & 1
        sign = (1 - 2 * odd).astype(jnp.float32)
        for axis, step in ((0, point // 4), (1, point % 4)):
            sums[axis] += sign * ((2 * step - 3) * LEVEL / 16.0)
    for axis in range(2):
        for t in range(16):
            coefs[axis * 16 + t] = jnp.broadcast_to(sums[axis][t : t + 1, :], (8, LANES))
    scale[...] = jnp.broadcast_to(0.5 / taken[:, 3 * slots : 3 * slots + 1], scale.shape)

    def matrix(out, skip, height, which):
        beams = jnp.broadcast_to(own[which : which + 1, :], (height, own.shape[1]))
        real = jnp.zeros(beams.shape, jnp.float32)
        imag = jnp.zeros(beams.shape, jnp.float32)
        for k in range(slots):
            near, r, i = (
                taken[skip : skip + height, g * slots + k : g * slots + k + 1] for g in range(3)
            )
            hit = near == beams
            real += jnp.where(hit, r, 0.0)
            imag += jnp.where(hit, i, 0.0)
        width = own.shape[1]
        out[:height, :width] = real.astype(jnp.bfloat16)
        out[:height, width:] = (-imag).astype(jnp.bfloat16)
        out[height:, :width] = imag.astype(jnp.bfloat16)
        out[height:, width:] = real.astype(jnp.bfloat16)

    matrix(first, margin, inner, 0)
    matrix(second, 2 * margin, tile, 1)


def tables(bit_labels, taken, own, slots, tile):
    rows, width = taken.shape[0], own.shape[1]
    inner = rows - 2 * COLS
    vmem, smem = (pl.BlockSpec(memory_space=m) for m in (pltpu.VMEM, pltpu.SMEM))
    return pl.pallas_call(
        functools.partial(tables_kernel, (slots, rows, inner, tile)),
        in_specs=[smem, vmem, vmem],
        out_specs=[smem, vmem, vmem, vmem, vmem],
        out_shape=[
            jax.ShapeDtypeStruct((32,), jnp.int32),
            jax.ShapeDtypeStruct((32, 8, LANES), jnp.float32),
            jax.ShapeDtypeStruct((2 * inner, 2 * width), jnp.bfloat16),
            jax.ShapeDtypeStruct((2 * tile, 2 * width), jnp.bfloat16),
            jax.ShapeDtypeStruct((rows, LANES), jnp.float32),
        ],
        compiler_params=pltpu.CompilerParams(vmem_limit_bytes=16 * MEBI),
        cost_estimate=pl.CostEstimate(
            flops=60 * rows * width, bytes_accessed=16 * rows * width, transcendentals=0
        ),
        name="tables",
    )(bit_labels, taken, own)


def on_device(places, element_signals, beam_weights, beam_order, neighbours, leakage, noise_var, bit_labels):
    count = beam_order.shape[0]
    tile = count // places.beam
    rows = tile + 2 * HALO
    slots = neighbours.shape[1]
    padded = jnp.pad(beam_order, (HALO, HALO), constant_values=-1)
    windows = jnp.stack([padded[d * tile : d * tile + rows] for d in range(places.beam)])
    own = lax.dynamic_slice_in_dim(padded, lax.axis_index("beam") * tile, rows)
    width = -(-rows // LANES) * LANES
    sides = jnp.stack(
        [
            jnp.pad(own, (0, width - rows), constant_values=-1),
            jnp.pad(own[COLS:-COLS], (0, width - rows + 2 * COLS), constant_values=-1),
        ]
    ).astype(jnp.float32)
    table = jnp.concatenate(
        [
            neighbours.astype(jnp.float32),
            leakage[0].astype(jnp.float32),
            leakage[1].astype(jnp.float32),
            noise_var[:, None],
        ],
        axis=1,
    )
    taken = jnp.take(table, own, axis=0, mode="clip")
    index, coefs, first, second, scale = tables(bit_labels, taken, sides, slots, tile)
    held = rows_held(places, beam_weights.shape[1])
    select = (windows[:, :, None] == held[None, None, :]).astype(jnp.bfloat16)
    beams = all_beams(places, element_signals, beam_weights, (select, first, second))
    ordered = order_beams(select, beams)
    field = lax.all_to_all(ordered, "beam", split_axis=0, concat_axis=0, tiled=True)
    return cancel(index, field, first, second, scale, coefs)


def solution(mesh):
    in_specs = (
        P(None, None, ("tm", "beam")),
        P(None, ("tm", "beam"), None),
        P(),
        P(),
        P(),
        P(),
        P(),
    )
    return jax.shard_map(
        functools.partial(on_device, Places(mesh)),
        mesh=mesh,
        in_specs=in_specs,
        out_specs=P(None, "beam", "tm"),
        check_vma=False,
    )
```

time: 123 us -> 91.7 us (0.75)
  waiting for transfers between devices: 60.8 us -> 27.4 us
  blocking collectives: 0 us -> 26 us
  local copies, waits for them, and re-layouts: 16.2 us -> 3.05 us
  starting transfers between devices: 18.9 us -> 12.4 us
  other arithmetic: 5.56 us -> 2.82 us
  Pallas kernels: 21 us -> 19.5 us
    all_to_all x0 -> x1, blocking collectives: none -> 26 us  [on_device(): lax.all_to_all(ordered, 'beam', split_axis=0, concat_axis=0, tiled=True)]
    all_to_all x1 -> x0, waiting for transfers between devices: 19.2 us -> none  [on_device(): lax.all_to_all(ordered, 'beam', split_axis=0, concat_axis=0, tiled=True)]
    ppermute x15 -> x17, waiting for transfers between devices: 41.5 us -> 27.4 us  [swap(): return lax.ppermute(value, ('tm', 'beam'), pairs)]
    slice x9 -> x2, local copies, waits for them, and re-layouts: 8.04 us -> 1.16 us  [the longest x1 1.09 us: on_device(): padded[d * tile:d * tile + rows]]
    gather x1 -> x0, local copies, waits for them, and re-layouts: 5.85 us -> none  [on_device(): beam_order[np.clip(starts, 0, count - 1)]]
    concatenate x5 -> x0, other arithmetic: 3.76 us -> none  [the longest x1 1.28 us: all_beams(): jnp.concatenate([places.across_core(part) for part in x_parts], axis=1)]
    all_to_all x1 -> x0, starting transfers between devices: 3.68 us -> none  [on_device(): lax.all_to_all(ordered, 'beam', split_axis=0, concat_axis=0, tiled=True)]
    ppermute x15 -> x17, starting transfers between devices: 15.2 us -> 12.4 us  [swap(): return lax.ppermute(value, ('tm', 'beam'), pairs)]
  transfers between devices with their start and end apart: 16 -> 17, of which waited for: 9 -> 11; matrix products, arithmetic and copies ran while one was open for 17% -> 6% of each run, Pallas kernels for 0% -> 4%
where the time goes in v2:
time: 91.7 us; the launch traced here: 91.3 us
  waiting for transfers between devices  27.4 us (30%)
  blocking collectives  26 us (28%)
  Pallas kernels  19.5 us (21%)
  starting transfers between devices  12.4 us (14%)
  local copies, waits for them, and re-layouts  3.05 us (3%)
  other arithmetic  2.82 us (3%)
    ppermute x17, waiting for transfers between devices, swap(): return lax.ppermute(value, ('tm', 'beam'), pairs)  27.4 us
    all_to_all x1, blocking collectives, on_device(): lax.all_to_all(ordered, 'beam', split_axis=0, concat_axis=0, tiled=True)  26 us
    pallas_call x1, Pallas kernels, cancel(): pl.pallas_call(functools.partial(soft_kernel, (blocks, rows, inner, tile)...  14 us
    ppermute x17, starting transfers between devices, swap(): return lax.ppermute(value, ('tm', 'beam'), pairs)  12.4 us
    pallas_call x2, Pallas kernels, form_beams(): pl.pallas_call(functools.partial(beams_kernel, pieces), in_specs=[whole]...  2.5 us
    pallas_call x1, Pallas kernels, tables(): pl.pallas_call(functools.partial(tables_kernel, (slots, rows, inner, tile...  2 us
  transfers between devices with their start and end apart: 17, of which 11 were waited for; matrix products, arithmetic and copies ran while one was open for 6% of the time, Pallas kernels for 4%

profile of v2, /device:TPU:0, one launch (start us, length us, event | category | flops | bytes accessed | tf_op | source)
XLA Modules:
  0.0 91.3 jit_solution(16807673012167283726)
XLA Ops:
  0.0 3.0 %collective-permute-start.4 = (bf16[2,32,2048]{2,1,0:T(8,128)(2,1)}, bf16[2,32,2048]{2,1,0:T(8,128)(2,1)S(1)}, u32[]{:S(2)}, u32[]{:S(2)}) collective-permute-start(bf16[2,32,2048]{2,1,0:T(8,128)(2,1)} %refs_0_.3), channel_id=1, source_target_pairs={{0,16},{1,17},{2,18},{3,19},{4,20},{5,21},{6,22},{7,23},{8,24},{9,... | collective-permute-start | bytes 786440 | tf_op jit(solution)/shard_map/ppermute | solution.py:240
  3.0 1.5 %collective-permute-start.2 = (bf16[2,32,2048]{2,1,0:T(8,128)(2,1)}, bf16[2,32,2048]{2,1,0:T(8,128)(2,1)S(1)}, u32[]{:S(2)}, u32[]{:S(2)}) collective-permute-start(bf16[2,32,2048]{2,1,0:T(8,128)(2,1)} %refs_0_.3), channel_id=1, source_target_pairs={{0,8},{1,9},{2,10},{3,11},{4,12},{5,13},{6,14},{7,15},{8,0},{9,1},... | collective-permute-start | bytes 786440 | tf_op jit(solution)/shard_map/ppermute | solution.py:240
  4.5 2.6 %collective-permute-start = (bf16[2,32,2048]{2,1,0:T(8,128)(2,1)}, bf16[2,32,2048]{2,1,0:T(8,128)(2,1)S(1)}, u32[]{:S(2)}, u32[]{:S(2)}) collective-permute-start(bf16[2,32,2048]{2,1,0:T(8,128)(2,1)} %refs_0_.3), channel_id=1, source_target_pairs={{0,4},{1,5},{2,6},{3,7},{4,0},{5,1},{6,2},{7,3},{8,12},{9,13},{10,... | collective-permute-start | bytes 786440 | tf_op jit(solution)/shard_map/ppermute | solution.py:240
  7.1 1.1 %pad_slice_fusion = (s32[192]{0:T(256)S(1)}, s32[192]{0:T(256)S(1)}, s32[192]{0:T(256)S(1)}, s32[192]{0:T(256)S(1)}, s32[192]{0:T(256)S(1)}, /*index=5*/s32[192]...) fusion(s32[1024]{0:T(1024)} %param.10, s32[]{:T(128)S(6)} %select_n.3), kind=kLoop, calls=%fused_computation.8 | loop fusion | bytes 17156 | tf_op jit(solution)/shard_map/slice | solution.py:353
  8.3 0.7 xor_multiply_fusion
  9.1 0.8 convert_element_type.21
  9.9 0.9 fusion.2
  10.8 0.7 pad_maximum_fusion
  11.7 0.7 gather_fusion
  12.4 0.6 compare_convert_fusion.refs_0_
  13.0 0.6 collective-permute-start.5
  13.6 2.0 %tables.1 = (s32[32]{0:T(128)S(1)}, f32[32,8,128]{2,1,0:T(8,128)S(1)}, bf16[320,512]{1,0:T(8,128)(2,1)S(1)}, bf16[256,512]{1,0:T(8,128)(2,1)S(1)}, f32[192,128]{1,0:T(8,128)S(1)}) custom-call(s32[16]{0:T(128)S(1)} %copy-done.2, f32[192,19]{1,0:T(8,128)S(1)} %gather_fusion, f32[2,256]{1,0:T(2,128)S(1)} %add_convert_fusion.own), custom_call_target="tpu_custom_call" | custom-call | flops 2949120 | bytes 786432 | tf_op jit(solution)/shard_map/tables/pallas_call | solution.py:328
  15.7 1.6 %collective-permute-start.15 = (bf16[2,2048,128]{2,1,0:T(8,128)(2,1)S(1)}, bf16[2,2048,128]{2,1,0:T(8,128)(2,1)S(1)}, u32[]{:S(2)}, u32[]{:S(2)}) collective-permute-start(bf16[2,2048,128]{2,1,0:T(8,128)(2,1)S(1)} %copy-done), channel_id=1, source_target_pairs={{0,2},{1,3},{2,0},{3,1},{4,6},{5,7},{6,4},{7,5},{8,10},{9,11},{10,... | collective-permute-start | bytes 3145736 | tf_op jit(solution)/shard_map/ppermute | solution.py:240
  17.3 1.6 %collective-permute-done.refs_8_ = bf16[2,32,2048]{2,1,0:T(8,128)(2,1)S(1)} collective-permute-done((bf16[2,32,2048]{2,1,0:T(8,128)(2,1)}, bf16[2,32,2048]{2,1,0:T(8,128)(2,1)S(1)}, u32[]{:S(2)}, u32[]{:S(2)}) %collective-permute-start) | collective-permute-done | bytes 262176 | tf_op jit(solution)/shard_map/ppermute | solution.py:240
  18.9 0.5 collective-permute-start.11
  19.3 0.5 collective-permute-start.9
  19.8 0.5 collective-permute-done.5.refs_6_
  20.3 5.6 %collective-permute-done.11.refs_12_ = bf16[2,32,2048]{2,1,0:T(8,128)(2,1)S(1)} collective-permute-done((bf16[2,32,2048]{2,1,0:T(8,128)(2,1)S(1)}, bf16[2,32,2048]{2,1,0:T(8,128)(2,1)S(1)}, u32[]{:S(2)}, u32[]{:S(2)}) %collective-permute-start.11) | collective-permute-done | bytes 262176 | tf_op jit(solution)/shard_map/ppermute | solution.py:240
  26.1 0.5 collective-permute-start.13
  26.6 0.5 collective-permute-start.1
  27.2 5.3 %collective-permute-done.13.refs_14_ = bf16[2,32,2048]{2,1,0:T(8,128)(2,1)S(1)} collective-permute-done((bf16[2,32,2048]{2,1,0:T(8,128)(2,1)S(1)}, bf16[2,32,2048]{2,1,0:T(8,128)(2,1)S(1)}, u32[]{:S(2)}, u32[]{:S(2)}) %collective-permute-start.13) | collective-permute-done | bytes 262176 | tf_op jit(solution)/shard_map/ppermute | solution.py:240
  32.5 0.5 collective-permute-start.14
  33.1 0.4 collective-permute-start.10
  33.5 0.5 collective-permute-done.6.refs_5_
  34.4 0.4 collective-permute-done.12.refs_13_
  35.2 1.2 %form_beams.2.refs_1_ = bf16[2,512,128]{2,1,0:T(8,128)(2,1)S(1)} custom-call(bf16[2,32,2048]{2,1,0:T(8,128)(2,1)S(1)} %copy-done.1, bf16[2,32,2048]{2,1,0:T(8,128)(2,1)S(1)} %collective-permute-done.1.refs_1_, bf16[2,32,2048]{2,1,0:T(8,128)(2,1)S(1)} %collective-permute-done.2.refs_2_, bf16[2,32,2048]{2,1,0:T(8,128)(2,1)S(1)} %collective-permute-done.3.refs_3_, ...), custom_call_target="tpu_custom_call" | custom-call | flops 1073741824 | bytes 5242880 | tf_op jit(solution)/shard_map/form_beams/pallas_call | solution.py:45
  36.4 4.8 %collective-permute-done.15.refs_16_ = bf16[2,2048,128]{2,1,0:T(8,128)(2,1)S(1)} collective-permute-done((bf16[2,2048,128]{2,1,0:T(8,128)(2,1)S(1)}, bf16[2,2048,128]{2,1,0:T(8,128)(2,1)S(1)}, u32[]{:S(2)}, u32[]{:S(2)}) %collective-permute-start.15) | collective-permute-done | bytes 1048608 | tf_op jit(solution)/shard_map/ppermute | solution.py:240
  41.2 1.2 %form_beams.3 = bf16[2,512,128]{2,1,0:T(8,128)(2,1)S(1)} custom-call(bf16[2,32,2048]{2,1,0:T(8,128)(2,1)S(1)} %copy-done.1, bf16[2,32,2048]{2,1,0:T(8,128)(2,1)S(1)} %collective-permute-done.1.refs_1_, bf16[2,32,2048]{2,1,0:T(8,128)(2,1)S(1)} %collective-permute-done.2.refs_2_, bf16[2,32,2048]{2,1,0:T(8,128)(2,1)S(1)} %collective-permute-done.3.refs_3_, ...), custom_call_target="tpu_custom_call" | custom-call | flops 1073741824 | bytes 5242880 | tf_op jit(solution)/shard_map/form_beams/pallas_call | solution.py:45
  42.6 7.7 %collective-permute-done.16.refs_2_ = bf16[2,512,128]{2,1,0:T(8,128)(2,1)S(1)} collective-permute-done((bf16[2,512,128]{2,1,0:T(8,128)(2,1)S(1)}, bf16[2,512,128]{2,1,0:T(8,128)(2,1)S(1)}, u32[]{:S(2)}, u32[]{:S(2)}) %collective-permute-start.16) | collective-permute-done | bytes 262176 | tf_op jit(solution)/shard_map/ppermute | solution.py:240
  50.3 1.0 %order_beams.1 = bf16[8,2,192,128]{3,2,1,0:T(8,128)(2,1)S(1)} custom-call(bf16[8,192,1024]{2,1,0:T(8,128)(2,1)S(1)} %compare_convert_fusion.refs_0_, bf16[2,512,128]{2,1,0:T(8,128)(2,1)S(1)} %form_beams.2.refs_1_, bf16[2,512,128]{2,1,0:T(8,128)(2,1)S(1)} %collective-permute-done.16.refs_2_), custom_call_target="tpu_custom_call" | custom-call | flops 805306368 | bytes 3932160 | tf_op jit(solution)/shard_map/order_beams/pallas_call | solution.py:77
  51.3 26.0 %all_to_all.5.field = bf16[8,2,192,128]{3,2,1,0:T(8,128)(2,1)S(1)} all-to-all(bf16[8,2,192,128]{3,2,1,0:T(8,128)(2,1)S(1)} %order_beams.1), channel_id=1, replica_groups=mesh['tm'=4,'beam'=8] {'beam'}, dimensions={0} | all-to-all | bytes 1572864 | tf_op jit(solution)/shard_map/all_to_all | solution.py:377
  77.3 14.0 %cancel.1 = bf16[4,128,1024]{2,1,0:T(8,128)(2,1)} custom-call(s32[32]{0:T(128)S(1)} %get-tuple-element.22.index, bf16[8,2,192,128]{3,2,1,0:T(8,128)(2,1)S(1)} %all_to_all.5.field, bf16[320,512]{1,0:T(8,128)(2,1)S(1)} %get-tuple-element.33.first, bf16[256,512]{1,0:T(8,128)(2,1)S(1)} %get-tuple-element.34.second, f32[192,128]{1,0:T(8,128)S(1)} %get-tuple-element.37.scale, ...), custom_call_target="tpu_custom_call" | custom-call | flops 63897600 | bytes 1835008 | tf_op jit(solution)/shard_map/cancel/pallas_call | solution.py:200
  (31 shorter events, 1.7 us)
Async XLA Ops:
  0.0 26.6 %copy-start.1 = (bf16[2,32,2048]{2,1,0:T(8,128)(2,1)S(1)}, bf16[2,32,2048]{2,1,0:T(8,128)(2,1)}, u32[]{:S(2)}) copy-start(bf16[2,32,2048]{2,1,0:T(8,128)(2,1)} %refs_0_.3) | copy-start | bytes 786436
  0.0 13.6 %copy-start.2 = (s32[16]{0:T(128)S(1)}, s32[16]{0:T(128)}, u32[]{:S(2)}) copy-start(s32[16]{0:T(128)} %labels.1) | copy-start | bytes 196
  0.0 15.6 %copy-start = (bf16[2,2048,128]{2,1,0:T(8,128)(2,1)S(1)}, bf16[2,2048,128]{2,1,0:T(8,128)(2,1)}, u32[]{:S(2)}) copy-start(bf16[2,2048,128]{2,1,0:T(8,128)(2,1)} %refs_16_.1) | copy-start | bytes 3145732
  0.0 13.0 %collective-permute-start.4 = (bf16[2,32,2048]{2,1,0:T(8,128)(2,1)}, bf16[2,32,2048]{2,1,0:T(8,128)(2,1)S(1)}, u32[]{:S(2)}, u32[]{:S(2)}) collective-permute-start(bf16[2,32,2048]{2,1,0:T(8,128)(2,1)} %refs_0_.3), channel_id=1, source_target_pairs={{0,16},{1,17},{2,18},{3,19},{4,20},{5,21},{6,22},{7,23},{8,24},{9,... | collective-permute-start | bytes 786440 | tf_op jit(solution)/shard_map/ppermute | solution.py:240
  3.0 10.0 %collective-permute-start.2 = (bf16[2,32,2048]{2,1,0:T(8,128)(2,1)}, bf16[2,32,2048]{2,1,0:T(8,128)(2,1)S(1)}, u32[]{:S(2)}, u32[]{:S(2)}) collective-permute-start(bf16[2,32,2048]{2,1,0:T(8,128)(2,1)} %refs_0_.3), channel_id=1, source_target_pairs={{0,8},{1,9},{2,10},{3,11},{4,12},{5,13},{6,14},{7,15},{8,0},{9,1},... | collective-permute-start | bytes 786440 | tf_op jit(solution)/shard_map/ppermute | solution.py:240
  4.5 14.3 %collective-permute-start = (bf16[2,32,2048]{2,1,0:T(8,128)(2,1)}, bf16[2,32,2048]{2,1,0:T(8,128)(2,1)S(1)}, u32[]{:S(2)}, u32[]{:S(2)}) collective-permute-start(bf16[2,32,2048]{2,1,0:T(8,128)(2,1)} %refs_0_.3), channel_id=1, source_target_pairs={{0,4},{1,5},{2,6},{3,7},{4,0},{5,1},{6,2},{7,3},{8,12},{9,13},{10,... | collective-permute-start | bytes 786440 | tf_op jit(solution)/shard_map/ppermute | solution.py:240
  13.0 7.3 %collective-permute-start.5 = (bf16[2,32,2048]{2,1,0:T(8,128)(2,1)S(1)}, bf16[2,32,2048]{2,1,0:T(8,128)(2,1)S(1)}, u32[]{:S(2)}, u32[]{:S(2)}) collective-permute-start(bf16[2,32,2048]{2,1,0:T(8,128)(2,1)S(1)} %collective-permute-done.2.refs_2_), channel_id=1, source_target_pairs={{0,16},{1,17},{2,18},{3,19},{4,20},{5,21},{6,22},{7,23},{8,24},{9,... | collective-permute-start | bytes 786440 | tf_op jit(solution)/shard_map/ppermute | solution.py:240
  15.7 25.6 %collective-permute-start.15 = (bf16[2,2048,128]{2,1,0:T(8,128)(2,1)S(1)}, bf16[2,2048,128]{2,1,0:T(8,128)(2,1)S(1)}, u32[]{:S(2)}, u32[]{:S(2)}) collective-permute-start(bf16[2,2048,128]{2,1,0:T(8,128)(2,1)S(1)} %copy-done), channel_id=1, source_target_pairs={{0,2},{1,3},{2,0},{3,1},{4,6},{5,7},{6,4},{7,5},{8,10},{9,11},{10,... | collective-permute-start | bytes 3145736 | tf_op jit(solution)/shard_map/ppermute | solution.py:240
  18.9 7.1 %collective-permute-start.11 = (bf16[2,32,2048]{2,1,0:T(8,128)(2,1)S(1)}, bf16[2,32,2048]{2,1,0:T(8,128)(2,1)S(1)}, u32[]{:S(2)}, u32[]{:S(2)}) collective-permute-start(bf16[2,32,2048]{2,1,0:T(8,128)(2,1)S(1)} %collective-permute-done.refs_8_), channel_id=1, source_target_pairs={{0,16},{1,17},{2,18},{3,19},{4,20},{5,21},{6,22},{7,23},{8,24},{9,... | collective-permute-start | bytes 786440 | tf_op jit(solution)/shard_map/ppermute | solution.py:240
  19.3 6.8 %collective-permute-start.9 = (bf16[2,32,2048]{2,1,0:T(8,128)(2,1)S(1)}, bf16[2,32,2048]{2,1,0:T(8,128)(2,1)S(1)}, u32[]{:S(2)}, u32[]{:S(2)}) collective-permute-start(bf16[2,32,2048]{2,1,0:T(8,128)(2,1)S(1)} %collective-permute-done.refs_8_), channel_id=1, source_target_pairs={{0,8},{1,9},{2,10},{3,11},{4,12},{5,13},{6,14},{7,15},{8,0},{9,1},... | collective-permute-start | bytes 786440 | tf_op jit(solution)/shard_map/ppermute | solution.py:240
  20.3 6.3 %collective-permute-start.7 = (bf16[2,32,2048]{2,1,0:T(8,128)(2,1)S(1)}, bf16[2,32,2048]{2,1,0:T(8,128)(2,1)S(1)}, u32[]{:S(2)}, u32[]{:S(2)}) collective-permute-start(bf16[2,32,2048]{2,1,0:T(8,128)(2,1)S(1)} %collective-permute-done.refs_8_), channel_id=1, source_target_pairs={{0,1},{1,0},{2,3},{3,2},{4,5},{5,4},{6,7},{7,6},{8,9},{9,8},{10,11... | collective-permute-start | bytes 786440 | tf_op jit(solution)/shard_map/ppermute | solution.py:240
  26.1 6.4 %collective-permute-start.13 = (bf16[2,32,2048]{2,1,0:T(8,128)(2,1)S(1)}, bf16[2,32,2048]{2,1,0:T(8,128)(2,1)S(1)}, u32[]{:S(2)}, u32[]{:S(2)}) collective-permute-start(bf16[2,32,2048]{2,1,0:T(8,128)(2,1)S(1)} %collective-permute-done.11.refs_12_), channel_id=1, source_target_pairs={{0,8},{1,9},{2,10},{3,11},{4,12},{5,13},{6,14},{7,15},{8,0},{9,1},... | collective-permute-start | bytes 786440 | tf_op jit(solution)/shard_map/ppermute | solution.py:240
  26.6 5.9 %collective-permute-start.8 = (bf16[2,32,2048]{2,1,0:T(8,128)(2,1)S(1)}, bf16[2,32,2048]{2,1,0:T(8,128)(2,1)S(1)}, u32[]{:S(2)}, u32[]{:S(2)}) collective-permute-start(bf16[2,32,2048]{2,1,0:T(8,128)(2,1)S(1)} %collective-permute-done.5.refs_6_), channel_id=1, source_target_pairs={{0,1},{1,0},{2,3},{3,2},{4,5},{5,4},{6,7},{7,6},{8,9},{9,8},{10,11... | collective-permute-start | bytes 786440 | tf_op jit(solution)/shard_map/ppermute | solution.py:240
  26.6 6.4 %collective-permute-start.1 = (bf16[2,32,2048]{2,1,0:T(8,128)(2,1)S(1)}, bf16[2,32,2048]{2,1,0:T(8,128)(2,1)S(1)}, u32[]{:S(2)}, u32[]{:S(2)}) collective-permute-start(bf16[2,32,2048]{2,1,0:T(8,128)(2,1)S(1)} %copy-done.1), channel_id=1, source_target_pairs={{0,1},{1,0},{2,3},{3,2},{4,5},{5,4},{6,7},{7,6},{8,9},{9,8},{10,11... | collective-permute-start | bytes 786440 | tf_op jit(solution)/shard_map/ppermute | solution.py:240
  27.1 6.0 %collective-permute-start.3 = (bf16[2,32,2048]{2,1,0:T(8,128)(2,1)S(1)}, bf16[2,32,2048]{2,1,0:T(8,128)(2,1)S(1)}, u32[]{:S(2)}, u32[]{:S(2)}) collective-permute-start(bf16[2,32,2048]{2,1,0:T(8,128)(2,1)S(1)} %collective-permute-done.2.refs_2_), channel_id=1, source_target_pairs={{0,1},{1,0},{2,3},{3,2},{4,5},{5,4},{6,7},{7,6},{8,9},{9,8},{10,11... | collective-permute-start | bytes 786440 | tf_op jit(solution)/shard_map/ppermute | solution.py:240
  32.5 1.5 %collective-permute-start.6 = (bf16[2,32,2048]{2,1,0:T(8,128)(2,1)S(1)}, bf16[2,32,2048]{2,1,0:T(8,128)(2,1)S(1)}, u32[]{:S(2)}, u32[]{:S(2)}) collective-permute-start(bf16[2,32,2048]{2,1,0:T(8,128)(2,1)S(1)} %collective-permute-done.4.refs_4_), channel_id=1, source_target_pairs={{0,1},{1,0},{2,3},{3,2},{4,5},{5,4},{6,7},{7,6},{8,9},{9,8},{10,11... | collective-permute-start | bytes 786440 | tf_op jit(solution)/shard_map/ppermute | solution.py:240
  32.5 1.9 %collective-permute-start.14 = (bf16[2,32,2048]{2,1,0:T(8,128)(2,1)S(1)}, bf16[2,32,2048]{2,1,0:T(8,128)(2,1)S(1)}, u32[]{:S(2)}, u32[]{:S(2)}) collective-permute-start(bf16[2,32,2048]{2,1,0:T(8,128)(2,1)S(1)} %collective-permute-done.13.refs_14_), channel_id=1, source_target_pairs={{0,1},{1,0},{2,3},{3,2},{4,5},{5,4},{6,7},{7,6},{8,9},{9,8},{10,11... | collective-permute-start | bytes 786440 | tf_op jit(solution)/shard_map/ppermute | solution.py:240
  33.0 1.8 %collective-permute-start.12 = (bf16[2,32,2048]{2,1,0:T(8,128)(2,1)S(1)}, bf16[2,32,2048]{2,1,0:T(8,128)(2,1)S(1)}, u32[]{:S(2)}, u32[]{:S(2)}) collective-permute-start(bf16[2,32,2048]{2,1,0:T(8,128)(2,1)S(1)} %collective-permute-done.11.refs_12_), channel_id=1, source_target_pairs={{0,1},{1,0},{2,3},{3,2},{4,5},{5,4},{6,7},{7,6},{8,9},{9,8},{10,11... | collective-permute-start | bytes 786440 | tf_op jit(solution)/shard_map/ppermute | solution.py:240
  33.1 2.1 %collective-permute-start.10 = (bf16[2,32,2048]{2,1,0:T(8,128)(2,1)S(1)}, bf16[2,32,2048]{2,1,0:T(8,128)(2,1)S(1)}, u32[]{:S(2)}, u32[]{:S(2)}) collective-permute-start(bf16[2,32,2048]{2,1,0:T(8,128)(2,1)S(1)} %collective-permute-done.9.refs_10_), channel_id=1, source_target_pairs={{0,1},{1,0},{2,3},{3,2},{4,5},{5,4},{6,7},{7,6},{8,9},{9,8},{10,11... | collective-permute-start | bytes 786440 | tf_op jit(solution)/shard_map/ppermute | solution.py:240
  42.5 7.8 %collective-permute-start.16 = (bf16[2,512,128]{2,1,0:T(8,128)(2,1)S(1)}, bf16[2,512,128]{2,1,0:T(8,128)(2,1)S(1)}, u32[]{:S(2)}, u32[]{:S(2)}) collective-permute-start(bf16[2,512,128]{2,1,0:T(8,128)(2,1)S(1)} %form_beams.3), channel_id=1, source_target_pairs={{0,2},{1,3},{2,0},{3,1},{4,6},{5,7},{6,4},{7,5},{8,10},{9,11},{10,... | collective-permute-start | bytes 786440 | tf_op jit(solution)/shard_map/ppermute | solution.py:240

commit v3 on v2

--- a/solution.py
+++ b/solution.py
@@ -1,4 +1,5 @@
 import functools
+import itertools
 import math
 
 import jax
@@ -48,7 +49,7 @@
         out_specs=whole,
         out_shape=jax.ShapeDtypeStruct((2, all_rows, samples), jnp.bfloat16),
         scratch_shapes=[pltpu.VMEM((2 * all_rows, 2 * samples), jnp.float32)],
-        compiler_params=pltpu.CompilerParams(vmem_limit_bytes=24 * MEBI),
+        compiler_params=pltpu.CompilerParams(vmem_limit_bytes=12 * MEBI),
         cost_estimate=pl.CostEstimate(
             flops=8 * all_rows * elements * samples,
             bytes_accessed=4 * elements * (all_rows + samples),
@@ -59,15 +60,15 @@
 
 
 def order_kernel(parts, *refs):
-    select, beams, out = refs[0], refs[1 : 1 + parts], refs[-1]
+    select, beams, outs = refs[0], refs[1 : 1 + parts], refs[1 + parts :]
     real = jnp.concatenate([b[0] for b in beams], axis=0)
     imag = jnp.concatenate([b[1] for b in beams], axis=0)
     both = jnp.concatenate([real, imag], axis=1)
     samples = real.shape[1]
-    for d in range(select.shape[0]):
+    for d, out in enumerate(outs):
         picked = jnp.dot(select[d], both, preferred_element_type=jnp.float32)
-        out[d, 0] = picked[:, :samples].astype(jnp.bfloat16)
-        out[d, 1] = picked[:, samples:].astype(jnp.bfloat16)
+        out[0] = picked[:, :samples].astype(jnp.bfloat16)
+        out[1] = picked[:, samples:].astype(jnp.bfloat16)
 
 
 def order_beams(select, beams):
@@ -77,9 +78,9 @@
     return pl.pallas_call(
         functools.partial(order_kernel, len(beams)),
         in_specs=[whole] * (1 + len(beams)),
-        out_specs=whole,
-        out_shape=jax.ShapeDtypeStruct((tiles, 2, rows, samples), jnp.bfloat16),
-        compiler_params=pltpu.CompilerParams(vmem_limit_bytes=24 * MEBI),
+        out_specs=[whole] * tiles,
+        out_shape=[jax.ShapeDtypeStruct((2, rows, samples), jnp.bfloat16)] * tiles,
+        compiler_params=pltpu.CompilerParams(vmem_limit_bytes=12 * MEBI),
         cost_estimate=pl.CostEstimate(
             flops=4 * tiles * rows * count * samples,
             bytes_accessed=2 * tiles * rows * (count + 2 * samples),
@@ -89,14 +90,13 @@
     )(select, *beams)
 
 
-def bit_gaps(real, imag, index, scratch):
-    shift = 8.0 * LEVEL * LEVEL
+def bit_gaps(real, imag, step, shift, index, scratch):
     for axis, field in ((0, real), (1, imag)):
-        step = field * (2.0 * LEVEL)
-        triple = field * (6.0 * LEVEL)
+        near = field * step
+        triple = near * 3.0
         scratch[axis * 4] = shift + triple
-        scratch[axis * 4 + 1] = step
-        scratch[axis * 4 + 2] = -step
+        scratch[axis * 4 + 1] = near
+        scratch[axis * 4 + 2] = -near
         scratch[axis * 4 + 3] = shift - triple
     far = [scratch[index[label]] + scratch[index[16 + label]] for label in range(16)]
     least = jnp.minimum
@@ -121,109 +121,112 @@
     return terms[0] + signs[0] * terms[1]
 
 
-def soft_kernel(shape, index, field, first, second, scale, coefs, out, s_one, s_two, rest, scratch):
+def cancel_kernel(shape, place, index, *refs):
     blocks, rows, inner, tile = shape
+    fields, refs = refs[:blocks], refs[blocks:]
+    first, second, scale, coefs = refs[:4]
+    out, s_one, s_two, r_one, r_two = refs[-9:-4]
+    spare = itertools.cycle(refs[-4:])
     margin = (rows - inner) // 2
+    width = first.shape[1] // 2
+    chunk = 16
     dot = functools.partial(jnp.dot, preferred_element_type=jnp.float32)
-    chunk = 16
 
     def tiles(value):
         return value.reshape(chunk // 8, 8, LANES)
 
-    def soften(real, imag, start, slot):
-        gaps = bit_gaps(real, imag, index, scratch.at[slot])
-        half = tiles(scale[pl.ds(start, chunk), :])
-        signs = [jnp.tanh(gap * half) for gap in gaps]
-        return [
-            expand(signs, coefs, base).reshape(chunk, LANES).astype(jnp.bfloat16)
-            for base in (0, 16)
-        ]
-
-    width = first.shape[1] // 2
-
-    @pl.when(pl.program_id(0) == 0)
-    def _():
-        s_one[...] = jnp.zeros_like(s_one)
-        s_two[...] = jnp.zeros_like(s_two)
-
-    count = 0
-    for block in range(blocks):
-        lanes = pl.ds(block * LANES, LANES)
-        for start in range(0, rows, chunk):
-            real = tiles(field[block, 0, start : start + chunk, :].astype(jnp.float32))
-            imag = tiles(field[block, 1, start : start + chunk, :].astype(jnp.float32))
-            a, b = soften(real, imag, start, count % 2)
-            s_one[start : start + chunk, lanes] = a
-            s_one[width + start : width + start + chunk, lanes] = b
-            count += 1
-    rest[...] = dot(first[...], s_one[...])
-    for block in range(blocks):
-        lanes = pl.ds(block * LANES, LANES)
-        for start in range(0, inner, chunk):
-            away = start + margin
-            real = field[block, 0, away : away + chunk, :].astype(jnp.float32) - rest[
-                start : start + chunk, lanes
+    def gaps_at(block, start, rest=None, row=0, height=0):
+        parts = []
+        for part in range(2):
+            value = fields[block][part, pl.ds(start, chunk), :].astype(jnp.float32)
+            if rest is not None:
+                value = value - rest[block, pl.ds(part * height + row, chunk), :]
+            parts.append(tiles(value))
+        step, shift = (tiles(scale[i, pl.ds(start, chunk), :]) for i in range(2))
+        return bit_gaps(*parts, step, shift, index, next(spare))
+
+    def soften(block, out_ref, row, gaps):
+        signs = [jnp.tanh(gap) for gap in gaps]
+        for part in range(2):
+            value = expand(signs, coefs, 16 * part).reshape(chunk, LANES)
+            out_ref[block, pl.ds(part * width + row, chunk), :] = value.astype(jnp.bfloat16)
+
+    def over(height, body):
+        def step(i, carry):
+            for part in range(2):
+                row = pl.multiple_of((2 * i + part) * chunk, chunk)
+                for block in range(blocks):
+                    body(block, row)
+            return carry
+
+        lax.fori_loop(0, height // (2 * chunk), step, 0)
+
+    for ref, used_rows in ((s_one, rows), (s_two, inner)):
+        if used_rows < width:
+            blank = jnp.zeros((width - used_rows, LANES), jnp.bfloat16)
+            for block in range(blocks):
+                ref[block, used_rows:width, :] = blank
+                ref[block, width + used_rows :, :] = blank
+
+    def first_round(block, row):
+        soften(block, s_one, row, gaps_at(block, row))
+
+    def second_round(block, row):
+        soften(block, s_two, row, gaps_at(block, row + margin, r_one, row, inner))
+
+    def metrics(block, row):
+        core = place[1] if block == 0 else 1 - place[1]
+        lanes = pl.ds(pl.multiple_of(core * LANES, LANES), LANES)
+        gaps = gaps_at(block, row + 2 * margin, r_two, row, tile)
+        for bit in range(4):
+            value = (gaps[bit] * 2.0).reshape(chunk, LANES)
+            out[bit, pl.ds(row, chunk), lanes] = value.astype(jnp.bfloat16)
+
+    def product(matrix, ref, into):
+        both = jnp.concatenate([ref[block] for block in range(blocks)], axis=1)
+        result = dot(matrix[...], both)
+        for block in range(blocks):
+            into[block] = result[:, block * LANES : (block + 1) * LANES]
+
+    over(rows, first_round)
+    product(first, s_one, r_one)
+    over(inner, second_round)
+    product(second, s_two, r_two)
+    over(tile, metrics)
+
+
+def cancel(place, index, fields, first, second, scale, coefs, elements, before):
+    _, rows, samples = fields[0].shape
+    inner, tile = first.shape[0] // 2, second.shape[0] // 2
+    blocks = len(fields)
+    vmem, smem = (pl.BlockSpec(memory_space=m) for m in (pltpu.VMEM, pltpu.SMEM))
+    given = [] if before is None else [before]
+    wide = blocks * samples
+    return pl.pallas_call(
+        functools.partial(cancel_kernel, (blocks, rows, inner, tile)),
+        grid_spec=pltpu.PrefetchScalarGridSpec(
+            num_scalar_prefetch=1,
+            grid=(1,),
+            in_specs=[smem] + [vmem] * (blocks + 4) + [pl.BlockSpec(memory_space=pl.ANY)] * len(given),
+            out_specs=pl.BlockSpec((4, tile, wide), lambda s, place: (0, 0, place[0])),
+            scratch_shapes=[
+                pltpu.VMEM((blocks, first.shape[1], samples), jnp.bfloat16),
+                pltpu.VMEM((blocks, second.shape[1], samples), jnp.bfloat16),
+                pltpu.VMEM((blocks, 2 * inner, samples), jnp.float32),
+                pltpu.VMEM((blocks, 2 * tile, samples), jnp.float32),
             ]
-            imag = field[block, 1, away : away + chunk, :].astype(jnp.float32) - rest[
-                inner + start : inner + start + chunk, lanes
-            ]
-            a, b = soften(tiles(real), tiles(imag), away, count % 2)
-            s_two[start : start + chunk, lanes] = a
-            s_two[width + start : width + start + chunk, lanes] = b
-            count += 1
-    rest[0 : 2 * tile, :] = dot(second[...], s_two[...])
-    for block in range(blocks):
-        lanes = pl.ds(block * LANES, LANES)
-        for start in range(0, tile, chunk):
-            away = start + 2 * margin
-            real = field[block, 0, away : away + chunk, :].astype(jnp.float32) - rest[
-                start : start + chunk, lanes
-            ]
-            imag = field[block, 1, away : away + chunk, :].astype(jnp.float32) - rest[
-                tile + start : tile + start + chunk, lanes
-            ]
-            gaps = bit_gaps(tiles(real), tiles(imag), index, scratch.at[count % 2])
-            whole = 2.0 * tiles(scale[away : away + chunk, :])
-            for bit in range(4):
-                out[bit, start : start + chunk, lanes] = (
-                    (gaps[bit] * whole).reshape(chunk, LANES).astype(jnp.bfloat16)
-                )
-            count += 1
-
-
-def cancel(index, field, first, second, scale, coefs):
-    sources, _, rows, samples = field.shape
-    inner, tile = first.shape[0] // 2, second.shape[0] // 2
-    blocks = 2
-    wide = blocks * samples
-    elements = sources * samples
-    return pl.pallas_call(
-        functools.partial(soft_kernel, (blocks, rows, inner, tile)),
-        grid=(sources // blocks,),
-        in_specs=[
-            pl.BlockSpec(memory_space=pltpu.SMEM),
-            pl.BlockSpec((blocks, 2, rows, samples), lambda s: (s, 0, 0, 0)),
-            pl.BlockSpec(first.shape, lambda s: (0, 0)),
-            pl.BlockSpec(second.shape, lambda s: (0, 0)),
-            pl.BlockSpec(scale.shape, lambda s: (0, 0)),
-            pl.BlockSpec(coefs.shape, lambda s: (0, 0, 0)),
-        ],
-        out_specs=pl.BlockSpec((4, tile, wide), lambda s: (0, 0, s)),
+            + [pltpu.VMEM((8, 2, 8, LANES), jnp.float32)] * 4,
+        ),
         out_shape=jax.ShapeDtypeStruct((4, tile, elements), jnp.bfloat16),
-        scratch_shapes=[
-            pltpu.VMEM((first.shape[1], wide), jnp.bfloat16),
-            pltpu.VMEM((second.shape[1], wide), jnp.bfloat16),
-            pltpu.VMEM((2 * inner, wide), jnp.float32),
-            pltpu.VMEM((2, 8, 2, 8, LANES), jnp.float32),
-        ],
-        compiler_params=pltpu.CompilerParams(vmem_limit_bytes=24 * MEBI),
+        input_output_aliases={6 + blocks: 0} if given else {},
+        compiler_params=pltpu.CompilerParams(vmem_limit_bytes=12 * MEBI),
         cost_estimate=pl.CostEstimate(
-            flops=130 * (rows + inner + tile) * elements,
-            bytes_accessed=4 * rows * elements + 8 * tile * elements,
-            transcendentals=4 * (rows + inner) * elements,
+            flops=130 * (rows + inner + tile) * wide + 8 * inner * rows * wide,
+            bytes_accessed=4 * rows * wide + 8 * tile * wide,
+            transcendentals=4 * (rows + inner) * wide,
         ),
         name="cancel",
-    )(index, field, first, second, scale, coefs)
+    )(place, index, *fields, first, second, scale, coefs, *given)
 
 
 class Places:
@@ -238,6 +241,10 @@
         mask = self.flat(y, x, z, core)
         pairs = [(i, i ^ mask) for i in range(self.tm * self.beam)]
         return lax.ppermute(value, ("tm", "beam"), pairs)
+
+    def shift(self, value, z, core):
+        pairs = [(i, ((i + 2 * z) % self.beam) ^ core) for i in range(self.beam)]
+        return lax.ppermute(value, "beam", pairs)
 
 
 def after(value, *others):
@@ -260,7 +267,7 @@
 def all_beams(places, element_signals, beam_weights, ready):
     if not places.square:
         gathered = lax.all_gather(beam_weights, ("tm", "beam"), axis=1, tiled=True)
-        return [form_beams([gathered], element_signals)]
+        return form_beams([gathered], element_signals), None
     swap, w = places.swap, beam_weights
     w_z, w_x, w_y = swap(w, z=2), swap(w, x=1), swap(w, y=1)
     far = swap(after(element_signals, *ready), z=1)
@@ -277,7 +284,7 @@
     pieces += [w_z, w_zc, w_xz, w_xzc, w_yz, w_yzc, w_xyz, w_xyzc]
     mine = form_beams(pieces, element_signals)
     other = form_beams(pieces, after(far, mine))
-    return [mine, swap(other, z=1)]
+    return mine, other
 
 
 def tables_kernel(shape, labels, taken, own, index, coefs, first, second, scale):
@@ -298,7 +305,9 @@
     for axis in range(2):
         for t in range(16):
             coefs[axis * 16 + t] = jnp.broadcast_to(sums[axis][t : t + 1, :], (8, LANES))
-    scale[...] = jnp.broadcast_to(0.5 / taken[:, 3 * slots : 3 * slots + 1], scale.shape)
+    half = jnp.broadcast_to(0.5 / taken[:, 3 * slots : 3 * slots + 1], scale.shape[1:])
+    scale[0] = half * (2.0 * LEVEL)
+    scale[1] = half * (8.0 * LEVEL * LEVEL)
 
     def matrix(out, skip, height, which):
         beams = jnp.broadcast_to(own[which : which + 1, :], (height, own.shape[1]))
@@ -334,9 +343,9 @@
             jax.ShapeDtypeStruct((32, 8, LANES), jnp.float32),
             jax.ShapeDtypeStruct((2 * inner, 2 * width), jnp.bfloat16),
             jax.ShapeDtypeStruct((2 * tile, 2 * width), jnp.bfloat16),
-            jax.ShapeDtypeStruct((rows, LANES), jnp.float32),
+            jax.ShapeDtypeStruct((2, rows, LANES), jnp.float32),
         ],
-        compiler_params=pltpu.CompilerParams(vmem_limit_bytes=16 * MEBI),
+        compiler_params=pltpu.CompilerParams(vmem_limit_bytes=12 * MEBI),
         cost_estimate=pl.CostEstimate(
             flops=60 * rows * width, bytes_accessed=16 * rows * width, transcendentals=0
         ),
@@ -369,13 +378,41 @@
         axis=1,
     )
     taken = jnp.take(table, own, axis=0, mode="clip")
+    held = rows_held(places, beam_weights.shape[1])
+    me = lax.axis_index("beam")
+    if places.square:
+        moves = [(0, 0), (0, 1), (1, 0), (1, 1), (3, 0), (3, 1), (2, 0), (2, 1)]
+        z, core = (np.array(v, np.int32) for v in zip(*moves))
+        windows = windows[((me + 2 * z) % places.beam) ^ core]
+    select = (windows[:, :, None] == held[None, None, :]).astype(jnp.bfloat16)
+    mine, other = all_beams(places, element_signals, beam_weights, (select, taken, sides))
+    beams = [mine]
+    if other is not None:
+        beams.append(places.swap(other, z=1))
+        taken = after(taken, other)
     index, coefs, first, second, scale = tables(bit_labels, taken, sides, slots, tile)
-    held = rows_held(places, beam_weights.shape[1])
-    select = (windows[:, :, None] == held[None, None, :]).astype(jnp.bfloat16)
-    beams = all_beams(places, element_signals, beam_weights, (select, first, second))
-    ordered = order_beams(select, beams)
-    field = lax.all_to_all(ordered, "beam", split_axis=0, concat_axis=0, tiled=True)
-    return cancel(index, field, first, second, scale, coefs)
+    select = after(select, first, second, scale, coefs)
+    ordered = list(order_beams(select, beams))
+    chips = places.beam // 2
+    elements = element_signals.shape[2] * places.beam
+    out = None
+    if places.square:
+        fields = ordered[:1] + [
+            places.shift(value, *move) for value, move in zip(ordered[1:6], moves[1:6])
+        ]
+        spots = [((me // 2 - z) % chips, me % 2) for z, _ in moves[::2]]
+    else:
+        fields = list(
+            lax.all_to_all(jnp.stack(ordered), "beam", split_axis=0, concat_axis=0, tiled=True)
+        )
+        spots = [(chip, 0) for chip in range(chips)]
+    for i, spot in enumerate(spots):
+        place = jnp.stack([jnp.asarray(v, jnp.int32) for v in spot])
+        pair = fields[2 * i : 2 * i + 2]
+        out = cancel(place, index, pair, first, second, scale, coefs, elements, out)
+        if places.square and i == 0:
+            fields += [places.shift(after(ordered[j], out), *moves[j]) for j in (6, 7)]
+    return out
 
 
 def solution(mesh):

time: 91.7 us -> 83.8 us (0.914)
  blocking collectives: 26 us -> 0 us
  Pallas kernels: 19.5 us -> 29.4 us
  starting transfers between devices: 12.4 us -> 21.2 us
  waiting for transfers between devices: 27.4 us -> 25.2 us
    all_to_all x1 -> x0, blocking collectives: 26 us -> none  [on_device(): lax.all_to_all(ordered, 'beam', split_axis=0, concat_axis=0, tiled=True)]
    ppermute x0 -> x7, starting transfers between devices: none -> 8.39 us  [shift(): return lax.ppermute(value, 'beam', pairs)]
    pallas_call x1 -> x4, Pallas kernels: 14 us -> 20 us  [cancel(): pl.pallas_call(functools.partial(cancel_kernel, (blocks, rows, inner, til...]
    pallas_call x2, Pallas kernels: 2.5 us -> 5.42 us  [form_beams(): pl.pallas_call(functools.partial(beams_kernel, pieces), in_specs=[whole]...]
    ppermute x17, waiting for transfers between devices: 27.4 us -> 25.2 us  [swap(): return lax.ppermute(value, ('tm', 'beam'), pairs)]
    pallas_call x1, Pallas kernels: 0.98 us -> 1.93 us  [order_beams(): pl.pallas_call(functools.partial(order_kernel, len(beams)), in_specs=[who...]
  transfers between devices with their start and end apart: 17 -> 24, of which waited for: 11 -> 10; matrix products, arithmetic and copies ran while one was open for 6% -> 9% of each run, Pallas kernels for 4% -> 23%
where the time goes in v3:
time: 83.8 us; the launch traced here: 83.3 us
  Pallas kernels  29.4 us (35%)
  waiting for transfers between devices  25.2 us (30%)
  starting transfers between devices  21.2 us (25%)
  other arithmetic  3.73 us (4%)
  local copies, waits for them, and re-layouts  3.65 us (4%)
    ppermute x17, waiting for transfers between devices, swap(): return lax.ppermute(value, ('tm', 'beam'), pairs)  25.2 us
    pallas_call x4, Pallas kernels, cancel(): pl.pallas_call(functools.partial(cancel_kernel, (blocks, rows, inner, til...  20 us
    ppermute x17, starting transfers between devices, swap(): return lax.ppermute(value, ('tm', 'beam'), pairs)  12.8 us
    ppermute x7, starting transfers between devices, shift(): return lax.ppermute(value, 'beam', pairs)  8.39 us
    pallas_call x2, Pallas kernels, form_beams(): pl.pallas_call(functools.partial(beams_kernel, pieces), in_specs=[whole]...  5.42 us
    pallas_call x1, Pallas kernels, tables(): pl.pallas_call(functools.partial(tables_kernel, (slots, rows, inner, tile...  2 us
    pallas_call x1, Pallas kernels, order_beams(): pl.pallas_call(functools.partial(order_kernel, len(beams)), in_specs=[who...  1.93 us
  transfers between devices with their start and end apart: 24, of which 10 were waited for; matrix products, arithmetic and copies ran while one was open for 9% of the time, Pallas kernels for 23%

profile of v3, /device:TPU:0, one launch (start us, length us, event | category | flops | bytes accessed | tf_op | source)
XLA Modules:
  0.0 83.3 jit_solution(5252441495133151545)
XLA Ops:
  0.0 3.0 %collective-permute-start.4 = (bf16[2,32,2048]{2,1,0:T(8,128)(2,1)}, bf16[2,32,2048]{2,1,0:T(8,128)(2,1)}, u32[]{:S(2)}, u32[]{:S(2)}) collective-permute-start(bf16[2,32,2048]{2,1,0:T(8,128)(2,1)} %refs_0_.3), channel_id=1, source_target_pairs={{0,16},{1,17},{2,18},{3,19},{4,20},{5,21},{6,22},{7,23},{8,24},{9,... | collective-permute-start | bytes 786440 | tf_op jit(solution)/shard_map/ppermute | solution.py:243
  3.0 1.5 %collective-permute-start.2 = (bf16[2,32,2048]{2,1,0:T(8,128)(2,1)}, bf16[2,32,2048]{2,1,0:T(8,128)(2,1)}, u32[]{:S(2)}, u32[]{:S(2)}) collective-permute-start(bf16[2,32,2048]{2,1,0:T(8,128)(2,1)} %refs_0_.3), channel_id=1, source_target_pairs={{0,8},{1,9},{2,10},{3,11},{4,12},{5,13},{6,14},{7,15},{8,0},{9,1},... | collective-permute-start | bytes 786440 | tf_op jit(solution)/shard_map/ppermute | solution.py:243
  4.5 2.6 %collective-permute-start = (bf16[2,32,2048]{2,1,0:T(8,128)(2,1)}, bf16[2,32,2048]{2,1,0:T(8,128)(2,1)}, u32[]{:S(2)}, u32[]{:S(2)}) collective-permute-start(bf16[2,32,2048]{2,1,0:T(8,128)(2,1)} %refs_0_.3), channel_id=1, source_target_pairs={{0,4},{1,5},{2,6},{3,7},{4,0},{5,1},{6,2},{7,3},{8,12},{9,13},{10,... | collective-permute-start | bytes 786440 | tf_op jit(solution)/shard_map/ppermute | solution.py:243
  7.1 1.1 %pad_slice_fusion = (s32[192]{0:T(256)S(1)}, s32[192]{0:T(256)S(1)}, s32[192]{0:T(256)S(1)}, s32[192]{0:T(256)S(1)}, s32[192]{0:T(256)S(1)}, /*index=5*/s32[192]...) fusion(s32[1024]{0:T(1024)} %param.12, s32[]{:T(128)S(6)} %select_n.51), kind=kLoop, calls=%fused_computation.9 | loop fusion | bytes 17156 | tf_op jit(solution)/shard_map/slice | solution.py:362
  8.2 0.7 compare_select_fusion
  8.9 0.7 xor_multiply_fusion
  9.7 0.9 %fusion.4 = (bf16[1,1024,6]{1,0,2:T(2,128)(2,1)S(1)}, bf16[1,1024,6]{1,0,2:T(2,128)(2,1)S(1)}) fusion(bf16[2,1024,6]{1,0,2:T(2,128)(2,1)} %param.14), kind=kLoop, calls=%fused_computation.26 | loop fusion | bytes 49152 | tf_op jit(solution)/shard_map/slice | solution.py:374
  10.6 0.8 convert_element_type.21
  11.4 0.7 pad_maximum_fusion
  12.9 0.7 gather_fusion
  14.9 1.6 %collective-permute-start.15 = (bf16[2,2048,128]{2,1,0:T(8,128)(2,1)S(1)}, bf16[2,2048,128]{2,1,0:T(8,128)(2,1)S(1)}, u32[]{:S(2)}, u32[]{:S(2)}) collective-permute-start(bf16[2,2048,128]{2,1,0:T(8,128)(2,1)S(1)} %copy-done), channel_id=1, source_target_pairs={{0,2},{1,3},{2,0},{3,1},{4,6},{5,7},{6,4},{7,5},{8,10},{9,11},{10,... | collective-permute-start | bytes 3145736 | tf_op jit(solution)/shard_map/ppermute | solution.py:243
  16.5 2.4 %collective-permute-done.refs_8_ = bf16[2,32,2048]{2,1,0:T(8,128)(2,1)} collective-permute-done((bf16[2,32,2048]{2,1,0:T(8,128)(2,1)}, bf16[2,32,2048]{2,1,0:T(8,128)(2,1)}, u32[]{:S(2)}, u32[]{:S(2)}) %collective-permute-start) | collective-permute-done | bytes 262176 | tf_op jit(solution)/shard_map/ppermute | solution.py:243
  19.9 2.7 %collective-permute-done.5.refs_6_ = bf16[2,32,2048]{2,1,0:T(8,128)(2,1)S(1)} collective-permute-done((bf16[2,32,2048]{2,1,0:T(8,128)(2,1)}, bf16[2,32,2048]{2,1,0:T(8,128)(2,1)S(1)}, u32[]{:S(2)}, u32[]{:S(2)}) %collective-permute-start.5) | collective-permute-done | bytes 262176 | tf_op jit(solution)/shard_map/ppermute | solution.py:243
  22.6 3.6 %collective-permute-done.9.refs_10_ = bf16[2,32,2048]{2,1,0:T(8,128)(2,1)S(1)} collective-permute-done((bf16[2,32,2048]{2,1,0:T(8,128)(2,1)}, bf16[2,32,2048]{2,1,0:T(8,128)(2,1)S(1)}, u32[]{:S(2)}, u32[]{:S(2)}) %collective-permute-start.9) | collective-permute-done | bytes 262176 | tf_op jit(solution)/shard_map/ppermute | solution.py:243
  26.2 1.2 %collective-permute-done.11.refs_12_ = bf16[2,32,2048]{2,1,0:T(8,128)(2,1)S(1)} collective-permute-done((bf16[2,32,2048]{2,1,0:T(8,128)(2,1)}, bf16[2,32,2048]{2,1,0:T(8,128)(2,1)S(1)}, u32[]{:S(2)}, u32[]{:S(2)}) %collective-permute-start.11) | collective-permute-done | bytes 262176 | tf_op jit(solution)/shard_map/ppermute | solution.py:243
  28.4 5.7 %collective-permute-done.13.refs_14_ = bf16[2,32,2048]{2,1,0:T(8,128)(2,1)S(1)} collective-permute-done((bf16[2,32,2048]{2,1,0:T(8,128)(2,1)S(1)}, bf16[2,32,2048]{2,1,0:T(8,128)(2,1)S(1)}, u32[]{:S(2)}, u32[]{:S(2)}) %collective-permute-start.13) | collective-permute-done | bytes 262176 | tf_op jit(solution)/shard_map/ppermute | solution.py:243
  35.2 1.0 %collective-permute-done.6.refs_5_ = bf16[2,32,2048]{2,1,0:T(8,128)(2,1)S(1)} collective-permute-done((bf16[2,32,2048]{2,1,0:T(8,128)(2,1)}, bf16[2,32,2048]{2,1,0:T(8,128)(2,1)S(1)}, u32[]{:S(2)}, u32[]{:S(2)}) %collective-permute-start.6) | collective-permute-done | bytes 262176 | tf_op jit(solution)/shard_map/ppermute | solution.py:243
  36.8 2.4 %form_beams.2.refs_1_ = bf16[2,512,128]{2,1,0:T(8,128)(2,1)S(1)} custom-call(bf16[2,32,2048]{2,1,0:T(8,128)(2,1)S(1)} %copy-done.2, bf16[2,32,2048]{2,1,0:T(8,128)(2,1)S(1)} %collective-permute-done.1.refs_1_, bf16[2,32,2048]{2,1,0:T(8,128)(2,1)} %collective-permute-done.2.refs_2_, bf16[2,32,2048]{2,1,0:T(8,128)(2,1)S(1)} %collective-permute-done.3.refs_3_, ...), custom_call_target="tpu_custom_call" | custom-call | flops 1073741824 | bytes 5242880 | tf_op jit(solution)/shard_map/form_beams/pallas_call | solution.py:46
  39.2 2.0 %collective-permute-done.15.refs_16_ = bf16[2,2048,128]{2,1,0:T(8,128)(2,1)S(1)} collective-permute-done((bf16[2,2048,128]{2,1,0:T(8,128)(2,1)S(1)}, bf16[2,2048,128]{2,1,0:T(8,128)(2,1)S(1)}, u32[]{:S(2)}, u32[]{:S(2)}) %collective-permute-start.15) | collective-permute-done | bytes 1048608 | tf_op jit(solution)/shard_map/ppermute | solution.py:243
  41.2 3.1 %form_beams.3 = bf16[2,512,128]{2,1,0:T(8,128)(2,1)} custom-call(bf16[2,32,2048]{2,1,0:T(8,128)(2,1)S(1)} %copy-done.2, bf16[2,32,2048]{2,1,0:T(8,128)(2,1)S(1)} %collective-permute-done.1.refs_1_, bf16[2,32,2048]{2,1,0:T(8,128)(2,1)} %collective-permute-done.2.refs_2_, bf16[2,32,2048]{2,1,0:T(8,128)(2,1)S(1)} %collective-permute-done.3.refs_3_, ...), custom_call_target="tpu_custom_call" | custom-call | flops 1073741824 | bytes 5242880 | tf_op jit(solution)/shard_map/form_beams/pallas_call | solution.py:46
  44.8 2.0 %tables.1 = (s32[32]{0:T(128)S(1)}, f32[32,8,128]{2,1,0:T(8,128)S(1)}, bf16[320,512]{1,0:T(8,128)(2,1)S(1)}, bf16[256,512]{1,0:T(8,128)(2,1)S(1)}, f32[2,192,128]{2,1,0:T(8,128)S(1)}) custom-call(s32[16]{0:T(128)S(1)} %copy-done.3, f32[192,19]{1,0:T(8,128)S(1)} %gather_fusion, f32[2,256]{1,0:T(2,128)S(1)} %add_convert_fusion.own), custom_call_target="tpu_custom_call" | custom-call | flops 2949120 | bytes 786432 | tf_op jit(solution)/shard_map/tables/pallas_call | solution.py:337
  46.8 6.0 %collective-permute-done.16.refs_2_ = bf16[2,512,128]{2,1,0:T(8,128)(2,1)} collective-permute-done((bf16[2,512,128]{2,1,0:T(8,128)(2,1)}, bf16[2,512,128]{2,1,0:T(8,128)(2,1)}, u32[]{:S(2)}, u32[]{:S(2)}) %collective-permute-start.16) | collective-permute-done | bytes 262176 | tf_op jit(solution)/shard_map/ppermute | solution.py:243
  52.8 1.9 %order_beams.1 = (bf16[2,192,128]{2,1,0:T(8,128)(2,1)S(1)}, bf16[2,192,128]{2,1,0:T(8,128)(2,1)S(1)}, bf16[2,192,128]{2,1,0:T(8,128)(2,1)S(1)}, bf16[2,192,128]{...) custom-call(bf16[8,192,1024]{2,1,0:T(8,128)(2,1)S(1)} %compare_conve, ...), custom_call_target="tpu_custom_call" | custom-call | flops 805306368 | bytes 3932160 | tf_op jit(solution)/shard_map/order_beams/pallas_call | solution.py:78
  54.8 0.7 collective-permute-start.22
  55.5 2.0 %collective-permute-start.23 = (bf16[2,192,128]{2,1,0:T(8,128)(2,1)S(1)}, bf16[2,192,128]{2,1,0:T(8,128)(2,1)S(1)}, u32[]{:S(2)}, u32[]{:S(2)}) collective-permute-start(bf16[2,192,128]{2,1,0:T(8,128)(2,1)S(1)} %get-tuple-element.62), channel_id=1, source_target_pairs={{0,3},{1,2},{2,5},{3,4},{4,7},{5,6},{6,1},{7,0},{8,11},{9,10},{10,... | collective-permute-start | bytes 294920 | tf_op jit(solution)/shard_map/ppermute | solution.py:247
  57.5 1.6 %collective-permute-start.20 = (bf16[2,192,128]{2,1,0:T(8,128)(2,1)S(1)}, bf16[2,192,128]{2,1,0:T(8,128)(2,1)S(1)}, u32[]{:S(2)}, u32[]{:S(2)}) collective-permute-start(bf16[2,192,128]{2,1,0:T(8,128)(2,1)S(1)} %get-tuple-element.59), channel_id=1, source_target_pairs={{0,6},{1,7},{2,0},{3,1},{4,2},{5,3},{6,4},{7,5},{8,14},{9,15},{10,... | collective-permute-start | bytes 294920 | tf_op jit(solution)/shard_map/ppermute | solution.py:247
  59.1 1.1 %collective-permute-start.21 = (bf16[2,192,128]{2,1,0:T(8,128)(2,1)S(1)}, bf16[2,192,128]{2,1,0:T(8,128)(2,1)S(1)}, u32[]{:S(2)}, u32[]{:S(2)}) collective-permute-start(bf16[2,192,128]{2,1,0:T(8,128)(2,1)S(1)} %get-tuple-element.60), channel_id=1, source_target_pairs={{0,7},{1,6},{2,1},{3,0},{4,3},{5,2},{6,5},{7,4},{8,15},{9,14},{10,... | collective-permute-start | bytes 294920 | tf_op jit(solution)/shard_map/ppermute | solution.py:247
  60.2 5.0 %cancel.4.refs_6_ = bf16[4,128,1024]{2,1,0:T(8,128)(2,1)} custom-call(s32[2]{0:T(128)S(1)} %pad_add_fusion.1.place, s32[32]{0:T(128)S(1)} %get-tuple-element.47.index, bf16[2,192,128]{2,1,0:T(8,128)(2,1)S(1)} %get-tuple-element.54.refs_0_, bf16[2,192,128]{2,1,0:T(8,128)(2,1)S(1)} %collective-permute-done.17.refs_1_, ...), custom_call_target="tpu_custom_call" | custom-call | flops 78888960 | bytes 458752 | tf_op jit(solution)/shard_map/cancel/pallas_call | solution.py:205
  65.8 2.4 %collective-permute-start.18 = (bf16[2,192,128]{2,1,0:T(8,128)(2,1)S(1)}, bf16[2,192,128]{2,1,0:T(8,128)(2,1)S(1)}, u32[]{:S(2)}, u32[]{:S(2)}) collective-permute-start(bf16[2,192,128]{2,1,0:T(8,128)(2,1)S(1)} %get-tuple-element.56), channel_id=1, source_target_pairs={{0,4},{1,5},{2,6},{3,7},{4,0},{5,1},{6,2},{7,3},{8,12},{9,13},{10,... | collective-permute-start | bytes 294920 | tf_op jit(solution)/shard_map/ppermute | solution.py:247
  68.3 5.0 %cancel.5.refs_6_ = bf16[4,128,1024]{2,1,0:T(8,128)(2,1)} custom-call(s32[2]{0:T(128)S(1)} %pad_add_fusion.3.place, s32[32]{0:T(128)S(1)} %get-tuple-element.47.index, bf16[2,192,128]{2,1,0:T(8,128)(2,1)S(1)} %collective-permute-done.22.refs_0_, bf16[2,192,128]{2,1,0:T(8,128)(2,1)S(1)} %collective-permute-done.23.refs_1_, ...), custom_call_target="tpu_custom_call", output_to_operand_aliasing={{}: (8, {})} | custom-call | flops 78888960 | bytes 458752 | tf_op jit(solution)/shard_map/cancel/pallas_call | solution.py:205
  73.3 5.0 %cancel.6.refs_6_ = bf16[4,128,1024]{2,1,0:T(8,128)(2,1)} custom-call(s32[2]{0:T(128)S(1)} %get-tuple-element.75.place, s32[32]{0:T(128)S(1)} %get-tuple-element.47.index, bf16[2,192,128]{2,1,0:T(8,128)(2,1)S(1)} %collective-permute-done.20.refs_0_, bf16[2,192,128]{2,1,0:T(8,128)(2,1)S(1)} %collective-permute-done.21.refs_1_, ...), custom_call_target="tpu_custom_call", output_to_operand_aliasing={{}: (8, {})} | custom-call | flops 78888960 | bytes 458752 | tf_op jit(solution)/shard_map/cancel/pallas_call | solution.py:205
  78.3 5.0 %cancel.7 = bf16[4,128,1024]{2,1,0:T(8,128)(2,1)} custom-call(s32[2]{0:T(128)S(1)} %get-tuple-element.74.place, s32[32]{0:T(128)S(1)} %get-tuple-element.47.index, bf16[2,192,128]{2,1,0:T(8,128)(2,1)S(1)} %collective-permute-done.18.refs_0_, bf16[2,192,128]{2,1,0:T(8,128)(2,1)S(1)} %collective-permute-done.19.refs_1_, ...), custom_call_target="tpu_custom_call", output_to_operand_aliasing={{}: (8, {})} | custom-call | flops 78888960 | bytes 458752 | tf_op jit(solution)/shard_map/cancel/pallas_call | solution.py:205
  (55 shorter events, 7.3 us)
Async XLA Ops:
  0.0 28.4 %copy-start.1 = (bf16[2,32,2048]{2,1,0:T(8,128)(2,1)S(1)}, bf16[2,32,2048]{2,1,0:T(8,128)(2,1)}, u32[]{:S(2)}) copy-start(bf16[2,32,2048]{2,1,0:T(8,128)(2,1)} %refs_0_.3) | copy-start | bytes 786436
  0.0 14.2 %collective-permute-start.4 = (bf16[2,32,2048]{2,1,0:T(8,128)(2,1)}, bf16[2,32,2048]{2,1,0:T(8,128)(2,1)}, u32[]{:S(2)}, u32[]{:S(2)}) collective-permute-start(bf16[2,32,2048]{2,1,0:T(8,128)(2,1)} %refs_0_.3), channel_id=1, source_target_pairs={{0,16},{1,17},{2,18},{3,19},{4,20},{5,21},{6,22},{7,23},{8,24},{9,... | collective-permute-start | bytes 786440 | tf_op jit(solution)/shard_map/ppermute | solution.py:243
  3.0 11.3 %collective-permute-start.2 = (bf16[2,32,2048]{2,1,0:T(8,128)(2,1)}, bf16[2,32,2048]{2,1,0:T(8,128)(2,1)}, u32[]{:S(2)}, u32[]{:S(2)}) collective-permute-start(bf16[2,32,2048]{2,1,0:T(8,128)(2,1)} %refs_0_.3), channel_id=1, source_target_pairs={{0,8},{1,9},{2,10},{3,11},{4,12},{5,13},{6,14},{7,15},{8,0},{9,1},... | collective-permute-start | bytes 786440 | tf_op jit(solution)/shard_map/ppermute | solution.py:243
  4.5 14.4 %collective-permute-start = (bf16[2,32,2048]{2,1,0:T(8,128)(2,1)}, bf16[2,32,2048]{2,1,0:T(8,128)(2,1)}, u32[]{:S(2)}, u32[]{:S(2)}) collective-permute-start(bf16[2,32,2048]{2,1,0:T(8,128)(2,1)} %refs_0_.3), channel_id=1, source_target_pairs={{0,4},{1,5},{2,6},{3,7},{4,0},{5,1},{6,2},{7,3},{8,12},{9,13},{10,... | collective-permute-start | bytes 786440 | tf_op jit(solution)/shard_map/ppermute | solution.py:243
  13.6 1.2 %copy-start = (bf16[2,2048,128]{2,1,0:T(8,128)(2,1)S(1)}, bf16[2,2048,128]{2,1,0:T(8,128)(2,1)}, u32[]{:S(2)}) copy-start(bf16[2,2048,128]{2,1,0:T(8,128)(2,1)} %refs_16_.1) | copy-start | bytes 3145732
  13.6 23.2 %copy-start.2 = (bf16[2,32,2048]{2,1,0:T(8,128)(2,1)S(1)}, bf16[2,32,2048]{2,1,0:T(8,128)(2,1)}, u32[]{:S(2)}) copy-start(bf16[2,32,2048]{2,1,0:T(8,128)(2,1)} %refs_0_.3) | copy-start | bytes 786436
  14.2 8.4 %collective-permute-start.5 = (bf16[2,32,2048]{2,1,0:T(8,128)(2,1)}, bf16[2,32,2048]{2,1,0:T(8,128)(2,1)S(1)}, u32[]{:S(2)}, u32[]{:S(2)}) collective-permute-start(bf16[2,32,2048]{2,1,0:T(8,128)(2,1)} %collective-permute-done.2.refs_2_), channel_id=1, source_target_pairs={{0,16},{1,17},{2,18},{3,19},{4,20},{5,21},{6,22},{7,23},{8,24},{9,... | collective-permute-start | bytes 786440 | tf_op jit(solution)/shard_map/ppermute | solution.py:243
  14.9 26.3 %collective-permute-start.15 = (bf16[2,2048,128]{2,1,0:T(8,128)(2,1)S(1)}, bf16[2,2048,128]{2,1,0:T(8,128)(2,1)S(1)}, u32[]{:S(2)}, u32[]{:S(2)}) collective-permute-start(bf16[2,2048,128]{2,1,0:T(8,128)(2,1)S(1)} %copy-done), channel_id=1, source_target_pairs={{0,2},{1,3},{2,0},{3,1},{4,6},{5,7},{6,4},{7,5},{8,10},{9,11},{10,... | collective-permute-start | bytes 3145736 | tf_op jit(solution)/shard_map/ppermute | solution.py:243
  18.9 7.3 %collective-permute-start.9 = (bf16[2,32,2048]{2,1,0:T(8,128)(2,1)}, bf16[2,32,2048]{2,1,0:T(8,128)(2,1)S(1)}, u32[]{:S(2)}, u32[]{:S(2)}) collective-permute-start(bf16[2,32,2048]{2,1,0:T(8,128)(2,1)} %collective-permute-done.refs_8_), channel_id=1, source_target_pairs={{0,8},{1,9},{2,10},{3,11},{4,12},{5,13},{6,14},{7,15},{8,0},{9,1},... | collective-permute-start | bytes 786440 | tf_op jit(solution)/shard_map/ppermute | solution.py:243
  19.4 7.9 %collective-permute-start.11 = (bf16[2,32,2048]{2,1,0:T(8,128)(2,1)}, bf16[2,32,2048]{2,1,0:T(8,128)(2,1)S(1)}, u32[]{:S(2)}, u32[]{:S(2)}) collective-permute-start(bf16[2,32,2048]{2,1,0:T(8,128)(2,1)} %collective-permute-done.refs_8_), channel_id=1, source_target_pairs={{0,16},{1,17},{2,18},{3,19},{4,20},{5,21},{6,22},{7,23},{8,24},{9,... | collective-permute-start | bytes 786440 | tf_op jit(solution)/shard_map/ppermute | solution.py:243
  22.6 5.3 %collective-permute-start.7 = (bf16[2,32,2048]{2,1,0:T(8,128)(2,1)}, bf16[2,32,2048]{2,1,0:T(8,128)(2,1)S(1)}, u32[]{:S(2)}, u32[]{:S(2)}) collective-permute-start(bf16[2,32,2048]{2,1,0:T(8,128)(2,1)} %collective-permute-done.refs_8_), channel_id=1, source_target_pairs={{0,1},{1,0},{2,3},{3,2},{4,5},{5,4},{6,7},{7,6},{8,9},{9,8},{10,11... | collective-permute-start | bytes 786440 | tf_op jit(solution)/shard_map/ppermute | solution.py:243
  27.3 6.8 %collective-permute-start.13 = (bf16[2,32,2048]{2,1,0:T(8,128)(2,1)S(1)}, bf16[2,32,2048]{2,1,0:T(8,128)(2,1)S(1)}, u32[]{:S(2)}, u32[]{:S(2)}) collective-permute-start(bf16[2,32,2048]{2,1,0:T(8,128)(2,1)S(1)} %collective-permute-done.11.refs_12_), channel_id=1, source_target_pairs={{0,8},{1,9},{2,10},{3,11},{4,12},{5,13},{6,14},{7,15},{8,0},{9,1},... | collective-permute-start | bytes 786440 | tf_op jit(solution)/shard_map/ppermute | solution.py:243
  27.9 6.2 %collective-permute-start.8 = (bf16[2,32,2048]{2,1,0:T(8,128)(2,1)S(1)}, bf16[2,32,2048]{2,1,0:T(8,128)(2,1)S(1)}, u32[]{:S(2)}, u32[]{:S(2)}) collective-permute-start(bf16[2,32,2048]{2,1,0:T(8,128)(2,1)S(1)} %collective-permute-done.5.refs_6_), channel_id=1, source_target_pairs={{0,1},{1,0},{2,3},{3,2},{4,5},{5,4},{6,7},{7,6},{8,9},{9,8},{10,11... | collective-permute-start | bytes 786440 | tf_op jit(solution)/shard_map/ppermute | solution.py:243
  27.9 6.7 %collective-permute-start.3 = (bf16[2,32,2048]{2,1,0:T(8,128)(2,1)}, bf16[2,32,2048]{2,1,0:T(8,128)(2,1)S(1)}, u32[]{:S(2)}, u32[]{:S(2)}) collective-permute-start(bf16[2,32,2048]{2,1,0:T(8,128)(2,1)} %collective-permute-done.2.refs_2_), channel_id=1, source_target_pairs={{0,1},{1,0},{2,3},{3,2},{4,5},{5,4},{6,7},{7,6},{8,9},{9,8},{10,11... | collective-permute-start | bytes 786440 | tf_op jit(solution)/shard_map/ppermute | solution.py:243
  28.4 6.3 %collective-permute-start.1 = (bf16[2,32,2048]{2,1,0:T(8,128)(2,1)S(1)}, bf16[2,32,2048]{2,1,0:T(8,128)(2,1)S(1)}, u32[]{:S(2)}, u32[]{:S(2)}) collective-permute-start(bf16[2,32,2048]{2,1,0:T(8,128)(2,1)S(1)} %copy-done.1), channel_id=1, source_target_pairs={{0,1},{1,0},{2,3},{3,2},{4,5},{5,4},{6,7},{7,6},{8,9},{9,8},{10,11... | collective-permute-start | bytes 786440 | tf_op jit(solution)/shard_map/ppermute | solution.py:243
  34.1 2.0 %collective-permute-start.6 = (bf16[2,32,2048]{2,1,0:T(8,128)(2,1)}, bf16[2,32,2048]{2,1,0:T(8,128)(2,1)S(1)}, u32[]{:S(2)}, u32[]{:S(2)}) collective-permute-start(bf16[2,32,2048]{2,1,0:T(8,128)(2,1)} %collective-permute-done.4.refs_4_), channel_id=1, source_target_pairs={{0,1},{1,0},{2,3},{3,2},{4,5},{5,4},{6,7},{7,6},{8,9},{9,8},{10,11... | collective-permute-start | bytes 786440 | tf_op jit(solution)/shard_map/ppermute | solution.py:243
  34.1 2.0 %collective-permute-start.14 = (bf16[2,32,2048]{2,1,0:T(8,128)(2,1)S(1)}, bf16[2,32,2048]{2,1,0:T(8,128)(2,1)S(1)}, u32[]{:S(2)}, u32[]{:S(2)}) collective-permute-start(bf16[2,32,2048]{2,1,0:T(8,128)(2,1)S(1)} %collective-permute-done.13.refs_14_), channel_id=1, source_target_pairs={{0,1},{1,0},{2,3},{3,2},{4,5},{5,4},{6,7},{7,6},{8,9},{9,8},{10,11... | collective-permute-start | bytes 786440 | tf_op jit(solution)/shard_map/ppermute | solution.py:243
  34.6 1.8 %collective-permute-start.10 = (bf16[2,32,2048]{2,1,0:T(8,128)(2,1)S(1)}, bf16[2,32,2048]{2,1,0:T(8,128)(2,1)S(1)}, u32[]{:S(2)}, u32[]{:S(2)}) collective-permute-start(bf16[2,32,2048]{2,1,0:T(8,128)(2,1)S(1)} %collective-permute-done.9.refs_10_), channel_id=1, source_target_pairs={{0,1},{1,0},{2,3},{3,2},{4,5},{5,4},{6,7},{7,6},{8,9},{9,8},{10,11... | collective-permute-start | bytes 786440 | tf_op jit(solution)/shard_map/ppermute | solution.py:243
  34.7 2.1 %collective-permute-start.12 = (bf16[2,32,2048]{2,1,0:T(8,128)(2,1)S(1)}, bf16[2,32,2048]{2,1,0:T(8,128)(2,1)S(1)}, u32[]{:S(2)}, u32[]{:S(2)}) collective-permute-start(bf16[2,32,2048]{2,1,0:T(8,128)(2,1)S(1)} %collective-permute-done.11.refs_12_), channel_id=1, source_target_pairs={{0,1},{1,0},{2,3},{3,2},{4,5},{5,4},{6,7},{7,6},{8,9},{9,8},{10,11... | collective-permute-start | bytes 786440 | tf_op jit(solution)/shard_map/ppermute | solution.py:243
  39.2 5.6 %copy-start.3 = (s32[16]{0:T(128)S(1)}, s32[16]{0:T(128)}, u32[]{:S(2)}) copy-start(s32[16]{0:T(128)} %labels.1) | copy-start | bytes 196
  44.2 8.5 %collective-permute-start.16 = (bf16[2,512,128]{2,1,0:T(8,128)(2,1)}, bf16[2,512,128]{2,1,0:T(8,128)(2,1)}, u32[]{:S(2)}, u32[]{:S(2)}) collective-permute-start(bf16[2,512,128]{2,1,0:T(8,128)(2,1)} %form_beams.3), channel_id=1, source_target_pairs={{0,2},{1,3},{2,0},{3,1},{4,6},{5,7},{6,4},{7,5},{8,10},{9,11},{10,... | collective-permute-start | bytes 786440 | tf_op jit(solution)/shard_map/ppermute | solution.py:243
  54.7 5.5 %collective-permute-start.17 = (bf16[2,192,128]{2,1,0:T(8,128)(2,1)S(1)}, bf16[2,192,128]{2,1,0:T(8,128)(2,1)S(1)}, u32[]{:S(2)}, u32[]{:S(2)}) collective-permute-start(bf16[2,192,128]{2,1,0:T(8,128)(2,1)S(1)} %get-tuple-element.55), channel_id=1, source_target_pairs={{0,1},{1,0},{2,3},{3,2},{4,5},{5,4},{6,7},{7,6},{8,9},{9,8},{10,11... | collective-permute-start | bytes 294920 | tf_op jit(solution)/shard_map/ppermute | solution.py:247
  54.8 11.0 %collective-permute-start.22 = (bf16[2,192,128]{2,1,0:T(8,128)(2,1)S(1)}, bf16[2,192,128]{2,1,0:T(8,128)(2,1)S(1)}, u32[]{:S(2)}, u32[]{:S(2)}) collective-permute-start(bf16[2,192,128]{2,1,0:T(8,128)(2,1)S(1)} %get-tuple-element.61), channel_id=1, source_target_pairs={{0,2},{1,3},{2,4},{3,5},{4,6},{5,7},{6,0},{7,1},{8,10},{9,11},{10,... | collective-permute-start | bytes 294920 | tf_op jit(solution)/shard_map/ppermute | solution.py:247
  55.5 12.8 %collective-permute-start.23 = (bf16[2,192,128]{2,1,0:T(8,128)(2,1)S(1)}, bf16[2,192,128]{2,1,0:T(8,128)(2,1)S(1)}, u32[]{:S(2)}, u32[]{:S(2)}) collective-permute-start(bf16[2,192,128]{2,1,0:T(8,128)(2,1)S(1)} %get-tuple-element.62), channel_id=1, source_target_pairs={{0,3},{1,2},{2,5},{3,4},{4,7},{5,6},{6,1},{7,0},{8,11},{9,10},{10,... | collective-permute-start | bytes 294920 | tf_op jit(solution)/shard_map/ppermute | solution.py:247
  57.5 15.7 %collective-permute-start.20 = (bf16[2,192,128]{2,1,0:T(8,128)(2,1)S(1)}, bf16[2,192,128]{2,1,0:T(8,128)(2,1)S(1)}, u32[]{:S(2)}, u32[]{:S(2)}) collective-permute-start(bf16[2,192,128]{2,1,0:T(8,128)(2,1)S(1)} %get-tuple-element.59), channel_id=1, source_target_pairs={{0,6},{1,7},{2,0},{3,1},{4,2},{5,3},{6,4},{7,5},{8,14},{9,15},{10,... | collective-permute-start | bytes 294920 | tf_op jit(solution)/shard_map/ppermute | solution.py:247
  59.1 14.2 %collective-permute-start.21 = (bf16[2,192,128]{2,1,0:T(8,128)(2,1)S(1)}, bf16[2,192,128]{2,1,0:T(8,128)(2,1)S(1)}, u32[]{:S(2)}, u32[]{:S(2)}) collective-permute-start(bf16[2,192,128]{2,1,0:T(8,128)(2,1)S(1)} %get-tuple-element.60), channel_id=1, source_target_pairs={{0,7},{1,6},{2,1},{3,0},{4,3},{5,2},{6,5},{7,4},{8,15},{9,14},{10,... | collective-permute-start | bytes 294920 | tf_op jit(solution)/shard_map/ppermute | solution.py:247
  65.2 13.1 %collective-permute-start.19 = (bf16[2,192,128]{2,1,0:T(8,128)(2,1)S(1)}, bf16[2,192,128]{2,1,0:T(8,128)(2,1)S(1)}, u32[]{:S(2)}, u32[]{:S(2)}) collective-permute-start(bf16[2,192,128]{2,1,0:T(8,128)(2,1)S(1)} %get-tuple-element.58), channel_id=1, source_target_pairs={{0,5},{1,4},{2,7},{3,6},{4,1},{5,0},{6,3},{7,2},{8,13},{9,12},{10,... | collective-permute-start | bytes 294920 | tf_op jit(solution)/shard_map/ppermute | solution.py:247
  65.8 12.5 %collective-permute-start.18 = (bf16[2,192,128]{2,1,0:T(8,128)(2,1)S(1)}, bf16[2,192,128]{2,1,0:T(8,128)(2,1)S(1)}, u32[]{:S(2)}, u32[]{:S(2)}) collective-permute-start(bf16[2,192,128]{2,1,0:T(8,128)(2,1)S(1)} %get-tuple-element.56), channel_id=1, source_target_pairs={{0,4},{1,5},{2,6},{3,7},{4,0},{5,1},{6,2},{7,3},{8,12},{9,13},{10,... | collective-permute-start | bytes 294920 | tf_op jit(solution)/shard_map/ppermute | solution.py:247

commit v4 on v3

--- a/solution.py
+++ b/solution.py
@@ -121,15 +121,17 @@
     return terms[0] + signs[0] * terms[1]
 
 
-def cancel_kernel(shape, place, index, *refs):
+def cancel_kernel(shape, turn, place, index, *refs):
     blocks, rows, inner, tile = shape
     fields, refs = refs[:blocks], refs[blocks:]
     first, second, scale, coefs = refs[:4]
-    out, s_one, s_two, r_one, r_two = refs[-9:-4]
+    out, s_one, s_two, r_one, r_two, ready, sent = refs[-11:-4]
     spare = itertools.cycle(refs[-4:])
     margin = (rows - inner) // 2
     width = first.shape[1] // 2
     chunk = 16
+    mine = place[place.shape[0] - 1]
+    skip = pl.multiple_of(mine * tile, chunk)
     dot = functools.partial(jnp.dot, preferred_element_type=jnp.float32)
 
     def tiles(value):
@@ -138,7 +140,7 @@
     def gaps_at(block, start, rest=None, row=0, height=0):
         parts = []
         for part in range(2):
-            value = fields[block][part, pl.ds(start, chunk), :].astype(jnp.float32)
+            value = fields[block][part, pl.ds(skip + start, chunk), :].astype(jnp.float32)
             if rest is not None:
                 value = value - rest[block, pl.ds(part * height + row, chunk), :]
             parts.append(tiles(value))
@@ -151,15 +153,17 @@
             value = expand(signs, coefs, 16 * part).reshape(chunk, LANES)
             out_ref[block, pl.ds(part * width + row, chunk), :] = value.astype(jnp.bfloat16)
 
-    def over(height, body):
+    def over(height, body, wanted=tuple(range(blocks))):
+        parts = math.gcd(height // chunk, 4 // len(wanted))
+
         def step(i, carry):
-            for part in range(2):
-                row = pl.multiple_of((2 * i + part) * chunk, chunk)
-                for block in range(blocks):
+            for part in range(parts):
+                row = pl.multiple_of((parts * i + part) * chunk, chunk)
+                for block in wanted:
                     body(block, row)
             return carry
 
-        lax.fori_loop(0, height // (2 * chunk), step, 0)
+        lax.fori_loop(0, height // (parts * chunk), step, 0)
 
     for ref, used_rows in ((s_one, rows), (s_two, inner)):
         if used_rows < width:
@@ -175,12 +179,15 @@
         soften(block, s_two, row, gaps_at(block, row + margin, r_one, row, inner))
 
     def metrics(block, row):
-        core = place[1] if block == 0 else 1 - place[1]
-        lanes = pl.ds(pl.multiple_of(core * LANES, LANES), LANES)
         gaps = gaps_at(block, row + 2 * margin, r_two, row, tile)
         for bit in range(4):
             value = (gaps[bit] * 2.0).reshape(chunk, LANES)
-            out[bit, pl.ds(row, chunk), lanes] = value.astype(jnp.bfloat16)
+            ready[block, bit, pl.ds(row, chunk), :] = value.astype(jnp.bfloat16)
+
+    def send(block):
+        lane = pl.multiple_of(place[blocks * turn + block] * LANES, LANES)
+        target = out.at[:, :, pl.ds(lane, LANES)]
+        return pltpu.make_async_copy(ready.at[block], target, sent.at[block])
 
     def product(matrix, ref, into):
         both = jnp.concatenate([ref[block] for block in range(blocks)], axis=1)
@@ -192,31 +199,34 @@
     product(first, s_one, r_one)
     over(inner, second_round)
     product(second, s_two, r_two)
-    over(tile, metrics)
-
-
-def cancel(place, index, fields, first, second, scale, coefs, elements, before):
-    _, rows, samples = fields[0].shape
-    inner, tile = first.shape[0] // 2, second.shape[0] // 2
+    for block in range(blocks):
+        over(tile, metrics, (block,))
+        send(block).start()
+    for block in range(blocks):
+        send(block).wait()
+
+
+def cancel(turn, place, index, fields, first, second, scale, coefs, elements, before):
+    samples = fields[0].shape[2]
+    rows, inner, tile = scale.shape[1], first.shape[0] // 2, second.shape[0] // 2
     blocks = len(fields)
     vmem, smem = (pl.BlockSpec(memory_space=m) for m in (pltpu.VMEM, pltpu.SMEM))
+    anywhere = pl.BlockSpec(memory_space=pl.ANY)
     given = [] if before is None else [before]
     wide = blocks * samples
     return pl.pallas_call(
-        functools.partial(cancel_kernel, (blocks, rows, inner, tile)),
-        grid_spec=pltpu.PrefetchScalarGridSpec(
-            num_scalar_prefetch=1,
-            grid=(1,),
-            in_specs=[smem] + [vmem] * (blocks + 4) + [pl.BlockSpec(memory_space=pl.ANY)] * len(given),
-            out_specs=pl.BlockSpec((4, tile, wide), lambda s, place: (0, 0, place[0])),
-            scratch_shapes=[
-                pltpu.VMEM((blocks, first.shape[1], samples), jnp.bfloat16),
-                pltpu.VMEM((blocks, second.shape[1], samples), jnp.bfloat16),
-                pltpu.VMEM((blocks, 2 * inner, samples), jnp.float32),
-                pltpu.VMEM((blocks, 2 * tile, samples), jnp.float32),
-            ]
-            + [pltpu.VMEM((8, 2, 8, LANES), jnp.float32)] * 4,
-        ),
+        functools.partial(cancel_kernel, (blocks, rows, inner, tile), turn),
+        in_specs=[smem] * 2 + [vmem] * (blocks + 4) + [anywhere] * len(given),
+        out_specs=anywhere,
+        scratch_shapes=[
+            pltpu.VMEM((blocks, first.shape[1], samples), jnp.bfloat16),
+            pltpu.VMEM((blocks, second.shape[1], samples), jnp.bfloat16),
+            pltpu.VMEM((blocks, 2 * inner, samples), jnp.float32),
+            pltpu.VMEM((blocks, 2 * tile, samples), jnp.float32),
+            pltpu.VMEM((blocks, 4, tile, samples), jnp.bfloat16),
+            pltpu.SemaphoreType.DMA((blocks,)),
+        ]
+        + [pltpu.VMEM((8, 2, 8, LANES), jnp.float32)] * 4,
         out_shape=jax.ShapeDtypeStruct((4, tile, elements), jnp.bfloat16),
         input_output_aliases={6 + blocks: 0} if given else {},
         compiler_params=pltpu.CompilerParams(vmem_limit_bytes=12 * MEBI),
@@ -242,8 +252,8 @@
         pairs = [(i, i ^ mask) for i in range(self.tm * self.beam)]
         return lax.ppermute(value, ("tm", "beam"), pairs)
 
-    def shift(self, value, z, core):
-        pairs = [(i, ((i + 2 * z) % self.beam) ^ core) for i in range(self.beam)]
+    def shift(self, value, z):
+        pairs = [(i, (i + 2 * z) % self.beam) for i in range(self.beam)]
         return lax.ppermute(value, "beam", pairs)
 
 
@@ -358,16 +368,15 @@
     tile = count // places.beam
     rows = tile + 2 * HALO
     slots = neighbours.shape[1]
-    padded = jnp.pad(beam_order, (HALO, HALO), constant_values=-1)
-    windows = jnp.stack([padded[d * tile : d * tile + rows] for d in range(places.beam)])
-    own = lax.dynamic_slice_in_dim(padded, lax.axis_index("beam") * tile, rows)
     width = -(-rows // LANES) * LANES
-    sides = jnp.stack(
-        [
-            jnp.pad(own, (0, width - rows), constant_values=-1),
-            jnp.pad(own[COLS:-COLS], (0, width - rows + 2 * COLS), constant_values=-1),
-        ]
-    ).astype(jnp.float32)
+    padded = jnp.pad(beam_order, (HALO, width + COLS), constant_values=-1)
+    group = 2 if places.square else 1
+    reach = group * tile
+    span = reach + 2 * HALO
+    windows = [padded[i : i + count : 1] for i in range(0, span, reach)]
+    windows = jnp.concatenate([v.reshape(-1, reach) for v in windows], axis=1)[:, :span]
+    own = lax.dynamic_slice_in_dim(padded, lax.axis_index("beam") * tile, width + COLS)
+    sides = jnp.stack([own[:width], own[COLS:]]).astype(jnp.float32)
     table = jnp.concatenate(
         [
             neighbours.astype(jnp.float32),
@@ -377,13 +386,13 @@
         ],
         axis=1,
     )
-    taken = jnp.take(table, own, axis=0, mode="clip")
+    taken = jnp.take(table, own[:rows], axis=0, mode="clip")
     held = rows_held(places, beam_weights.shape[1])
     me = lax.axis_index("beam")
+    chips = places.beam // 2
+    moves = (0, 1, 3, 2)
     if places.square:
-        moves = [(0, 0), (0, 1), (1, 0), (1, 1), (3, 0), (3, 1), (2, 0), (2, 1)]
-        z, core = (np.array(v, np.int32) for v in zip(*moves))
-        windows = windows[((me + 2 * z) % places.beam) ^ core]
+        windows = windows[(me // 2 + np.array(moves, np.int32)) % chips]
     select = (windows[:, :, None] == held[None, None, :]).astype(jnp.bfloat16)
     mine, other = all_beams(places, element_signals, beam_weights, (select, taken, sides))
     beams = [mine]
@@ -393,25 +402,37 @@
     index, coefs, first, second, scale = tables(bit_labels, taken, sides, slots, tile)
     select = after(select, first, second, scale, coefs)
     ordered = list(order_beams(select, beams))
-    chips = places.beam // 2
     elements = element_signals.shape[2] * places.beam
-    out = None
     if places.square:
-        fields = ordered[:1] + [
-            places.shift(value, *move) for value, move in zip(ordered[1:6], moves[1:6])
-        ]
-        spots = [((me // 2 - z) % chips, me % 2) for z, _ in moves[::2]]
+        here, *away = ordered
+        one, three = places.shift(away[0], 1), places.shift(away[1], 3)
+        pairs = [[here, places.swap(here, core=1)]]
+        shifts = np.array([0, 0, 1, 3, 1, 3, 2, 2], np.int32)
+        flips = np.array([0, 1, 0, 0, 1, 1, 0, 1], np.int32)
+        place = (me - 2 * shifts) % places.beam ^ flips
+        place = jnp.concatenate([place, (me % 2)[None]])
     else:
         fields = list(
             lax.all_to_all(jnp.stack(ordered), "beam", split_axis=0, concat_axis=0, tiled=True)
         )
-        spots = [(chip, 0) for chip in range(chips)]
-    for i, spot in enumerate(spots):
-        place = jnp.stack([jnp.asarray(v, jnp.int32) for v in spot])
-        pair = fields[2 * i : 2 * i + 2]
-        out = cancel(place, index, pair, first, second, scale, coefs, elements, out)
-        if places.square and i == 0:
-            fields += [places.shift(after(ordered[j], out), *moves[j]) for j in (6, 7)]
+        pairs = [fields[2 * i : 2 * i + 2] for i in range(chips)]
+        place = jnp.arange(places.beam + 1, dtype=jnp.int32) % places.beam
+
+    def run(turn, pair, before):
+        return cancel(turn, place, index, pair, first, second, scale, coefs, elements, before)
+
+    out = run(0, pairs[0], None)
+    if places.square:
+        two = places.shift(after(away[2], out), 2)
+        one, three = after(one, out), after(three, out)
+        far_one, far_three = places.swap(one, core=1), places.swap(three, core=1)
+        out = run(1, [one, three], out)
+        two = after(two, out)
+        far_two = places.swap(two, core=1)
+        out = run(2, [far_one, far_three], out)
+        return run(3, [two, far_two], out)
+    for i in range(1, chips):
+        out = run(i, pairs[i], out)
     return out
 
 

time: 83.8 us -> 80.1 us (0.956)
  Pallas kernels: 29.4 us -> 23.4 us
  waiting for transfers between devices: 25.2 us -> 30.9 us
  starting transfers between devices: 21.2 us -> 17.5 us
    ppermute x7 -> x3, waiting for transfers between devices: 0.02 us -> 4.83 us  [shift(): return lax.ppermute(value, 'beam', pairs)]
    ppermute x7 -> x3, starting transfers between devices: 8.39 us -> 4.47 us  [shift(): return lax.ppermute(value, 'beam', pairs)]
    pallas_call x2, Pallas kernels: 5.42 us -> 2.49 us  [form_beams(): pl.pallas_call(functools.partial(beams_kernel, pieces), in_specs=[whole]...]
    pallas_call x4, Pallas kernels: 20 us -> 18.1 us  [cancel(): pl.pallas_call(functools.partial(cancel_kernel, (blocks, rows, inner, til...]
    pallas_call x1, Pallas kernels: 1.93 us -> 0.85 us  [order_beams(): pl.pallas_call(functools.partial(order_kernel, len(beams)), in_specs=[who...]
    ppermute x17 -> x21, waiting for transfers between devices: 25.2 us -> 26.1 us  [swap(): return lax.ppermute(value, ('tm', 'beam'), pairs)]
    ppermute x17 -> x21, starting transfers between devices: 12.8 us -> 13.1 us  [swap(): return lax.ppermute(value, ('tm', 'beam'), pairs)]
  transfers between devices with their start and end apart: 24 -> 24, of which waited for: 10 -> 12; matrix products, arithmetic and copies ran while one was open for 9% -> 10% of each run, Pallas kernels for 23% -> 21%
where the time goes in v4:
time: 80.1 us; the launch traced here: 79.7 us
  waiting for transfers between devices  30.9 us (39%)
  Pallas kernels  23.4 us (29%)
  starting transfers between devices  17.5 us (22%)
  local copies, waits for them, and re-layouts  4.12 us (5%)
  other arithmetic  3.5 us (4%)
    ppermute x21, waiting for transfers between devices, swap(): return lax.ppermute(value, ('tm', 'beam'), pairs)  26.1 us
    pallas_call x4, Pallas kernels, cancel(): pl.pallas_call(functools.partial(cancel_kernel, (blocks, rows, inner, til...  18.1 us
    ppermute x21, starting transfers between devices, swap(): return lax.ppermute(value, ('tm', 'beam'), pairs)  13.1 us
    ppermute x3, waiting for transfers between devices, shift(): return lax.ppermute(value, 'beam', pairs)  4.83 us
    ppermute x3, starting transfers between devices, shift(): return lax.ppermute(value, 'beam', pairs)  4.47 us
    pallas_call x2, Pallas kernels, form_beams(): pl.pallas_call(functools.partial(beams_kernel, pieces), in_specs=[whole]...  2.49 us
    pallas_call x1, Pallas kernels, tables(): pl.pallas_call(functools.partial(tables_kernel, (slots, rows, inner, tile...  2 us
  transfers between devices with their start and end apart: 24, of which 12 were waited for; matrix products, arithmetic and copies ran while one was open for 10% of the time, Pallas kernels for 21%

profile of v4, /device:TPU:0, one launch (start us, length us, event | category | flops | bytes accessed | tf_op | source)
XLA Modules:
  0.0 79.7 jit_solution(15244856556447210507)
XLA Ops:
  0.0 3.0 %collective-permute-start.4 = (bf16[2,32,2048]{2,1,0:T(8,128)(2,1)}, bf16[2,32,2048]{2,1,0:T(8,128)(2,1)S(1)}, u32[]{:S(2)}, u32[]{:S(2)}) collective-permute-start(bf16[2,32,2048]{2,1,0:T(8,128)(2,1)} %refs_0_.3), channel_id=1, source_target_pairs={{0,16},{1,17},{2,18},{3,19},{4,20},{5,21},{6,22},{7,23},{8,24},{9,... | collective-permute-start | bytes 786440 | tf_op jit(solution)/shard_map/ppermute | solution.py:253
  3.0 1.5 %collective-permute-start.2 = (bf16[2,32,2048]{2,1,0:T(8,128)(2,1)}, bf16[2,32,2048]{2,1,0:T(8,128)(2,1)S(1)}, u32[]{:S(2)}, u32[]{:S(2)}) collective-permute-start(bf16[2,32,2048]{2,1,0:T(8,128)(2,1)} %refs_0_.3), channel_id=1, source_target_pairs={{0,8},{1,9},{2,10},{3,11},{4,12},{5,13},{6,14},{7,15},{8,0},{9,1},... | collective-permute-start | bytes 786440 | tf_op jit(solution)/shard_map/ppermute | solution.py:253
  4.5 2.6 %collective-permute-start = (bf16[2,32,2048]{2,1,0:T(8,128)(2,1)}, bf16[2,32,2048]{2,1,0:T(8,128)(2,1)S(1)}, u32[]{:S(2)}, u32[]{:S(2)}) collective-permute-start(bf16[2,32,2048]{2,1,0:T(8,128)(2,1)} %refs_0_.3), channel_id=1, source_target_pairs={{0,4},{1,5},{2,6},{3,7},{4,0},{5,1},{6,2},{7,3},{8,12},{9,13},{10,... | collective-permute-start | bytes 786440 | tf_op jit(solution)/shard_map/ppermute | solution.py:253
  7.1 0.8 pad_dynamic-slice_fusion
  7.9 0.8 %pad_slice_fusion.1 = (s32[1024]{0:T(1024)S(1)}, s32[1024]{0:T(1024)S(1)}) fusion(s32[1024]{0:T(1024)} %param.13), kind=kLoop, calls=%fused_computation.10 | loop fusion | bytes 12288 | tf_op jit(solution)/shard_map/slice | solution.py:376
  8.7 0.7 compare_select_fusion
  9.4 0.7 xor_multiply_fusion
  10.2 0.8 convert_element_type.21
  11.0 0.9 %fusion.5 = (bf16[1,1024,6]{1,0,2:T(2,128)(2,1)S(1)}, bf16[1,1024,6]{1,0,2:T(2,128)(2,1)S(1)}) fusion(bf16[2,1024,6]{1,0,2:T(2,128)(2,1)} %param.15), kind=kLoop, calls=%fused_computation.28 | loop fusion | bytes 49152 | tf_op jit(solution)/shard_map/slice | solution.py:383
  11.9 0.7 pad_maximum_fusion
  12.8 0.6 gather_fusion.1
  13.4 0.7 gather_fusion
  14.6 0.6 collective-permute-start.5
  15.2 1.6 %collective-permute-start.15 = (bf16[2,2048,128]{2,1,0:T(8,128)(2,1)S(1)}, bf16[2,2048,128]{2,1,0:T(8,128)(2,1)S(1)}, u32[]{:S(2)}, u32[]{:S(2)}) collective-permute-start(bf16[2,2048,128]{2,1,0:T(8,128)(2,1)S(1)} %copy-done), channel_id=1, source_target_pairs={{0,2},{1,3},{2,0},{3,1},{4,6},{5,7},{6,4},{7,5},{8,10},{9,11},{10,... | collective-permute-start | bytes 3145736 | tf_op jit(solution)/shard_map/ppermute | solution.py:253
  16.8 2.0 %collective-permute-done.refs_8_ = bf16[2,32,2048]{2,1,0:T(8,128)(2,1)S(1)} collective-permute-done((bf16[2,32,2048]{2,1,0:T(8,128)(2,1)}, bf16[2,32,2048]{2,1,0:T(8,128)(2,1)S(1)}, u32[]{:S(2)}, u32[]{:S(2)}) %collective-permute-start) | collective-permute-done | bytes 262176 | tf_op jit(solution)/shard_map/ppermute | solution.py:253
  19.8 3.7 %collective-permute-done.5.refs_6_ = bf16[2,32,2048]{2,1,0:T(8,128)(2,1)S(1)} collective-permute-done((bf16[2,32,2048]{2,1,0:T(8,128)(2,1)S(1)}, bf16[2,32,2048]{2,1,0:T(8,128)(2,1)S(1)}, u32[]{:S(2)}, u32[]{:S(2)}) %collective-permute-start.5) | collective-permute-done | bytes 262176 | tf_op jit(solution)/shard_map/ppermute | solution.py:253
  23.5 4.0 %collective-permute-done.11.refs_12_ = bf16[2,32,2048]{2,1,0:T(8,128)(2,1)S(1)} collective-permute-done((bf16[2,32,2048]{2,1,0:T(8,128)(2,1)S(1)}, bf16[2,32,2048]{2,1,0:T(8,128)(2,1)S(1)}, u32[]{:S(2)}, u32[]{:S(2)}) %collective-permute-start.11) | collective-permute-done | bytes 262176 | tf_op jit(solution)/shard_map/ppermute | solution.py:253
  28.6 5.6 %collective-permute-done.13.refs_14_ = bf16[2,32,2048]{2,1,0:T(8,128)(2,1)S(1)} collective-permute-done((bf16[2,32,2048]{2,1,0:T(8,128)(2,1)S(1)}, bf16[2,32,2048]{2,1,0:T(8,128)(2,1)S(1)}, u32[]{:S(2)}, u32[]{:S(2)}) %collective-permute-start.13) | collective-permute-done | bytes 262176 | tf_op jit(solution)/shard_map/ppermute | solution.py:253
  36.9 1.2 %form_beams.2.refs_1_ = bf16[2,512,128]{2,1,0:T(8,128)(2,1)S(1)} custom-call(bf16[2,32,2048]{2,1,0:T(8,128)(2,1)S(1)} %copy-done.1, bf16[2,32,2048]{2,1,0:T(8,128)(2,1)S(1)} %collective-permute-done.1.refs_1_, bf16[2,32,2048]{2,1,0:T(8,128)(2,1)S(1)} %collective-permute-done.2.refs_2_, bf16[2,32,2048]{2,1,0:T(8,128)(2,1)S(1)} %collective-permute-done.3.refs_3_, ...), custom_call_target="tpu_custom_call" | custom-call | flops 1073741824 | bytes 5242880 | tf_op jit(solution)/shard_map/form_beams/pallas_call | solution.py:46
  38.2 3.0 %collective-permute-done.15.refs_16_ = bf16[2,2048,128]{2,1,0:T(8,128)(2,1)S(1)} collective-permute-done((bf16[2,2048,128]{2,1,0:T(8,128)(2,1)S(1)}, bf16[2,2048,128]{2,1,0:T(8,128)(2,1)S(1)}, u32[]{:S(2)}, u32[]{:S(2)}) %collective-permute-start.15) | collective-permute-done | bytes 1048608 | tf_op jit(solution)/shard_map/ppermute | solution.py:253
  41.2 1.2 %form_beams.3 = bf16[2,512,128]{2,1,0:T(8,128)(2,1)S(1)} custom-call(bf16[2,32,2048]{2,1,0:T(8,128)(2,1)S(1)} %copy-done.1, bf16[2,32,2048]{2,1,0:T(8,128)(2,1)S(1)} %collective-permute-done.1.refs_1_, bf16[2,32,2048]{2,1,0:T(8,128)(2,1)S(1)} %collective-permute-done.2.refs_2_, bf16[2,32,2048]{2,1,0:T(8,128)(2,1)S(1)} %collective-permute-done.3.refs_3_, ...), custom_call_target="tpu_custom_call" | custom-call | flops 1073741824 | bytes 5242880 | tf_op jit(solution)/shard_map/form_beams/pallas_call | solution.py:46
  42.5 2.0 %tables.1 = (s32[32]{0:T(128)S(1)}, f32[32,8,128]{2,1,0:T(8,128)S(1)}, bf16[320,512]{1,0:T(8,128)(2,1)S(1)}, bf16[256,512]{1,0:T(8,128)(2,1)S(1)}, f32[2,192,128]{2,1,0:T(8,128)S(1)}) custom-call(s32[16]{0:T(128)S(1)} %copy-done.2, f32[192,19]{1,0:T(8,128)S(1)} %gather_fusion, f32[2,256]{1,0:T(2,128)S(1)} %add_convert_fusion.own), custom_call_target="tpu_custom_call" | custom-call | flops 2949120 | bytes 786432 | tf_op jit(solution)/shard_map/tables/pallas_call | solution.py:347
  44.5 6.2 %collective-permute-done.16.refs_2_ = bf16[2,512,128]{2,1,0:T(8,128)(2,1)S(1)} collective-permute-done((bf16[2,512,128]{2,1,0:T(8,128)(2,1)S(1)}, bf16[2,512,128]{2,1,0:T(8,128)(2,1)S(1)}, u32[]{:S(2)}, u32[]{:S(2)}) %collective-permute-start.16) | collective-permute-done | bytes 262176 | tf_op jit(solution)/shard_map/ppermute | solution.py:253
  50.7 0.8 %order_beams.1 = (bf16[2,320,128]{2,1,0:T(8,128)(2,1)S(1)}, bf16[2,320,128]{2,1,0:T(8,128)(2,1)S(1)}, bf16[2,320,128]{2,1,0:T(8,128)(2,1)S(1)}, bf16[2,320,128]{2,1,0:T(8,128)(2,1)S(1)}) custom-call(bf16[4,320,1024]{2,1,0:T(8,128)(2,1)S(1)} %compare_convert_fusion.refs_0_, bf16[2,512,128]{2,1,0:T(8,128)(2,1)S(1)} %form_beams.2.refs_1_, ...), custom_call_target="tpu_custom_call" | custom-call | flops 671088640 | bytes 3276800 | tf_op jit(solution)/shard_map/order_beams/pallas_call | solution.py:78
  51.7 3.6 %collective-permute-start.20 = (bf16[2,320,128]{2,1,0:T(8,128)(2,1)S(1)}, bf16[2,320,128]{2,1,0:T(8,128)(2,1)S(1)}, u32[]{:S(2)}, u32[]{:S(2)}) collective-permute-start(bf16[2,320,128]{2,1,0:T(8,128)(2,1)S(1)} %get-tuple-element.56), channel_id=1, source_target_pairs={{0,6},{1,7},{2,0},{3,1},{4,2},{5,3},{6,4},{7,5},{8,14},{9,15},{10,... | collective-permute-start | bytes 491528 | tf_op jit(solution)/shard_map/ppermute | solution.py:257
  55.3 4.5 %cancel.4.refs_6_ = bf16[4,128,1024]{2,1,0:T(8,128)(2,1)} custom-call(s32[9]{0:T(128)S(1)} %pad_add_fusion.1.place, s32[32]{0:T(128)S(1)} %get-tuple-element.45.index, bf16[2,320,128]{2,1,0:T(8,128)(2,1)S(1)} %get-tuple-element.52.refs_0_, bf16[2,320,128]{2,1,0:T(8,128)(2,1)S(1)} %collective-permute-done.17.refs_1_, ...), custom_call_target="tpu_custom_call" | custom-call | flops 78888960 | bytes 458752 | tf_op jit(solution)/shard_map/cancel/pallas_call | solution.py:217
  59.9 0.9 %collective-permute-start.18 = (bf16[2,320,128]{2,1,0:T(8,128)(2,1)S(1)}, bf16[2,320,128]{2,1,0:T(8,128)(2,1)S(1)}, u32[]{:S(2)}, u32[]{:S(2)}) collective-permute-start(bf16[2,320,128]{2,1,0:T(8,128)(2,1)S(1)} %get-tuple-element.53), channel_id=1, source_target_pairs={{0,4},{1,5},{2,6},{3,7},{4,0},{5,1},{6,2},{7,3},{8,12},{9,13},{10,... | collective-permute-start | bytes 491528 | tf_op jit(solution)/shard_map/ppermute | solution.py:257
  60.8 2.8 %collective-permute-done.19.refs_0_ = bf16[2,320,128]{2,1,0:T(8,128)(2,1)S(1)} collective-permute-done((bf16[2,320,128]{2,1,0:T(8,128)(2,1)S(1)}, bf16[2,320,128]{2,1,0:T(8,128)(2,1)S(1)}, u32[]{:S(2)}, u32[]{:S(2)}) %collective-permute-start.19) | collective-permute-done | bytes 163872 | tf_op jit(solution)/shard_map/ppermute | solution.py:257
  64.1 4.5 %cancel.5.refs_6_ = bf16[4,128,1024]{2,1,0:T(8,128)(2,1)} custom-call(s32[9]{0:T(128)S(1)} %pad_add_fusion.1.place, s32[32]{0:T(128)S(1)} %get-tuple-element.45.index, bf16[2,320,128]{2,1,0:T(8,128)(2,1)S(1)} %collective-permute-done.19.refs_0_, bf16[2,320,128]{2,1,0:T(8,128)(2,1)S(1)} %collective-permute-done.20.refs_1_, ...), custom_call_target="tpu_custom_call", output_to_operand_aliasing={{}: (8, {})} | custom-call | flops 78888960 | bytes 458752 | tf_op jit(solution)/shard_map/cancel/pallas_call | solution.py:217
  68.6 2.0 %collective-permute-done.18.refs_0_ = bf16[2,320,128]{2,1,0:T(8,128)(2,1)S(1)} collective-permute-done((bf16[2,320,128]{2,1,0:T(8,128)(2,1)S(1)}, bf16[2,320,128]{2,1,0:T(8,128)(2,1)S(1)}, u32[]{:S(2)}, u32[]{:S(2)}) %collective-permute-start.18) | collective-permute-done | bytes 163872 | tf_op jit(solution)/shard_map/ppermute | solution.py:257
  70.6 4.5 %cancel.6.refs_6_ = bf16[4,128,1024]{2,1,0:T(8,128)(2,1)} custom-call(s32[9]{0:T(128)S(1)} %pad_add_fusion.1.place, s32[32]{0:T(128)S(1)} %get-tuple-element.45.index, bf16[2,320,128]{2,1,0:T(8,128)(2,1)S(1)} %collective-permute-done.22.refs_0_, bf16[2,320,128]{2,1,0:T(8,128)(2,1)S(1)} %collective-permute-done.23.refs_1_, ...), custom_call_target="tpu_custom_call", output_to_operand_aliasing={{}: (8, {})} | custom-call | flops 78888960 | bytes 458752 | tf_op jit(solution)/shard_map/cancel/pallas_call | solution.py:217
  75.2 4.5 %cancel.7 = bf16[4,128,1024]{2,1,0:T(8,128)(2,1)} custom-call(s32[9]{0:T(128)S(1)} %pad_add_fusion.1.place, s32[32]{0:T(128)S(1)} %get-tuple-element.45.index, bf16[2,320,128]{2,1,0:T(8,128)(2,1)S(1)} %collective-permute-done.18.refs_0_, bf16[2,320,128]{2,1,0:T(8,128)(2,1)S(1)} %collective-permute-done.21.refs_1_, ...), custom_call_target="tpu_custom_call", output_to_operand_aliasing={{}: (8, {})} | custom-call | flops 78888960 | bytes 458752 | tf_op jit(solution)/shard_map/cancel/pallas_call | solution.py:217
  (58 shorter events, 6.6 us)
Async XLA Ops:
  0.0 28.1 %copy-start.1 = (bf16[2,32,2048]{2,1,0:T(8,128)(2,1)S(1)}, bf16[2,32,2048]{2,1,0:T(8,128)(2,1)}, u32[]{:S(2)}) copy-start(bf16[2,32,2048]{2,1,0:T(8,128)(2,1)} %refs_0_.3) | copy-start | bytes 786436
  0.0 15.2 %copy-start = (bf16[2,2048,128]{2,1,0:T(8,128)(2,1)S(1)}, bf16[2,2048,128]{2,1,0:T(8,128)(2,1)}, u32[]{:S(2)}) copy-start(bf16[2,2048,128]{2,1,0:T(8,128)(2,1)} %refs_16_.1) | copy-start | bytes 3145732
  0.0 14.6 %collective-permute-start.4 = (bf16[2,32,2048]{2,1,0:T(8,128)(2,1)}, bf16[2,32,2048]{2,1,0:T(8,128)(2,1)S(1)}, u32[]{:S(2)}, u32[]{:S(2)}) collective-permute-start(bf16[2,32,2048]{2,1,0:T(8,128)(2,1)} %refs_0_.3), channel_id=1, source_target_pairs={{0,16},{1,17},{2,18},{3,19},{4,20},{5,21},{6,22},{7,23},{8,24},{9,... | collective-permute-start | bytes 786440 | tf_op jit(solution)/shard_map/ppermute | solution.py:253
  3.0 11.6 %collective-permute-start.2 = (bf16[2,32,2048]{2,1,0:T(8,128)(2,1)}, bf16[2,32,2048]{2,1,0:T(8,128)(2,1)S(1)}, u32[]{:S(2)}, u32[]{:S(2)}) collective-permute-start(bf16[2,32,2048]{2,1,0:T(8,128)(2,1)} %refs_0_.3), channel_id=1, source_target_pairs={{0,8},{1,9},{2,10},{3,11},{4,12},{5,13},{6,14},{7,15},{8,0},{9,1},... | collective-permute-start | bytes 786440 | tf_op jit(solution)/shard_map/ppermute | solution.py:253
  4.5 14.3 %collective-permute-start = (bf16[2,32,2048]{2,1,0:T(8,128)(2,1)}, bf16[2,32,2048]{2,1,0:T(8,128)(2,1)S(1)}, u32[]{:S(2)}, u32[]{:S(2)}) collective-permute-start(bf16[2,32,2048]{2,1,0:T(8,128)(2,1)} %refs_0_.3), channel_id=1, source_target_pairs={{0,4},{1,5},{2,6},{3,7},{4,0},{5,1},{6,2},{7,3},{8,12},{9,13},{10,... | collective-permute-start | bytes 786440 | tf_op jit(solution)/shard_map/ppermute | solution.py:253
  14.6 8.9 %collective-permute-start.5 = (bf16[2,32,2048]{2,1,0:T(8,128)(2,1)S(1)}, bf16[2,32,2048]{2,1,0:T(8,128)(2,1)S(1)}, u32[]{:S(2)}, u32[]{:S(2)}) collective-permute-start(bf16[2,32,2048]{2,1,0:T(8,128)(2,1)S(1)} %collective-permute-done.2.refs_2_), channel_id=1, source_target_pairs={{0,16},{1,17},{2,18},{3,19},{4,20},{5,21},{6,22},{7,23},{8,24},{9,... | collective-permute-start | bytes 786440 | tf_op jit(solution)/shard_map/ppermute | solution.py:253
  15.2 26.0 %collective-permute-start.15 = (bf16[2,2048,128]{2,1,0:T(8,128)(2,1)S(1)}, bf16[2,2048,128]{2,1,0:T(8,128)(2,1)S(1)}, u32[]{:S(2)}, u32[]{:S(2)}) collective-permute-start(bf16[2,2048,128]{2,1,0:T(8,128)(2,1)S(1)} %copy-done), channel_id=1, source_target_pairs={{0,2},{1,3},{2,0},{3,1},{4,6},{5,7},{6,4},{7,5},{8,10},{9,11},{10,... | collective-permute-start | bytes 3145736 | tf_op jit(solution)/shard_map/ppermute | solution.py:253
  18.8 8.7 %collective-permute-start.11 = (bf16[2,32,2048]{2,1,0:T(8,128)(2,1)S(1)}, bf16[2,32,2048]{2,1,0:T(8,128)(2,1)S(1)}, u32[]{:S(2)}, u32[]{:S(2)}) collective-permute-start(bf16[2,32,2048]{2,1,0:T(8,128)(2,1)S(1)} %collective-permute-done.refs_8_), channel_id=1, source_target_pairs={{0,16},{1,17},{2,18},{3,19},{4,20},{5,21},{6,22},{7,23},{8,24},{9,... | collective-permute-start | bytes 786440 | tf_op jit(solution)/shard_map/ppermute | solution.py:253
  19.3 8.2 %collective-permute-start.9 = (bf16[2,32,2048]{2,1,0:T(8,128)(2,1)S(1)}, bf16[2,32,2048]{2,1,0:T(8,128)(2,1)S(1)}, u32[]{:S(2)}, u32[]{:S(2)}) collective-permute-start(bf16[2,32,2048]{2,1,0:T(8,128)(2,1)S(1)} %collective-permute-done.refs_8_), channel_id=1, source_target_pairs={{0,8},{1,9},{2,10},{3,11},{4,12},{5,13},{6,14},{7,15},{8,0},{9,1},... | collective-permute-start | bytes 786440 | tf_op jit(solution)/shard_map/ppermute | solution.py:253
  23.5 4.6 %collective-permute-start.7 = (bf16[2,32,2048]{2,1,0:T(8,128)(2,1)S(1)}, bf16[2,32,2048]{2,1,0:T(8,128)(2,1)S(1)}, u32[]{:S(2)}, u32[]{:S(2)}) collective-permute-start(bf16[2,32,2048]{2,1,0:T(8,128)(2,1)S(1)} %collective-permute-done.refs_8_), channel_id=1, source_target_pairs={{0,1},{1,0},{2,3},{3,2},{4,5},{5,4},{6,7},{7,6},{8,9},{9,8},{10,11... | collective-permute-start | bytes 786440 | tf_op jit(solution)/shard_map/ppermute | solution.py:253
  27.5 6.7 %collective-permute-start.13 = (bf16[2,32,2048]{2,1,0:T(8,128)(2,1)S(1)}, bf16[2,32,2048]{2,1,0:T(8,128)(2,1)S(1)}, u32[]{:S(2)}, u32[]{:S(2)}) collective-permute-start(bf16[2,32,2048]{2,1,0:T(8,128)(2,1)S(1)} %collective-permute-done.11.refs_12_), channel_id=1, source_target_pairs={{0,8},{1,9},{2,10},{3,11},{4,12},{5,13},{6,14},{7,15},{8,0},{9,1},... | collective-permute-start | bytes 786440 | tf_op jit(solution)/shard_map/ppermute | solution.py:253
  28.0 6.2 %collective-permute-start.8 = (bf16[2,32,2048]{2,1,0:T(8,128)(2,1)S(1)}, bf16[2,32,2048]{2,1,0:T(8,128)(2,1)S(1)}, u32[]{:S(2)}, u32[]{:S(2)}) collective-permute-start(bf16[2,32,2048]{2,1,0:T(8,128)(2,1)S(1)} %collective-permute-done.5.refs_6_), channel_id=1, source_target_pairs={{0,1},{1,0},{2,3},{3,2},{4,5},{5,4},{6,7},{7,6},{8,9},{9,8},{10,11... | collective-permute-start | bytes 786440 | tf_op jit(solution)/shard_map/ppermute | solution.py:253
  28.1 6.7 %collective-permute-start.1 = (bf16[2,32,2048]{2,1,0:T(8,128)(2,1)S(1)}, bf16[2,32,2048]{2,1,0:T(8,128)(2,1)S(1)}, u32[]{:S(2)}, u32[]{:S(2)}) collective-permute-start(bf16[2,32,2048]{2,1,0:T(8,128)(2,1)S(1)} %copy-done.1), channel_id=1, source_target_pairs={{0,1},{1,0},{2,3},{3,2},{4,5},{5,4},{6,7},{7,6},{8,9},{9,8},{10,11... | collective-permute-start | bytes 786440 | tf_op jit(solution)/shard_map/ppermute | solution.py:253
  28.6 6.3 %collective-permute-start.3 = (bf16[2,32,2048]{2,1,0:T(8,128)(2,1)S(1)}, bf16[2,32,2048]{2,1,0:T(8,128)(2,1)S(1)}, u32[]{:S(2)}, u32[]{:S(2)}) collective-permute-start(bf16[2,32,2048]{2,1,0:T(8,128)(2,1)S(1)} %collective-permute-done.2.refs_2_), channel_id=1, source_target_pairs={{0,1},{1,0},{2,3},{3,2},{4,5},{5,4},{6,7},{7,6},{8,9},{9,8},{10,11... | collective-permute-start | bytes 786440 | tf_op jit(solution)/shard_map/ppermute | solution.py:253
  34.2 1.5 %collective-permute-start.6 = (bf16[2,32,2048]{2,1,0:T(8,128)(2,1)S(1)}, bf16[2,32,2048]{2,1,0:T(8,128)(2,1)S(1)}, u32[]{:S(2)}, u32[]{:S(2)}) collective-permute-start(bf16[2,32,2048]{2,1,0:T(8,128)(2,1)S(1)} %collective-permute-done.4.refs_4_), channel_id=1, source_target_pairs={{0,1},{1,0},{2,3},{3,2},{4,5},{5,4},{6,7},{7,6},{8,9},{9,8},{10,11... | collective-permute-start | bytes 786440 | tf_op jit(solution)/shard_map/ppermute | solution.py:253
  34.2 1.9 %collective-permute-start.14 = (bf16[2,32,2048]{2,1,0:T(8,128)(2,1)S(1)}, bf16[2,32,2048]{2,1,0:T(8,128)(2,1)S(1)}, u32[]{:S(2)}, u32[]{:S(2)}) collective-permute-start(bf16[2,32,2048]{2,1,0:T(8,128)(2,1)S(1)} %collective-permute-done.13.refs_14_), channel_id=1, source_target_pairs={{0,1},{1,0},{2,3},{3,2},{4,5},{5,4},{6,7},{7,6},{8,9},{9,8},{10,11... | collective-permute-start | bytes 786440 | tf_op jit(solution)/shard_map/ppermute | solution.py:253
  34.8 1.8 %collective-permute-start.12 = (bf16[2,32,2048]{2,1,0:T(8,128)(2,1)S(1)}, bf16[2,32,2048]{2,1,0:T(8,128)(2,1)S(1)}, u32[]{:S(2)}, u32[]{:S(2)}) collective-permute-start(bf16[2,32,2048]{2,1,0:T(8,128)(2,1)S(1)} %collective-permute-done.11.refs_12_), channel_id=1, source_target_pairs={{0,1},{1,0},{2,3},{3,2},{4,5},{5,4},{6,7},{7,6},{8,9},{9,8},{10,11... | collective-permute-start | bytes 786440 | tf_op jit(solution)/shard_map/ppermute | solution.py:253
  34.8 2.1 %collective-permute-start.10 = (bf16[2,32,2048]{2,1,0:T(8,128)(2,1)S(1)}, bf16[2,32,2048]{2,1,0:T(8,128)(2,1)S(1)}, u32[]{:S(2)}, u32[]{:S(2)}) collective-permute-start(bf16[2,32,2048]{2,1,0:T(8,128)(2,1)S(1)} %collective-permute-done.9.refs_10_), channel_id=1, source_target_pairs={{0,1},{1,0},{2,3},{3,2},{4,5},{5,4},{6,7},{7,6},{8,9},{9,8},{10,11... | collective-permute-start | bytes 786440 | tf_op jit(solution)/shard_map/ppermute | solution.py:253
  38.2 4.4 %copy-start.2 = (s32[16]{0:T(128)S(1)}, s32[16]{0:T(128)}, u32[]{:S(2)}) copy-start(s32[16]{0:T(128)} %labels.1) | copy-start | bytes 196
  42.4 9.2 %copy-start.3 = (s32[8]{0:T(128)S(1)}, s32[8]{0:T(128)}, u32[]{:S(2)}) copy-start(s32[8]{0:T(128)} %constant.84) | copy-start | bytes 100
  42.4 9.2 %copy-start.4 = (s32[8]{0:T(128)S(1)}, s32[8]{0:T(128)}, u32[]{:S(2)}) copy-start(s32[8]{0:T(128)} %constant.81.clone) | copy-start | bytes 100
  42.4 8.3 %collective-permute-start.16 = (bf16[2,512,128]{2,1,0:T(8,128)(2,1)S(1)}, bf16[2,512,128]{2,1,0:T(8,128)(2,1)S(1)}, u32[]{:S(2)}, u32[]{:S(2)}) collective-permute-start(bf16[2,512,128]{2,1,0:T(8,128)(2,1)S(1)} %form_beams.3), channel_id=1, source_target_pairs={{0,2},{1,3},{2,0},{3,1},{4,6},{5,7},{6,4},{7,5},{8,10},{9,11},{10,... | collective-permute-start | bytes 786440 | tf_op jit(solution)/shard_map/ppermute | solution.py:253
  51.6 3.8 %collective-permute-start.17 = (bf16[2,320,128]{2,1,0:T(8,128)(2,1)S(1)}, bf16[2,320,128]{2,1,0:T(8,128)(2,1)S(1)}, u32[]{:S(2)}, u32[]{:S(2)}) collective-permute-start(bf16[2,320,128]{2,1,0:T(8,128)(2,1)S(1)} %get-tuple-element.52.refs_0_), channel_id=1, source_target_pairs={{0,1},{1,0},{2,3},{3,2},{4,5},{5,4},{6,7},{7,6},{8,9},{9,8},{10,11... | collective-permute-start | bytes 491528 | tf_op jit(solution)/shard_map/ppermute | solution.py:253
  51.7 9.1 %collective-permute-start.20 = (bf16[2,320,128]{2,1,0:T(8,128)(2,1)S(1)}, bf16[2,320,128]{2,1,0:T(8,128)(2,1)S(1)}, u32[]{:S(2)}, u32[]{:S(2)}) collective-permute-start(bf16[2,320,128]{2,1,0:T(8,128)(2,1)S(1)} %get-tuple-element.56), channel_id=1, source_target_pairs={{0,6},{1,7},{2,0},{3,1},{4,2},{5,3},{6,4},{7,5},{8,14},{9,15},{10,... | collective-permute-start | bytes 491528 | tf_op jit(solution)/shard_map/ppermute | solution.py:257
  55.3 8.3 %collective-permute-start.19 = (bf16[2,320,128]{2,1,0:T(8,128)(2,1)S(1)}, bf16[2,320,128]{2,1,0:T(8,128)(2,1)S(1)}, u32[]{:S(2)}, u32[]{:S(2)}) collective-permute-start(bf16[2,320,128]{2,1,0:T(8,128)(2,1)S(1)} %get-tuple-element.54), channel_id=1, source_target_pairs={{0,2},{1,3},{2,4},{3,5},{4,6},{5,7},{6,0},{7,1},{8,10},{9,11},{10,... | collective-permute-start | bytes 491528 | tf_op jit(solution)/shard_map/ppermute | solution.py:257
  59.9 10.8 %collective-permute-start.18 = (bf16[2,320,128]{2,1,0:T(8,128)(2,1)S(1)}, bf16[2,320,128]{2,1,0:T(8,128)(2,1)S(1)}, u32[]{:S(2)}, u32[]{:S(2)}) collective-permute-start(bf16[2,320,128]{2,1,0:T(8,128)(2,1)S(1)} %get-tuple-element.53), channel_id=1, source_target_pairs={{0,4},{1,5},{2,6},{3,7},{4,0},{5,1},{6,2},{7,3},{8,12},{9,13},{10,... | collective-permute-start | bytes 491528 | tf_op jit(solution)/shard_map/ppermute | solution.py:257
  63.6 7.0 %collective-permute-start.22 = (bf16[2,320,128]{2,1,0:T(8,128)(2,1)S(1)}, bf16[2,320,128]{2,1,0:T(8,128)(2,1)S(1)}, u32[]{:S(2)}, u32[]{:S(2)}) collective-permute-start(bf16[2,320,128]{2,1,0:T(8,128)(2,1)S(1)} %collective-permute-done.19.refs_0_), channel_id=1, source_target_pairs={{0,1},{1,0},{2,3},{3,2},{4,5},{5,4},{6,7},{7,6},{8,9},{9,8},{10,11... | collective-permute-start | bytes 491528 | tf_op jit(solution)/shard_map/ppermute | solution.py:253
  63.6 7.0 %collective-permute-start.23 = (bf16[2,320,128]{2,1,0:T(8,128)(2,1)S(1)}, bf16[2,320,128]{2,1,0:T(8,128)(2,1)S(1)}, u32[]{:S(2)}, u32[]{:S(2)}) collective-permute-start(bf16[2,320,128]{2,1,0:T(8,128)(2,1)S(1)} %collective-permute-done.20.refs_1_), channel_id=1, source_target_pairs={{0,1},{1,0},{2,3},{3,2},{4,5},{5,4},{6,7},{7,6},{8,9},{9,8},{10,11... | collective-permute-start | bytes 491528 | tf_op jit(solution)/shard_map/ppermute | solution.py:253
  70.6 4.5 %collective-permute-start.21 = (bf16[2,320,128]{2,1,0:T(8,128)(2,1)S(1)}, bf16[2,320,128]{2,1,0:T(8,128)(2,1)S(1)}, u32[]{:S(2)}, u32[]{:S(2)}) collective-permute-start(bf16[2,320,128]{2,1,0:T(8,128)(2,1)S(1)} %collective-permute-done.18.refs_0_), channel_id=1, source_target_pairs={{0,1},{1,0},{2,3},{3,2},{4,5},{5,4},{6,7},{7,6},{8,9},{9,8},{10,11... | collective-permute-start | bytes 491528 | tf_op jit(solution)/shard_map/ppermute | solution.py:253

commit v5 on v4

--- a/solution.py
+++ b/solution.py
@@ -252,10 +252,6 @@
         pairs = [(i, i ^ mask) for i in range(self.tm * self.beam)]
         return lax.ppermute(value, ("tm", "beam"), pairs)
 
-    def shift(self, value, z):
-        pairs = [(i, (i + 2 * z) % self.beam) for i in range(self.beam)]
-        return lax.ppermute(value, "beam", pairs)
-
 
 def after(value, *others):
     return lax.optimization_barrier((value, *others))[0]
@@ -280,9 +276,9 @@
         return form_beams([gathered], element_signals), None
     swap, w = places.swap, beam_weights
     w_z, w_x, w_y = swap(w, z=2), swap(w, x=1), swap(w, y=1)
-    far = swap(after(element_signals, *ready), z=1)
+    far = swap(after(element_signals, ready[2]), z=1)
     w_xy = swap(after(w_x, w_y), y=1)
-    w_xz, w_yz = swap(after(w_z, w_y), x=1), swap(after(w_z, w_y), y=1)
+    w_xz, w_yz = swap(after(w_z, w_y, *ready), x=1), swap(after(w_z, w_y, *ready), y=1)
     w_c, w_xc = swap(after(w, w_z), core=1), swap(after(w_x, w_z), core=1)
     w_yc, w_zc = swap(after(w_y, w_xy), core=1), swap(after(w_z, w_xy), core=1)
     w_xyc = swap(after(w_xy, w_zc), core=1)
@@ -390,9 +386,9 @@
     held = rows_held(places, beam_weights.shape[1])
     me = lax.axis_index("beam")
     chips = places.beam // 2
-    moves = (0, 1, 3, 2)
+    moves = (0, 1, 2, 3)
     if places.square:
-        windows = windows[(me // 2 + np.array(moves, np.int32)) % chips]
+        windows = windows[(me // 2) ^ np.array(moves, np.int32)]
     select = (windows[:, :, None] == held[None, None, :]).astype(jnp.bfloat16)
     mine, other = all_beams(places, element_signals, beam_weights, (select, taken, sides))
     beams = [mine]
@@ -404,12 +400,11 @@
     ordered = list(order_beams(select, beams))
     elements = element_signals.shape[2] * places.beam
     if places.square:
-        here, *away = ordered
-        one, three = places.shift(away[0], 1), places.shift(away[1], 3)
-        pairs = [[here, places.swap(here, core=1)]]
-        shifts = np.array([0, 0, 1, 3, 1, 3, 2, 2], np.int32)
+        here, one, two, three = ordered
+        one = places.swap(one, z=1)
+        shifts = np.array([0, 0, 1, 2, 1, 2, 3, 3], np.int32)
         flips = np.array([0, 1, 0, 0, 1, 1, 0, 1], np.int32)
-        place = (me - 2 * shifts) % places.beam ^ flips
+        place = me ^ (2 * shifts + flips)
         place = jnp.concatenate([place, (me % 2)[None]])
     else:
         fields = list(
@@ -421,17 +416,18 @@
     def run(turn, pair, before):
         return cancel(turn, place, index, pair, first, second, scale, coefs, elements, before)
 
-    out = run(0, pairs[0], None)
     if places.square:
-        two = places.shift(after(away[2], out), 2)
-        one, three = after(one, out), after(three, out)
-        far_one, far_three = places.swap(one, core=1), places.swap(three, core=1)
-        out = run(1, [one, three], out)
-        two = after(two, out)
-        far_two = places.swap(two, core=1)
-        out = run(2, [far_one, far_three], out)
-        return run(3, [two, far_two], out)
-    for i in range(1, chips):
+        two = places.swap(two, z=2)
+        out = run(0, [here, places.swap(here, core=1)], None)
+        three = places.swap(after(three, out), z=3)
+        one, two = after(one, out), after(two, out)
+        far_one, far_two = places.swap(one, core=1), places.swap(two, core=1)
+        out = run(1, [one, two], out)
+        out = run(2, [far_one, far_two], out)
+        three = after(three, out)
+        return run(3, [three, places.swap(three, core=1)], out)
+    out = None
+    for i in range(chips):
         out = run(i, pairs[i], out)
     return out
 

time: 80.1 us -> 78.4 us (0.979)
  waiting for transfers between devices: 30.9 us -> 27.4 us
  local copies, waits for them, and re-layouts: 4.12 us -> 5.95 us
    ppermute x21 -> x24, starting transfers between devices: 13.1 us -> 18.2 us  [swap(): return lax.ppermute(value, ('tm', 'beam'), pairs)]
    ppermute x3 -> x0, waiting for transfers between devices: 4.83 us -> none  [shift(): return lax.ppermute(value, 'beam', pairs)]
    ppermute x3 -> x0, starting transfers between devices: 4.47 us -> none  [shift(): return lax.ppermute(value, 'beam', pairs)]
    ppermute x21 -> x24, waiting for transfers between devices: 26.1 us -> 27.4 us  [swap(): return lax.ppermute(value, ('tm', 'beam'), pairs)]
    gather x1, local copies, waits for them, and re-layouts: 0.69 us -> 1.73 us  [on_device(): taken = jnp.take(table, own[:rows], axis=0, mode='clip')]
    concatenate x1, local copies, waits for them, and re-layouts: 0.21 us -> 1.02 us  [on_device(): jnp.concatenate([neighbours.astype(jnp.float32), leakage[0].astype(jnp.fl...]
  transfers between devices with their start and end apart: 24 -> 24, of which waited for: 12 -> 12; matrix products, arithmetic and copies ran while one was open for 10% -> 11% of each run, Pallas kernels for 21% -> 22%
where the time goes in v5:
time: 78.4 us; the launch traced here: 78 us
  waiting for transfers between devices  27.4 us (35%)
  Pallas kernels  23.4 us (30%)
  starting transfers between devices  18.2 us (23%)
  local copies, waits for them, and re-layouts  5.95 us (8%)
  other arithmetic  2.82 us (4%)
    ppermute x24, waiting for transfers between devices, swap(): return lax.ppermute(value, ('tm', 'beam'), pairs)  27.4 us
    ppermute x24, starting transfers between devices, swap(): return lax.ppermute(value, ('tm', 'beam'), pairs)  18.2 us
    pallas_call x4, Pallas kernels, cancel(): pl.pallas_call(functools.partial(cancel_kernel, (blocks, rows, inner, til...  18 us
    pallas_call x2, Pallas kernels, form_beams(): pl.pallas_call(functools.partial(beams_kernel, pieces), in_specs=[whole]...  2.51 us
    pallas_call x1, Pallas kernels, tables(): pl.pallas_call(functools.partial(tables_kernel, (slots, rows, inner, tile...  2.01 us
    gather x1, local copies, waits for them, and re-layouts, on_device(): taken = jnp.take(table, own[:rows], axis=0, mode='clip')  1.73 us
  transfers between devices with their start and end apart: 24, of which 12 were waited for; matrix products, arithmetic and copies ran while one was open for 11% of the time, Pallas kernels for 22%

profile of v5, /device:TPU:0, one launch (start us, length us, event | category | flops | bytes accessed | tf_op | source)
XLA Modules:
  0.0 78.0 jit_solution(2150275220701298841)
XLA Ops:
  0.0 3.0 %collective-permute-start.4 = (bf16[2,32,2048]{2,1,0:T(8,128)(2,1)}, bf16[2,32,2048]{2,1,0:T(8,128)(2,1)S(1)}, u32[]{:S(2)}, u32[]{:S(2)}) collective-permute-start(bf16[2,32,2048]{2,1,0:T(8,128)(2,1)} %refs_0_.3), channel_id=1, source_target_pairs={{0,16},{1,17},{2,18},{3,19},{4,20},{5,21},{6,22},{7,23},{8,24},{9,... | collective-permute-start | bytes 786440 | tf_op jit(solution)/shard_map/ppermute | solution.py:253
  3.0 1.5 %collective-permute-start.2 = (bf16[2,32,2048]{2,1,0:T(8,128)(2,1)}, bf16[2,32,2048]{2,1,0:T(8,128)(2,1)S(1)}, u32[]{:S(2)}, u32[]{:S(2)}) collective-permute-start(bf16[2,32,2048]{2,1,0:T(8,128)(2,1)} %refs_0_.3), channel_id=1, source_target_pairs={{0,8},{1,9},{2,10},{3,11},{4,12},{5,13},{6,14},{7,15},{8,0},{9,1},... | collective-permute-start | bytes 786440 | tf_op jit(solution)/shard_map/ppermute | solution.py:253
  4.5 2.6 %collective-permute-start = (bf16[2,32,2048]{2,1,0:T(8,128)(2,1)}, bf16[2,32,2048]{2,1,0:T(8,128)(2,1)S(1)}, u32[]{:S(2)}, u32[]{:S(2)}) collective-permute-start(bf16[2,32,2048]{2,1,0:T(8,128)(2,1)} %refs_0_.3), channel_id=1, source_target_pairs={{0,4},{1,5},{2,6},{3,7},{4,0},{5,1},{6,2},{7,3},{8,12},{9,13},{10,... | collective-permute-start | bytes 786440 | tf_op jit(solution)/shard_map/ppermute | solution.py:253
  7.1 0.8 pad_dynamic-slice_fusion
  7.9 1.6 %collective-permute-start.15 = (bf16[2,2048,128]{2,1,0:T(8,128)(2,1)}, bf16[2,2048,128]{2,1,0:T(8,128)(2,1)S(1)}, u32[]{:S(2)}, u32[]{:S(2)}) collective-permute-start(bf16[2,2048,128]{2,1,0:T(8,128)(2,1)} %refs_16_.1), channel_id=1, source_target_pairs={{0,2},{1,3},{2,0},{3,1},{4,6},{5,7},{6,4},{7,5},{8,10},{9,11},{10,... | collective-permute-start | bytes 3145736 | tf_op jit(solution)/shard_map/ppermute | solution.py:253
  9.5 0.8 %pad_slice_fusion.1 = (s32[1024]{0:T(1024)S(1)}, s32[1024]{0:T(1024)S(1)}) fusion(s32[1024]{0:T(1024)} %param.12), kind=kLoop, calls=%fused_computation.10 | loop fusion | bytes 12288 | tf_op jit(solution)/shard_map/slice | solution.py:372
  10.3 0.7 xor_multiply_fusion
  11.1 0.8 convert_element_type.21
  11.8 0.9 %fusion.2 = (bf16[1,1024,6]{1,0,2:T(2,128)(2,1)S(1)}, bf16[1,1024,6]{1,0,2:T(2,128)(2,1)S(1)}) fusion(bf16[2,1024,6]{1,0,2:T(2,128)(2,1)} %param.14), kind=kLoop, calls=%fused_computation.20 | loop fusion | bytes 49152 | tf_op jit(solution)/shard_map/slice | solution.py:379
  12.7 0.7 pad_maximum_fusion
  13.5 1.0 %copy.23 = f32[1024,19]{1,0:T(8,128)} copy(f32[1024,19]{0,1:T(8,128)S(1)} %pad_maximum_fusion) | data formatting | bytes 155648 | tf_op jit(solution)/shard_map/concatenate | solution.py:376
  15.1 1.7 %gather_fusion = f32[192,19]{1,0:T(8,128)S(1)} fusion(f32[1024,19]{1,0:T(8,128)} %copy.23, s32[1024]{0:T(1024)S(1)} %pad_clamp_fusion.1), kind=kCustom, calls=%fused_computation | custom fusion | bytes 29952 | tf_op jit(solution)/shard_map/jit(_take)/gather | solution.py:385
  16.9 0.6 collective-permute-start.5
  18.0 0.8 %collective-permute-done.refs_8_ = bf16[2,32,2048]{2,1,0:T(8,128)(2,1)S(1)} collective-permute-done((bf16[2,32,2048]{2,1,0:T(8,128)(2,1)}, bf16[2,32,2048]{2,1,0:T(8,128)(2,1)S(1)}, u32[]{:S(2)}, u32[]{:S(2)}) %collective-permute-start) | collective-permute-done | bytes 262176 | tf_op jit(solution)/shard_map/ppermute | solution.py:253
  18.8 0.8 collective-permute-start.11
  20.1 6.1 %collective-permute-done.5.refs_6_ = bf16[2,32,2048]{2,1,0:T(8,128)(2,1)S(1)} collective-permute-done((bf16[2,32,2048]{2,1,0:T(8,128)(2,1)S(1)}, bf16[2,32,2048]{2,1,0:T(8,128)(2,1)S(1)}, u32[]{:S(2)}, u32[]{:S(2)}) %collective-permute-start.5) | collective-permute-done | bytes 262176 | tf_op jit(solution)/shard_map/ppermute | solution.py:253
  26.2 3.3 %collective-permute-done.11.refs_12_ = bf16[2,32,2048]{2,1,0:T(8,128)(2,1)S(1)} collective-permute-done((bf16[2,32,2048]{2,1,0:T(8,128)(2,1)S(1)}, bf16[2,32,2048]{2,1,0:T(8,128)(2,1)S(1)}, u32[]{:S(2)}, u32[]{:S(2)}) %collective-permute-start.11) | collective-permute-done | bytes 262176 | tf_op jit(solution)/shard_map/ppermute | solution.py:253
  30.6 5.2 %collective-permute-done.13.refs_14_ = bf16[2,32,2048]{2,1,0:T(8,128)(2,1)S(1)} collective-permute-done((bf16[2,32,2048]{2,1,0:T(8,128)(2,1)S(1)}, bf16[2,32,2048]{2,1,0:T(8,128)(2,1)S(1)}, u32[]{:S(2)}, u32[]{:S(2)}) %collective-permute-start.13) | collective-permute-done | bytes 262176 | tf_op jit(solution)/shard_map/ppermute | solution.py:253
  38.5 1.3 %form_beams.2.refs_1_ = bf16[2,512,128]{2,1,0:T(8,128)(2,1)S(1)} custom-call(bf16[2,32,2048]{2,1,0:T(8,128)(2,1)S(1)} %copy-done.1, bf16[2,32,2048]{2,1,0:T(8,128)(2,1)S(1)} %collective-permute-done.1.refs_1_, bf16[2,32,2048]{2,1,0:T(8,128)(2,1)S(1)} %collective-permute-done.2.refs_2_, bf16[2,32,2048]{2,1,0:T(8,128)(2,1)S(1)} %collective-permute-done.3.refs_3_, ...), custom_call_target="tpu_custom_call" | custom-call | flops 1073741824 | bytes 5242880 | tf_op jit(solution)/shard_map/form_beams/pallas_call | solution.py:46
  39.8 1.3 %form_beams.3 = bf16[2,512,128]{2,1,0:T(8,128)(2,1)S(1)} custom-call(bf16[2,32,2048]{2,1,0:T(8,128)(2,1)S(1)} %copy-done.1, bf16[2,32,2048]{2,1,0:T(8,128)(2,1)S(1)} %collective-permute-done.1.refs_1_, bf16[2,32,2048]{2,1,0:T(8,128)(2,1)S(1)} %collective-permute-done.2.refs_2_, bf16[2,32,2048]{2,1,0:T(8,128)(2,1)S(1)} %collective-permute-done.3.refs_3_, ...), custom_call_target="tpu_custom_call" | custom-call | flops 1073741824 | bytes 5242880 | tf_op jit(solution)/shard_map/form_beams/pallas_call | solution.py:46
  41.6 2.0 %tables.1 = (s32[32]{0:T(128)S(1)}, f32[32,8,128]{2,1,0:T(8,128)S(1)}, bf16[320,512]{1,0:T(8,128)(2,1)S(1)}, bf16[256,512]{1,0:T(8,128)(2,1)S(1)}, f32[2,192,128]{2,1,0:T(8,128)S(1)}) custom-call(s32[16]{0:T(128)S(1)} %copy-done.2, f32[192,19]{1,0:T(8,128)S(1)} %gather_fusion, f32[2,256]{1,0:T(2,128)S(1)} %add_convert_fusion.own), custom_call_target="tpu_custom_call" | custom-call | flops 2949120 | bytes 786432 | tf_op jit(solution)/shard_map/tables/pallas_call | solution.py:343
  43.6 5.9 %collective-permute-done.16.refs_2_ = bf16[2,512,128]{2,1,0:T(8,128)(2,1)S(1)} collective-permute-done((bf16[2,512,128]{2,1,0:T(8,128)(2,1)S(1)}, bf16[2,512,128]{2,1,0:T(8,128)(2,1)S(1)}, u32[]{:S(2)}, u32[]{:S(2)}) %collective-permute-start.16) | collective-permute-done | bytes 262176 | tf_op jit(solution)/shard_map/ppermute | solution.py:253
  49.5 0.8 %order_beams.1 = (bf16[2,320,128]{2,1,0:T(8,128)(2,1)S(1)}, bf16[2,320,128]{2,1,0:T(8,128)(2,1)S(1)}, bf16[2,320,128]{2,1,0:T(8,128)(2,1)S(1)}, bf16[2,320,128]{2,1,0:T(8,128)(2,1)S(1)}) custom-call(bf16[4,320,1024]{2,1,0:T(8,128)(2,1)S(1)} %compare_convert_fusion.refs_0_, bf16[2,512,128]{2,1,0:T(8,128)(2,1)S(1)} %form_beams.2.refs_1_, ...), custom_call_target="tpu_custom_call" | custom-call | flops 671088640 | bytes 3276800 | tf_op jit(solution)/shard_map/order_beams/pallas_call | solution.py:78
  50.9 2.0 %collective-permute-start.21 = (bf16[2,320,128]{2,1,0:T(8,128)(2,1)S(1)}, bf16[2,320,128]{2,1,0:T(8,128)(2,1)S(1)}, u32[]{:S(2)}, u32[]{:S(2)}) collective-permute-start(bf16[2,320,128]{2,1,0:T(8,128)(2,1)S(1)} %get-tuple-element.56), channel_id=1, source_target_pairs={{0,4},{1,5},{2,6},{3,7},{4,0},{5,1},{6,2},{7,3},{8,12},{9,13},{10,... | collective-permute-start | bytes 491528 | tf_op jit(solution)/shard_map/ppermute | solution.py:253
  53.0 1.3 %collective-permute-done.17.refs_1_ = bf16[2,320,128]{2,1,0:T(8,128)(2,1)S(1)} collective-permute-done((bf16[2,320,128]{2,1,0:T(8,128)(2,1)S(1)}, bf16[2,320,128]{2,1,0:T(8,128)(2,1)S(1)}, u32[]{:S(2)}, u32[]{:S(2)}) %collective-permute-start.17) | collective-permute-done | bytes 163872 | tf_op jit(solution)/shard_map/ppermute | solution.py:253
  54.3 4.5 %cancel.4.refs_6_ = bf16[4,128,1024]{2,1,0:T(8,128)(2,1)} custom-call(s32[9]{0:T(128)S(1)} %pad_add_fusion.1.place, s32[32]{0:T(128)S(1)} %get-tuple-element.45.index, bf16[2,320,128]{2,1,0:T(8,128)(2,1)S(1)} %get-tuple-element.52.refs_0_, bf16[2,320,128]{2,1,0:T(8,128)(2,1)S(1)} %collective-permute-done.17.refs_1_, ...), custom_call_target="tpu_custom_call" | custom-call | flops 78888960 | bytes 458752 | tf_op jit(solution)/shard_map/cancel/pallas_call | solution.py:217
  58.8 1.7 %collective-permute-done.21.refs_1_ = bf16[2,320,128]{2,1,0:T(8,128)(2,1)S(1)} collective-permute-done((bf16[2,320,128]{2,1,0:T(8,128)(2,1)S(1)}, bf16[2,320,128]{2,1,0:T(8,128)(2,1)S(1)}, u32[]{:S(2)}, u32[]{:S(2)}) %collective-permute-start.21) | collective-permute-done | bytes 163872 | tf_op jit(solution)/shard_map/ppermute | solution.py:253
  61.0 2.0 %collective-permute-start.18 = (bf16[2,320,128]{2,1,0:T(8,128)(2,1)S(1)}, bf16[2,320,128]{2,1,0:T(8,128)(2,1)S(1)}, u32[]{:S(2)}, u32[]{:S(2)}) collective-permute-start(bf16[2,320,128]{2,1,0:T(8,128)(2,1)S(1)} %get-tuple-element.53), channel_id=1, source_target_pairs={{0,6},{1,7},{2,4},{3,5},{4,2},{5,3},{6,0},{7,1},{8,14},{9,15},{10,... | collective-permute-start | bytes 491528 | tf_op jit(solution)/shard_map/ppermute | solution.py:253
  63.0 4.5 %cancel.5.refs_6_ = bf16[4,128,1024]{2,1,0:T(8,128)(2,1)} custom-call(s32[9]{0:T(128)S(1)} %pad_add_fusion.1.place, s32[32]{0:T(128)S(1)} %get-tuple-element.45.index, bf16[2,320,128]{2,1,0:T(8,128)(2,1)S(1)} %collective-permute-done.19.refs_0_, bf16[2,320,128]{2,1,0:T(8,128)(2,1)S(1)} %collective-permute-done.21.refs_1_, ...), custom_call_target="tpu_custom_call", output_to_operand_aliasing={{}: (8, {})} | custom-call | flops 78888960 | bytes 458752 | tf_op jit(solution)/shard_map/cancel/pallas_call | solution.py:217
  67.5 4.5 %cancel.6.refs_6_ = bf16[4,128,1024]{2,1,0:T(8,128)(2,1)} custom-call(s32[9]{0:T(128)S(1)} %pad_add_fusion.1.place, s32[32]{0:T(128)S(1)} %get-tuple-element.45.index, bf16[2,320,128]{2,1,0:T(8,128)(2,1)S(1)} %collective-permute-done.20.refs_0_, bf16[2,320,128]{2,1,0:T(8,128)(2,1)S(1)} %collective-permute-done.22.refs_1_, ...), custom_call_target="tpu_custom_call", output_to_operand_aliasing={{}: (8, {})} | custom-call | flops 78888960 | bytes 458752 | tf_op jit(solution)/shard_map/cancel/pallas_call | solution.py:217
  72.1 1.4 %collective-permute-done.23.refs_1_ = bf16[2,320,128]{2,1,0:T(8,128)(2,1)S(1)} collective-permute-done((bf16[2,320,128]{2,1,0:T(8,128)(2,1)S(1)}, bf16[2,320,128]{2,1,0:T(8,128)(2,1)S(1)}, u32[]{:S(2)}, u32[]{:S(2)}) %collective-permute-start.23) | collective-permute-done | bytes 163872 | tf_op jit(solution)/shard_map/ppermute | solution.py:253
  73.5 4.5 %cancel.7 = bf16[4,128,1024]{2,1,0:T(8,128)(2,1)} custom-call(s32[9]{0:T(128)S(1)} %pad_add_fusion.1.place, s32[32]{0:T(128)S(1)} %get-tuple-element.45.index, bf16[2,320,128]{2,1,0:T(8,128)(2,1)S(1)} %collective-permute-done.18.refs_0_, bf16[2,320,128]{2,1,0:T(8,128)(2,1)S(1)} %collective-permute-done.23.refs_1_, ...), custom_call_target="tpu_custom_call", output_to_operand_aliasing={{}: (8, {})} | custom-call | flops 78888960 | bytes 458752 | tf_op jit(solution)/shard_map/cancel/pallas_call | solution.py:217
  (56 shorter events, 7.4 us)
Async XLA Ops:
  0.0 30.0 %copy-start.1 = (bf16[2,32,2048]{2,1,0:T(8,128)(2,1)S(1)}, bf16[2,32,2048]{2,1,0:T(8,128)(2,1)}, u32[]{:S(2)}) copy-start(bf16[2,32,2048]{2,1,0:T(8,128)(2,1)} %refs_0_.3) | copy-start | bytes 786436
  0.0 38.5 %copy-start = (bf16[2,2048,128]{2,1,0:T(8,128)(2,1)S(1)}, bf16[2,2048,128]{2,1,0:T(8,128)(2,1)}, u32[]{:S(2)}) copy-start(bf16[2,2048,128]{2,1,0:T(8,128)(2,1)} %refs_16_.1) | copy-start | bytes 3145732
  0.0 16.9 %collective-permute-start.4 = (bf16[2,32,2048]{2,1,0:T(8,128)(2,1)}, bf16[2,32,2048]{2,1,0:T(8,128)(2,1)S(1)}, u32[]{:S(2)}, u32[]{:S(2)}) collective-permute-start(bf16[2,32,2048]{2,1,0:T(8,128)(2,1)} %refs_0_.3), channel_id=1, source_target_pairs={{0,16},{1,17},{2,18},{3,19},{4,20},{5,21},{6,22},{7,23},{8,24},{9,... | collective-permute-start | bytes 786440 | tf_op jit(solution)/shard_map/ppermute | solution.py:253
  3.0 13.9 %collective-permute-start.2 = (bf16[2,32,2048]{2,1,0:T(8,128)(2,1)}, bf16[2,32,2048]{2,1,0:T(8,128)(2,1)S(1)}, u32[]{:S(2)}, u32[]{:S(2)}) collective-permute-start(bf16[2,32,2048]{2,1,0:T(8,128)(2,1)} %refs_0_.3), channel_id=1, source_target_pairs={{0,8},{1,9},{2,10},{3,11},{4,12},{5,13},{6,14},{7,15},{8,0},{9,1},... | collective-permute-start | bytes 786440 | tf_op jit(solution)/shard_map/ppermute | solution.py:253
  4.5 14.3 %collective-permute-start = (bf16[2,32,2048]{2,1,0:T(8,128)(2,1)}, bf16[2,32,2048]{2,1,0:T(8,128)(2,1)S(1)}, u32[]{:S(2)}, u32[]{:S(2)}) collective-permute-start(bf16[2,32,2048]{2,1,0:T(8,128)(2,1)} %refs_0_.3), channel_id=1, source_target_pairs={{0,4},{1,5},{2,6},{3,7},{4,0},{5,1},{6,2},{7,3},{8,12},{9,13},{10,... | collective-permute-start | bytes 786440 | tf_op jit(solution)/shard_map/ppermute | solution.py:253
  7.9 31.9 %collective-permute-start.15 = (bf16[2,2048,128]{2,1,0:T(8,128)(2,1)}, bf16[2,2048,128]{2,1,0:T(8,128)(2,1)S(1)}, u32[]{:S(2)}, u32[]{:S(2)}) collective-permute-start(bf16[2,2048,128]{2,1,0:T(8,128)(2,1)} %refs_16_.1), channel_id=1, source_target_pairs={{0,2},{1,3},{2,0},{3,1},{4,6},{5,7},{6,4},{7,5},{8,10},{9,11},{10,... | collective-permute-start | bytes 3145736 | tf_op jit(solution)/shard_map/ppermute | solution.py:253
  16.9 9.3 %collective-permute-start.5 = (bf16[2,32,2048]{2,1,0:T(8,128)(2,1)S(1)}, bf16[2,32,2048]{2,1,0:T(8,128)(2,1)S(1)}, u32[]{:S(2)}, u32[]{:S(2)}) collective-permute-start(bf16[2,32,2048]{2,1,0:T(8,128)(2,1)S(1)} %collective-permute-done.2.refs_2_), channel_id=1, source_target_pairs={{0,16},{1,17},{2,18},{3,19},{4,20},{5,21},{6,22},{7,23},{8,24},{9,... | collective-permute-start | bytes 786440 | tf_op jit(solution)/shard_map/ppermute | solution.py:253
  18.8 10.7 %collective-permute-start.11 = (bf16[2,32,2048]{2,1,0:T(8,128)(2,1)S(1)}, bf16[2,32,2048]{2,1,0:T(8,128)(2,1)S(1)}, u32[]{:S(2)}, u32[]{:S(2)}) collective-permute-start(bf16[2,32,2048]{2,1,0:T(8,128)(2,1)S(1)} %collective-permute-done.refs_8_), channel_id=1, source_target_pairs={{0,16},{1,17},{2,18},{3,19},{4,20},{5,21},{6,22},{7,23},{8,24},{9,... | collective-permute-start | bytes 786440 | tf_op jit(solution)/shard_map/ppermute | solution.py:253
  19.6 9.9 %collective-permute-start.9 = (bf16[2,32,2048]{2,1,0:T(8,128)(2,1)S(1)}, bf16[2,32,2048]{2,1,0:T(8,128)(2,1)S(1)}, u32[]{:S(2)}, u32[]{:S(2)}) collective-permute-start(bf16[2,32,2048]{2,1,0:T(8,128)(2,1)S(1)} %collective-permute-done.refs_8_), channel_id=1, source_target_pairs={{0,8},{1,9},{2,10},{3,11},{4,12},{5,13},{6,14},{7,15},{8,0},{9,1},... | collective-permute-start | bytes 786440 | tf_op jit(solution)/shard_map/ppermute | solution.py:253
  26.2 3.8 %collective-permute-start.7 = (bf16[2,32,2048]{2,1,0:T(8,128)(2,1)S(1)}, bf16[2,32,2048]{2,1,0:T(8,128)(2,1)S(1)}, u32[]{:S(2)}, u32[]{:S(2)}) collective-permute-start(bf16[2,32,2048]{2,1,0:T(8,128)(2,1)S(1)} %collective-permute-done.refs_8_), channel_id=1, source_target_pairs={{0,1},{1,0},{2,3},{3,2},{4,5},{5,4},{6,7},{7,6},{8,9},{9,8},{10,11... | collective-permute-start | bytes 786440 | tf_op jit(solution)/shard_map/ppermute | solution.py:253
  29.5 6.4 %collective-permute-start.13 = (bf16[2,32,2048]{2,1,0:T(8,128)(2,1)S(1)}, bf16[2,32,2048]{2,1,0:T(8,128)(2,1)S(1)}, u32[]{:S(2)}, u32[]{:S(2)}) collective-permute-start(bf16[2,32,2048]{2,1,0:T(8,128)(2,1)S(1)} %collective-permute-done.11.refs_12_), channel_id=1, source_target_pairs={{0,8},{1,9},{2,10},{3,11},{4,12},{5,13},{6,14},{7,15},{8,0},{9,1},... | collective-permute-start | bytes 786440 | tf_op jit(solution)/shard_map/ppermute | solution.py:253
  30.0 5.8 %collective-permute-start.8 = (bf16[2,32,2048]{2,1,0:T(8,128)(2,1)S(1)}, bf16[2,32,2048]{2,1,0:T(8,128)(2,1)S(1)}, u32[]{:S(2)}, u32[]{:S(2)}) collective-permute-start(bf16[2,32,2048]{2,1,0:T(8,128)(2,1)S(1)} %collective-permute-done.5.refs_6_), channel_id=1, source_target_pairs={{0,1},{1,0},{2,3},{3,2},{4,5},{5,4},{6,7},{7,6},{8,9},{9,8},{10,11... | collective-permute-start | bytes 786440 | tf_op jit(solution)/shard_map/ppermute | solution.py:253
  30.1 6.3 %collective-permute-start.1 = (bf16[2,32,2048]{2,1,0:T(8,128)(2,1)S(1)}, bf16[2,32,2048]{2,1,0:T(8,128)(2,1)S(1)}, u32[]{:S(2)}, u32[]{:S(2)}) collective-permute-start(bf16[2,32,2048]{2,1,0:T(8,128)(2,1)S(1)} %copy-done.1), channel_id=1, source_target_pairs={{0,1},{1,0},{2,3},{3,2},{4,5},{5,4},{6,7},{7,6},{8,9},{9,8},{10,11... | collective-permute-start | bytes 786440 | tf_op jit(solution)/shard_map/ppermute | solution.py:253
  30.6 5.9 %collective-permute-start.3 = (bf16[2,32,2048]{2,1,0:T(8,128)(2,1)S(1)}, bf16[2,32,2048]{2,1,0:T(8,128)(2,1)S(1)}, u32[]{:S(2)}, u32[]{:S(2)}) collective-permute-start(bf16[2,32,2048]{2,1,0:T(8,128)(2,1)S(1)} %collective-permute-done.2.refs_2_), channel_id=1, source_target_pairs={{0,1},{1,0},{2,3},{3,2},{4,5},{5,4},{6,7},{7,6},{8,9},{9,8},{10,11... | collective-permute-start | bytes 786440 | tf_op jit(solution)/shard_map/ppermute | solution.py:253
  35.9 1.5 %collective-permute-start.6 = (bf16[2,32,2048]{2,1,0:T(8,128)(2,1)S(1)}, bf16[2,32,2048]{2,1,0:T(8,128)(2,1)S(1)}, u32[]{:S(2)}, u32[]{:S(2)}) collective-permute-start(bf16[2,32,2048]{2,1,0:T(8,128)(2,1)S(1)} %collective-permute-done.4.refs_4_), channel_id=1, source_target_pairs={{0,1},{1,0},{2,3},{3,2},{4,5},{5,4},{6,7},{7,6},{8,9},{9,8},{10,11... | collective-permute-start | bytes 786440 | tf_op jit(solution)/shard_map/ppermute | solution.py:253
  35.9 1.9 %collective-permute-start.14 = (bf16[2,32,2048]{2,1,0:T(8,128)(2,1)S(1)}, bf16[2,32,2048]{2,1,0:T(8,128)(2,1)S(1)}, u32[]{:S(2)}, u32[]{:S(2)}) collective-permute-start(bf16[2,32,2048]{2,1,0:T(8,128)(2,1)S(1)} %collective-permute-done.13.refs_14_), channel_id=1, source_target_pairs={{0,1},{1,0},{2,3},{3,2},{4,5},{5,4},{6,7},{7,6},{8,9},{9,8},{10,11... | collective-permute-start | bytes 786440 | tf_op jit(solution)/shard_map/ppermute | solution.py:253
  36.4 1.8 %collective-permute-start.12 = (bf16[2,32,2048]{2,1,0:T(8,128)(2,1)S(1)}, bf16[2,32,2048]{2,1,0:T(8,128)(2,1)S(1)}, u32[]{:S(2)}, u32[]{:S(2)}) collective-permute-start(bf16[2,32,2048]{2,1,0:T(8,128)(2,1)S(1)} %collective-permute-done.11.refs_12_), channel_id=1, source_target_pairs={{0,1},{1,0},{2,3},{3,2},{4,5},{5,4},{6,7},{7,6},{8,9},{9,8},{10,11... | collective-permute-start | bytes 786440 | tf_op jit(solution)/shard_map/ppermute | solution.py:253
  36.5 2.1 %collective-permute-start.10 = (bf16[2,32,2048]{2,1,0:T(8,128)(2,1)S(1)}, bf16[2,32,2048]{2,1,0:T(8,128)(2,1)S(1)}, u32[]{:S(2)}, u32[]{:S(2)}) collective-permute-start(bf16[2,32,2048]{2,1,0:T(8,128)(2,1)S(1)} %collective-permute-done.9.refs_10_), channel_id=1, source_target_pairs={{0,1},{1,0},{2,3},{3,2},{4,5},{5,4},{6,7},{7,6},{8,9},{9,8},{10,11... | collective-permute-start | bytes 786440 | tf_op jit(solution)/shard_map/ppermute | solution.py:253
  39.8 1.8 %copy-start.2 = (s32[16]{0:T(128)S(1)}, s32[16]{0:T(128)}, u32[]{:S(2)}) copy-start(s32[16]{0:T(128)} %labels.1) | copy-start | bytes 196
  41.1 11.8 %copy-start.3 = (s32[8]{0:T(128)S(1)}, s32[8]{0:T(128)}, u32[]{:S(2)}) copy-start(s32[8]{0:T(128)} %constant.52.clone) | copy-start | bytes 100
  41.1 8.4 %collective-permute-start.16 = (bf16[2,512,128]{2,1,0:T(8,128)(2,1)S(1)}, bf16[2,512,128]{2,1,0:T(8,128)(2,1)S(1)}, u32[]{:S(2)}, u32[]{:S(2)}) collective-permute-start(bf16[2,512,128]{2,1,0:T(8,128)(2,1)S(1)} %form_beams.3), channel_id=1, source_target_pairs={{0,2},{1,3},{2,0},{3,1},{4,6},{5,7},{6,4},{7,5},{8,10},{9,11},{10,... | collective-permute-start | bytes 786440 | tf_op jit(solution)/shard_map/ppermute | solution.py:253
  50.4 10.1 %collective-permute-start.19 = (bf16[2,320,128]{2,1,0:T(8,128)(2,1)S(1)}, bf16[2,320,128]{2,1,0:T(8,128)(2,1)S(1)}, u32[]{:S(2)}, u32[]{:S(2)}) collective-permute-start(bf16[2,320,128]{2,1,0:T(8,128)(2,1)S(1)} %get-tuple-element.54), channel_id=1, source_target_pairs={{0,2},{1,3},{2,0},{3,1},{4,6},{5,7},{6,4},{7,5},{8,10},{9,11},{10,... | collective-permute-start | bytes 491528 | tf_op jit(solution)/shard_map/ppermute | solution.py:253
  50.9 9.6 %collective-permute-start.21 = (bf16[2,320,128]{2,1,0:T(8,128)(2,1)S(1)}, bf16[2,320,128]{2,1,0:T(8,128)(2,1)S(1)}, u32[]{:S(2)}, u32[]{:S(2)}) collective-permute-start(bf16[2,320,128]{2,1,0:T(8,128)(2,1)S(1)} %get-tuple-element.56), channel_id=1, source_target_pairs={{0,4},{1,5},{2,6},{3,7},{4,0},{5,1},{6,2},{7,3},{8,12},{9,13},{10,... | collective-permute-start | bytes 491528 | tf_op jit(solution)/shard_map/ppermute | solution.py:253
  52.9 1.4 %collective-permute-start.17 = (bf16[2,320,128]{2,1,0:T(8,128)(2,1)S(1)}, bf16[2,320,128]{2,1,0:T(8,128)(2,1)S(1)}, u32[]{:S(2)}, u32[]{:S(2)}) collective-permute-start(bf16[2,320,128]{2,1,0:T(8,128)(2,1)S(1)} %get-tuple-element.52.refs_0_), channel_id=1, source_target_pairs={{0,1},{1,0},{2,3},{3,2},{4,5},{5,4},{6,7},{7,6},{8,9},{9,8},{10,11... | collective-permute-start | bytes 491528 | tf_op jit(solution)/shard_map/ppermute | solution.py:253
  60.5 7.0 %collective-permute-start.20 = (bf16[2,320,128]{2,1,0:T(8,128)(2,1)S(1)}, bf16[2,320,128]{2,1,0:T(8,128)(2,1)S(1)}, u32[]{:S(2)}, u32[]{:S(2)}) collective-permute-start(bf16[2,320,128]{2,1,0:T(8,128)(2,1)S(1)} %collective-permute-done.19.refs_0_), channel_id=1, source_target_pairs={{0,1},{1,0},{2,3},{3,2},{4,5},{5,4},{6,7},{7,6},{8,9},{9,8},{10,11... | collective-permute-start | bytes 491528 | tf_op jit(solution)/shard_map/ppermute | solution.py:253
  60.5 7.0 %collective-permute-start.22 = (bf16[2,320,128]{2,1,0:T(8,128)(2,1)S(1)}, bf16[2,320,128]{2,1,0:T(8,128)(2,1)S(1)}, u32[]{:S(2)}, u32[]{:S(2)}) collective-permute-start(bf16[2,320,128]{2,1,0:T(8,128)(2,1)S(1)} %collective-permute-done.21.refs_1_), channel_id=1, source_target_pairs={{0,1},{1,0},{2,3},{3,2},{4,5},{5,4},{6,7},{7,6},{8,9},{9,8},{10,11... | collective-permute-start | bytes 491528 | tf_op jit(solution)/shard_map/ppermute | solution.py:253
  61.0 11.1 %collective-permute-start.18 = (bf16[2,320,128]{2,1,0:T(8,128)(2,1)S(1)}, bf16[2,320,128]{2,1,0:T(8,128)(2,1)S(1)}, u32[]{:S(2)}, u32[]{:S(2)}) collective-permute-start(bf16[2,320,128]{2,1,0:T(8,128)(2,1)S(1)} %get-tuple-element.53), channel_id=1, source_target_pairs={{0,6},{1,7},{2,4},{3,5},{4,2},{5,3},{6,0},{7,1},{8,14},{9,15},{10,... | collective-permute-start | bytes 491528 | tf_op jit(solution)/shard_map/ppermute | solution.py:253
  72.1 1.5 %collective-permute-start.23 = (bf16[2,320,128]{2,1,0:T(8,128)(2,1)S(1)}, bf16[2,320,128]{2,1,0:T(8,128)(2,1)S(1)}, u32[]{:S(2)}, u32[]{:S(2)}) collective-permute-start(bf16[2,320,128]{2,1,0:T(8,128)(2,1)S(1)} %collective-permute-done.18.refs_0_), channel_id=1, source_target_pairs={{0,1},{1,0},{2,3},{3,2},{4,5},{5,4},{6,7},{7,6},{8,9},{9,8},{10,11... | collective-permute-start | bytes 491528 | tf_op jit(solution)/shard_map/ppermute | solution.py:253

commit v6 on v5

--- a/solution.py
+++ b/solution.py
@@ -419,8 +419,8 @@
     if places.square:
         two = places.swap(two, z=2)
         out = run(0, [here, places.swap(here, core=1)], None)
-        three = places.swap(after(three, out), z=3)
         one, two = after(one, out), after(two, out)
+        three = places.swap(after(three, two), z=3)
         far_one, far_two = places.swap(one, core=1), places.swap(two, core=1)
         out = run(1, [one, two], out)
         out = run(2, [far_one, far_two], out)

time: 78.4 us -> 78.1 us (level)
  no operation moved by 1% of the time
where the time goes in v6:
time: 78.1 us; the launch traced here: 77.7 us
  waiting for transfers between devices  27.1 us (35%)
  Pallas kernels  23.4 us (30%)
  starting transfers between devices  18.2 us (23%)
  local copies, waits for them, and re-layouts  5.95 us (8%)
  other arithmetic  2.82 us (4%)
    ppermute x24, waiting for transfers between devices, swap(): return lax.ppermute(value, ('tm', 'beam'), pairs)  27.1 us
    ppermute x24, starting transfers between devices, swap(): return lax.ppermute(value, ('tm', 'beam'), pairs)  18.2 us
    pallas_call x4, Pallas kernels, cancel(): pl.pallas_call(functools.partial(cancel_kernel, (blocks, rows, inner, til...  18 us
    pallas_call x2, Pallas kernels, form_beams(): pl.pallas_call(functools.partial(beams_kernel, pieces), in_specs=[whole]...  2.51 us
    pallas_call x1, Pallas kernels, tables(): pl.pallas_call(functools.partial(tables_kernel, (slots, rows, inner, tile...  2.01 us
    gather x1, local copies, waits for them, and re-layouts, on_device(): taken = jnp.take(table, own[:rows], axis=0, mode='clip')  1.73 us
  transfers between devices with their start and end apart: 24, of which 12 were waited for; matrix products, arithmetic and copies ran while one was open for 11% of the time, Pallas kernels for 22%

profile of v6, /device:TPU:0, one launch (start us, length us, event | category | flops | bytes accessed | tf_op | source)
XLA Modules:
  0.0 77.7 jit_solution(3933355084703854497)
XLA Ops:
  0.0 3.0 %collective-permute-start.4 = (bf16[2,32,2048]{2,1,0:T(8,128)(2,1)}, bf16[2,32,2048]{2,1,0:T(8,128)(2,1)S(1)}, u32[]{:S(2)}, u32[]{:S(2)}) collective-permute-start(bf16[2,32,2048]{2,1,0:T(8,128)(2,1)} %refs_0_.3), channel_id=1, source_target_pairs={{0,16},{1,17},{2,18},{3,19},{4,20},{5,21},{6,22},{7,23},{8,24},{9,... | collective-permute-start | bytes 786440 | tf_op jit(solution)/shard_map/ppermute | solution.py:253
  3.0 1.5 %collective-permute-start.2 = (bf16[2,32,2048]{2,1,0:T(8,128)(2,1)}, bf16[2,32,2048]{2,1,0:T(8,128)(2,1)S(1)}, u32[]{:S(2)}, u32[]{:S(2)}) collective-permute-start(bf16[2,32,2048]{2,1,0:T(8,128)(2,1)} %refs_0_.3), channel_id=1, source_target_pairs={{0,8},{1,9},{2,10},{3,11},{4,12},{5,13},{6,14},{7,15},{8,0},{9,1},... | collective-permute-start | bytes 786440 | tf_op jit(solution)/shard_map/ppermute | solution.py:253
  4.5 2.6 %collective-permute-start = (bf16[2,32,2048]{2,1,0:T(8,128)(2,1)}, bf16[2,32,2048]{2,1,0:T(8,128)(2,1)S(1)}, u32[]{:S(2)}, u32[]{:S(2)}) collective-permute-start(bf16[2,32,2048]{2,1,0:T(8,128)(2,1)} %refs_0_.3), channel_id=1, source_target_pairs={{0,4},{1,5},{2,6},{3,7},{4,0},{5,1},{6,2},{7,3},{8,12},{9,13},{10,... | collective-permute-start | bytes 786440 | tf_op jit(solution)/shard_map/ppermute | solution.py:253
  7.1 0.8 pad_dynamic-slice_fusion
  7.9 1.6 %collective-permute-start.15 = (bf16[2,2048,128]{2,1,0:T(8,128)(2,1)}, bf16[2,2048,128]{2,1,0:T(8,128)(2,1)S(1)}, u32[]{:S(2)}, u32[]{:S(2)}) collective-permute-start(bf16[2,2048,128]{2,1,0:T(8,128)(2,1)} %refs_16_.1), channel_id=1, source_target_pairs={{0,2},{1,3},{2,0},{3,1},{4,6},{5,7},{6,4},{7,5},{8,10},{9,11},{10,... | collective-permute-start | bytes 3145736 | tf_op jit(solution)/shard_map/ppermute | solution.py:253
  9.5 0.8 %pad_slice_fusion.1 = (s32[1024]{0:T(1024)S(1)}, s32[1024]{0:T(1024)S(1)}) fusion(s32[1024]{0:T(1024)} %param.12), kind=kLoop, calls=%fused_computation.10 | loop fusion | bytes 12288 | tf_op jit(solution)/shard_map/slice | solution.py:372
  10.3 0.7 xor_multiply_fusion
  11.1 0.8 convert_element_type.21
  11.8 0.9 %fusion.2 = (bf16[1,1024,6]{1,0,2:T(2,128)(2,1)S(1)}, bf16[1,1024,6]{1,0,2:T(2,128)(2,1)S(1)}) fusion(bf16[2,1024,6]{1,0,2:T(2,128)(2,1)} %param.14), kind=kLoop, calls=%fused_computation.20 | loop fusion | bytes 49152 | tf_op jit(solution)/shard_map/slice | solution.py:379
  12.7 0.7 pad_maximum_fusion
  13.5 1.0 %copy.23 = f32[1024,19]{1,0:T(8,128)} copy(f32[1024,19]{0,1:T(8,128)S(1)} %pad_maximum_fusion) | data formatting | bytes 155648 | tf_op jit(solution)/shard_map/concatenate | solution.py:376
  15.1 1.7 %gather_fusion = f32[192,19]{1,0:T(8,128)S(1)} fusion(f32[1024,19]{1,0:T(8,128)} %copy.23, s32[1024]{0:T(1024)S(1)} %pad_clamp_fusion.1), kind=kCustom, calls=%fused_computation | custom fusion | bytes 29952 | tf_op jit(solution)/shard_map/jit(_take)/gather | solution.py:385
  18.0 0.8 %collective-permute-done.refs_8_ = bf16[2,32,2048]{2,1,0:T(8,128)(2,1)S(1)} collective-permute-done((bf16[2,32,2048]{2,1,0:T(8,128)(2,1)}, bf16[2,32,2048]{2,1,0:T(8,128)(2,1)S(1)}, u32[]{:S(2)}, u32[]{:S(2)}) %collective-permute-start) | collective-permute-done | bytes 262176 | tf_op jit(solution)/shard_map/ppermute | solution.py:253
  18.8 0.8 collective-permute-start.11
  20.1 6.1 %collective-permute-done.5.refs_6_ = bf16[2,32,2048]{2,1,0:T(8,128)(2,1)S(1)} collective-permute-done((bf16[2,32,2048]{2,1,0:T(8,128)(2,1)S(1)}, bf16[2,32,2048]{2,1,0:T(8,128)(2,1)S(1)}, u32[]{:S(2)}, u32[]{:S(2)}) %collective-permute-start.5) | collective-permute-done | bytes 262176 | tf_op jit(solution)/shard_map/ppermute | solution.py:253
  26.2 3.3 %collective-permute-done.11.refs_12_ = bf16[2,32,2048]{2,1,0:T(8,128)(2,1)S(1)} collective-permute-done((bf16[2,32,2048]{2,1,0:T(8,128)(2,1)S(1)}, bf16[2,32,2048]{2,1,0:T(8,128)(2,1)S(1)}, u32[]{:S(2)}, u32[]{:S(2)}) %collective-permute-start.11) | collective-permute-done | bytes 262176 | tf_op jit(solution)/shard_map/ppermute | solution.py:253
  30.6 5.2 %collective-permute-done.13.refs_14_ = bf16[2,32,2048]{2,1,0:T(8,128)(2,1)S(1)} collective-permute-done((bf16[2,32,2048]{2,1,0:T(8,128)(2,1)S(1)}, bf16[2,32,2048]{2,1,0:T(8,128)(2,1)S(1)}, u32[]{:S(2)}, u32[]{:S(2)}) %collective-permute-start.13) | collective-permute-done | bytes 262176 | tf_op jit(solution)/shard_map/ppermute | solution.py:253
  38.5 1.3 %form_beams.2.refs_1_ = bf16[2,512,128]{2,1,0:T(8,128)(2,1)S(1)} custom-call(bf16[2,32,2048]{2,1,0:T(8,128)(2,1)S(1)} %copy-done.1, bf16[2,32,2048]{2,1,0:T(8,128)(2,1)S(1)} %collective-permute-done.1.refs_1_, bf16[2,32,2048]{2,1,0:T(8,128)(2,1)S(1)} %collective-permute-done.2.refs_2_, bf16[2,32,2048]{2,1,0:T(8,128)(2,1)S(1)} %collective-permute-done.3.refs_3_, ...), custom_call_target="tpu_custom_call" | custom-call | flops 1073741824 | bytes 5242880 | tf_op jit(solution)/shard_map/form_beams/pallas_call | solution.py:46
  39.8 1.3 %form_beams.3 = bf16[2,512,128]{2,1,0:T(8,128)(2,1)S(1)} custom-call(bf16[2,32,2048]{2,1,0:T(8,128)(2,1)S(1)} %copy-done.1, bf16[2,32,2048]{2,1,0:T(8,128)(2,1)S(1)} %collective-permute-done.1.refs_1_, bf16[2,32,2048]{2,1,0:T(8,128)(2,1)S(1)} %collective-permute-done.2.refs_2_, bf16[2,32,2048]{2,1,0:T(8,128)(2,1)S(1)} %collective-permute-done.3.refs_3_, ...), custom_call_target="tpu_custom_call" | custom-call | flops 1073741824 | bytes 5242880 | tf_op jit(solution)/shard_map/form_beams/pallas_call | solution.py:46
  41.6 2.0 %tables.1 = (s32[32]{0:T(128)S(1)}, f32[32,8,128]{2,1,0:T(8,128)S(1)}, bf16[320,512]{1,0:T(8,128)(2,1)S(1)}, bf16[256,512]{1,0:T(8,128)(2,1)S(1)}, f32[2,192,128]{2,1,0:T(8,128)S(1)}) custom-call(s32[16]{0:T(128)S(1)} %copy-done.2, f32[192,19]{1,0:T(8,128)S(1)} %gather_fusion, f32[2,256]{1,0:T(2,128)S(1)} %add_convert_fusion.own), custom_call_target="tpu_custom_call" | custom-call | flops 2949120 | bytes 786432 | tf_op jit(solution)/shard_map/tables/pallas_call | solution.py:343
  43.6 5.9 %collective-permute-done.16.refs_2_ = bf16[2,512,128]{2,1,0:T(8,128)(2,1)S(1)} collective-permute-done((bf16[2,512,128]{2,1,0:T(8,128)(2,1)S(1)}, bf16[2,512,128]{2,1,0:T(8,128)(2,1)S(1)}, u32[]{:S(2)}, u32[]{:S(2)}) %collective-permute-start.16) | collective-permute-done | bytes 262176 | tf_op jit(solution)/shard_map/ppermute | solution.py:253
  49.5 0.8 %order_beams.1 = (bf16[2,320,128]{2,1,0:T(8,128)(2,1)S(1)}, bf16[2,320,128]{2,1,0:T(8,128)(2,1)S(1)}, bf16[2,320,128]{2,1,0:T(8,128)(2,1)S(1)}, bf16[2,320,128]{2,1,0:T(8,128)(2,1)S(1)}) custom-call(bf16[4,320,1024]{2,1,0:T(8,128)(2,1)S(1)} %compare_convert_fusion.refs_0_, bf16[2,512,128]{2,1,0:T(8,128)(2,1)S(1)} %form_beams.2.refs_1_, ...), custom_call_target="tpu_custom_call" | custom-call | flops 671088640 | bytes 3276800 | tf_op jit(solution)/shard_map/order_beams/pallas_call | solution.py:78
  50.4 0.8 collective-permute-start.17
  51.1 1.7 %collective-permute-start.20 = (bf16[2,320,128]{2,1,0:T(8,128)(2,1)S(1)}, bf16[2,320,128]{2,1,0:T(8,128)(2,1)S(1)}, u32[]{:S(2)}, u32[]{:S(2)}) collective-permute-start(bf16[2,320,128]{2,1,0:T(8,128)(2,1)S(1)} %get-tuple-element.56), channel_id=1, source_target_pairs={{0,2},{1,3},{2,0},{3,1},{4,6},{5,7},{6,4},{7,5},{8,10},{9,11},{10,... | collective-permute-start | bytes 491528 | tf_op jit(solution)/shard_map/ppermute | solution.py:253
  53.0 1.3 %collective-permute-done.18.refs_1_ = bf16[2,320,128]{2,1,0:T(8,128)(2,1)S(1)} collective-permute-done((bf16[2,320,128]{2,1,0:T(8,128)(2,1)S(1)}, bf16[2,320,128]{2,1,0:T(8,128)(2,1)S(1)}, u32[]{:S(2)}, u32[]{:S(2)}) %collective-permute-start.18) | collective-permute-done | bytes 163872 | tf_op jit(solution)/shard_map/ppermute | solution.py:253
  54.3 4.5 %cancel.4.refs_6_ = bf16[4,128,1024]{2,1,0:T(8,128)(2,1)} custom-call(s32[9]{0:T(128)S(1)} %pad_add_fusion.1.place, s32[32]{0:T(128)S(1)} %get-tuple-element.45.index, bf16[2,320,128]{2,1,0:T(8,128)(2,1)S(1)} %get-tuple-element.53.refs_0_, bf16[2,320,128]{2,1,0:T(8,128)(2,1)S(1)} %collective-permute-done.18.refs_1_, ...), custom_call_target="tpu_custom_call" | custom-call | flops 78888960 | bytes 458752 | tf_op jit(solution)/shard_map/cancel/pallas_call | solution.py:217
  58.8 1.4 %collective-permute-done.17.refs_1_ = bf16[2,320,128]{2,1,0:T(8,128)(2,1)S(1)} collective-permute-done((bf16[2,320,128]{2,1,0:T(8,128)(2,1)S(1)}, bf16[2,320,128]{2,1,0:T(8,128)(2,1)S(1)}, u32[]{:S(2)}, u32[]{:S(2)}) %collective-permute-start.17) | collective-permute-done | bytes 163872 | tf_op jit(solution)/shard_map/ppermute | solution.py:253
  60.7 2.0 %collective-permute-start.19 = (bf16[2,320,128]{2,1,0:T(8,128)(2,1)S(1)}, bf16[2,320,128]{2,1,0:T(8,128)(2,1)S(1)}, u32[]{:S(2)}, u32[]{:S(2)}) collective-permute-start(bf16[2,320,128]{2,1,0:T(8,128)(2,1)S(1)} %get-tuple-element.55), channel_id=1, source_target_pairs={{0,6},{1,7},{2,4},{3,5},{4,2},{5,3},{6,0},{7,1},{8,14},{9,15},{10,... | collective-permute-start | bytes 491528 | tf_op jit(solution)/shard_map/ppermute | solution.py:253
  62.7 4.5 %cancel.5.refs_6_ = bf16[4,128,1024]{2,1,0:T(8,128)(2,1)} custom-call(s32[9]{0:T(128)S(1)} %pad_add_fusion.1.place, s32[32]{0:T(128)S(1)} %get-tuple-element.45.index, bf16[2,320,128]{2,1,0:T(8,128)(2,1)S(1)} %collective-permute-done.20.refs_0_, bf16[2,320,128]{2,1,0:T(8,128)(2,1)S(1)} %collective-permute-done.17.refs_1_, ...), custom_call_target="tpu_custom_call", output_to_operand_aliasing={{}: (8, {})} | custom-call | flops 78888960 | bytes 458752 | tf_op jit(solution)/shard_map/cancel/pallas_call | solution.py:217
  67.2 4.5 %cancel.6.refs_6_ = bf16[4,128,1024]{2,1,0:T(8,128)(2,1)} custom-call(s32[9]{0:T(128)S(1)} %pad_add_fusion.1.place, s32[32]{0:T(128)S(1)} %get-tuple-element.45.index, bf16[2,320,128]{2,1,0:T(8,128)(2,1)S(1)} %collective-permute-done.21.refs_0_, bf16[2,320,128]{2,1,0:T(8,128)(2,1)S(1)} %collective-permute-done.22.refs_1_, ...), custom_call_target="tpu_custom_call", output_to_operand_aliasing={{}: (8, {})} | custom-call | flops 78888960 | bytes 458752 | tf_op jit(solution)/shard_map/cancel/pallas_call | solution.py:217
  71.8 1.4 %collective-permute-done.23.refs_1_ = bf16[2,320,128]{2,1,0:T(8,128)(2,1)S(1)} collective-permute-done((bf16[2,320,128]{2,1,0:T(8,128)(2,1)S(1)}, bf16[2,320,128]{2,1,0:T(8,128)(2,1)S(1)}, u32[]{:S(2)}, u32[]{:S(2)}) %collective-permute-start.23) | collective-permute-done | bytes 163872 | tf_op jit(solution)/shard_map/ppermute | solution.py:253
  73.2 4.5 %cancel.7 = bf16[4,128,1024]{2,1,0:T(8,128)(2,1)} custom-call(s32[9]{0:T(128)S(1)} %pad_add_fusion.1.place, s32[32]{0:T(128)S(1)} %get-tuple-element.45.index, bf16[2,320,128]{2,1,0:T(8,128)(2,1)S(1)} %collective-permute-done.19.refs_0_, bf16[2,320,128]{2,1,0:T(8,128)(2,1)S(1)} %collective-permute-done.23.refs_1_, ...), custom_call_target="tpu_custom_call", output_to_operand_aliasing={{}: (8, {})} | custom-call | flops 78888960 | bytes 458752 | tf_op jit(solution)/shard_map/cancel/pallas_call | solution.py:217
  (56 shorter events, 7.4 us)
Async XLA Ops:
  0.0 30.0 %copy-start.1 = (bf16[2,32,2048]{2,1,0:T(8,128)(2,1)S(1)}, bf16[2,32,2048]{2,1,0:T(8,128)(2,1)}, u32[]{:S(2)}) copy-start(bf16[2,32,2048]{2,1,0:T(8,128)(2,1)} %refs_0_.3) | copy-start | bytes 786436
  0.0 38.5 %copy-start = (bf16[2,2048,128]{2,1,0:T(8,128)(2,1)S(1)}, bf16[2,2048,128]{2,1,0:T(8,128)(2,1)}, u32[]{:S(2)}) copy-start(bf16[2,2048,128]{2,1,0:T(8,128)(2,1)} %refs_16_.1) | copy-start | bytes 3145732
  0.0 16.9 %collective-permute-start.4 = (bf16[2,32,2048]{2,1,0:T(8,128)(2,1)}, bf16[2,32,2048]{2,1,0:T(8,128)(2,1)S(1)}, u32[]{:S(2)}, u32[]{:S(2)}) collective-permute-start(bf16[2,32,2048]{2,1,0:T(8,128)(2,1)} %refs_0_.3), channel_id=1, source_target_pairs={{0,16},{1,17},{2,18},{3,19},{4,20},{5,21},{6,22},{7,23},{8,24},{9,... | collective-permute-start | bytes 786440 | tf_op jit(solution)/shard_map/ppermute | solution.py:253
  3.0 13.9 %collective-permute-start.2 = (bf16[2,32,2048]{2,1,0:T(8,128)(2,1)}, bf16[2,32,2048]{2,1,0:T(8,128)(2,1)S(1)}, u32[]{:S(2)}, u32[]{:S(2)}) collective-permute-start(bf16[2,32,2048]{2,1,0:T(8,128)(2,1)} %refs_0_.3), channel_id=1, source_target_pairs={{0,8},{1,9},{2,10},{3,11},{4,12},{5,13},{6,14},{7,15},{8,0},{9,1},... | collective-permute-start | bytes 786440 | tf_op jit(solution)/shard_map/ppermute | solution.py:253
  4.5 14.3 %collective-permute-start = (bf16[2,32,2048]{2,1,0:T(8,128)(2,1)}, bf16[2,32,2048]{2,1,0:T(8,128)(2,1)S(1)}, u32[]{:S(2)}, u32[]{:S(2)}) collective-permute-start(bf16[2,32,2048]{2,1,0:T(8,128)(2,1)} %refs_0_.3), channel_id=1, source_target_pairs={{0,4},{1,5},{2,6},{3,7},{4,0},{5,1},{6,2},{7,3},{8,12},{9,13},{10,... | collective-permute-start | bytes 786440 | tf_op jit(solution)/shard_map/ppermute | solution.py:253
  7.9 31.9 %collective-permute-start.15 = (bf16[2,2048,128]{2,1,0:T(8,128)(2,1)}, bf16[2,2048,128]{2,1,0:T(8,128)(2,1)S(1)}, u32[]{:S(2)}, u32[]{:S(2)}) collective-permute-start(bf16[2,2048,128]{2,1,0:T(8,128)(2,1)} %refs_16_.1), channel_id=1, source_target_pairs={{0,2},{1,3},{2,0},{3,1},{4,6},{5,7},{6,4},{7,5},{8,10},{9,11},{10,... | collective-permute-start | bytes 3145736 | tf_op jit(solution)/shard_map/ppermute | solution.py:253
  16.9 9.3 %collective-permute-start.5 = (bf16[2,32,2048]{2,1,0:T(8,128)(2,1)S(1)}, bf16[2,32,2048]{2,1,0:T(8,128)(2,1)S(1)}, u32[]{:S(2)}, u32[]{:S(2)}) collective-permute-start(bf16[2,32,2048]{2,1,0:T(8,128)(2,1)S(1)} %collective-permute-done.2.refs_2_), channel_id=1, source_target_pairs={{0,16},{1,17},{2,18},{3,19},{4,20},{5,21},{6,22},{7,23},{8,24},{9,... | collective-permute-start | bytes 786440 | tf_op jit(solution)/shard_map/ppermute | solution.py:253
  18.8 10.7 %collective-permute-start.11 = (bf16[2,32,2048]{2,1,0:T(8,128)(2,1)S(1)}, bf16[2,32,2048]{2,1,0:T(8,128)(2,1)S(1)}, u32[]{:S(2)}, u32[]{:S(2)}) collective-permute-start(bf16[2,32,2048]{2,1,0:T(8,128)(2,1)S(1)} %collective-permute-done.refs_8_), channel_id=1, source_target_pairs={{0,16},{1,17},{2,18},{3,19},{4,20},{5,21},{6,22},{7,23},{8,24},{9,... | collective-permute-start | bytes 786440 | tf_op jit(solution)/shard_map/ppermute | solution.py:253
  19.6 10.0 %collective-permute-start.9 = (bf16[2,32,2048]{2,1,0:T(8,128)(2,1)S(1)}, bf16[2,32,2048]{2,1,0:T(8,128)(2,1)S(1)}, u32[]{:S(2)}, u32[]{:S(2)}) collective-permute-start(bf16[2,32,2048]{2,1,0:T(8,128)(2,1)S(1)} %collective-permute-done.refs_8_), channel_id=1, source_target_pairs={{0,8},{1,9},{2,10},{3,11},{4,12},{5,13},{6,14},{7,15},{8,0},{9,1},... | collective-permute-start | bytes 786440 | tf_op jit(solution)/shard_map/ppermute | solution.py:253
  26.2 3.8 %collective-permute-start.7 = (bf16[2,32,2048]{2,1,0:T(8,128)(2,1)S(1)}, bf16[2,32,2048]{2,1,0:T(8,128)(2,1)S(1)}, u32[]{:S(2)}, u32[]{:S(2)}) collective-permute-start(bf16[2,32,2048]{2,1,0:T(8,128)(2,1)S(1)} %collective-permute-done.refs_8_), channel_id=1, source_target_pairs={{0,1},{1,0},{2,3},{3,2},{4,5},{5,4},{6,7},{7,6},{8,9},{9,8},{10,11... | collective-permute-start | bytes 786440 | tf_op jit(solution)/shard_map/ppermute | solution.py:253
  29.5 6.4 %collective-permute-start.13 = (bf16[2,32,2048]{2,1,0:T(8,128)(2,1)S(1)}, bf16[2,32,2048]{2,1,0:T(8,128)(2,1)S(1)}, u32[]{:S(2)}, u32[]{:S(2)}) collective-permute-start(bf16[2,32,2048]{2,1,0:T(8,128)(2,1)S(1)} %collective-permute-done.11.refs_12_), channel_id=1, source_target_pairs={{0,8},{1,9},{2,10},{3,11},{4,12},{5,13},{6,14},{7,15},{8,0},{9,1},... | collective-permute-start | bytes 786440 | tf_op jit(solution)/shard_map/ppermute | solution.py:253
  30.0 5.8 %collective-permute-start.8 = (bf16[2,32,2048]{2,1,0:T(8,128)(2,1)S(1)}, bf16[2,32,2048]{2,1,0:T(8,128)(2,1)S(1)}, u32[]{:S(2)}, u32[]{:S(2)}) collective-permute-start(bf16[2,32,2048]{2,1,0:T(8,128)(2,1)S(1)} %collective-permute-done.5.refs_6_), channel_id=1, source_target_pairs={{0,1},{1,0},{2,3},{3,2},{4,5},{5,4},{6,7},{7,6},{8,9},{9,8},{10,11... | collective-permute-start | bytes 786440 | tf_op jit(solution)/shard_map/ppermute | solution.py:253
  30.1 6.3 %collective-permute-start.1 = (bf16[2,32,2048]{2,1,0:T(8,128)(2,1)S(1)}, bf16[2,32,2048]{2,1,0:T(8,128)(2,1)S(1)}, u32[]{:S(2)}, u32[]{:S(2)}) collective-permute-start(bf16[2,32,2048]{2,1,0:T(8,128)(2,1)S(1)} %copy-done.1), channel_id=1, source_target_pairs={{0,1},{1,0},{2,3},{3,2},{4,5},{5,4},{6,7},{7,6},{8,9},{9,8},{10,11... | collective-permute-start | bytes 786440 | tf_op jit(solution)/shard_map/ppermute | solution.py:253
  30.6 5.9 %collective-permute-start.3 = (bf16[2,32,2048]{2,1,0:T(8,128)(2,1)S(1)}, bf16[2,32,2048]{2,1,0:T(8,128)(2,1)S(1)}, u32[]{:S(2)}, u32[]{:S(2)}) collective-permute-start(bf16[2,32,2048]{2,1,0:T(8,128)(2,1)S(1)} %collective-permute-done.2.refs_2_), channel_id=1, source_target_pairs={{0,1},{1,0},{2,3},{3,2},{4,5},{5,4},{6,7},{7,6},{8,9},{9,8},{10,11... | collective-permute-start | bytes 786440 | tf_op jit(solution)/shard_map/ppermute | solution.py:253
  35.9 1.5 %collective-permute-start.6 = (bf16[2,32,2048]{2,1,0:T(8,128)(2,1)S(1)}, bf16[2,32,2048]{2,1,0:T(8,128)(2,1)S(1)}, u32[]{:S(2)}, u32[]{:S(2)}) collective-permute-start(bf16[2,32,2048]{2,1,0:T(8,128)(2,1)S(1)} %collective-permute-done.4.refs_4_), channel_id=1, source_target_pairs={{0,1},{1,0},{2,3},{3,2},{4,5},{5,4},{6,7},{7,6},{8,9},{9,8},{10,11... | collective-permute-start | bytes 786440 | tf_op jit(solution)/shard_map/ppermute | solution.py:253
  35.9 1.9 %collective-permute-start.14 = (bf16[2,32,2048]{2,1,0:T(8,128)(2,1)S(1)}, bf16[2,32,2048]{2,1,0:T(8,128)(2,1)S(1)}, u32[]{:S(2)}, u32[]{:S(2)}) collective-permute-start(bf16[2,32,2048]{2,1,0:T(8,128)(2,1)S(1)} %collective-permute-done.13.refs_14_), channel_id=1, source_target_pairs={{0,1},{1,0},{2,3},{3,2},{4,5},{5,4},{6,7},{7,6},{8,9},{9,8},{10,11... | collective-permute-start | bytes 786440 | tf_op jit(solution)/shard_map/ppermute | solution.py:253
  36.4 1.8 %collective-permute-start.12 = (bf16[2,32,2048]{2,1,0:T(8,128)(2,1)S(1)}, bf16[2,32,2048]{2,1,0:T(8,128)(2,1)S(1)}, u32[]{:S(2)}, u32[]{:S(2)}) collective-permute-start(bf16[2,32,2048]{2,1,0:T(8,128)(2,1)S(1)} %collective-permute-done.11.refs_12_), channel_id=1, source_target_pairs={{0,1},{1,0},{2,3},{3,2},{4,5},{5,4},{6,7},{7,6},{8,9},{9,8},{10,11... | collective-permute-start | bytes 786440 | tf_op jit(solution)/shard_map/ppermute | solution.py:253
  36.5 2.1 %collective-permute-start.10 = (bf16[2,32,2048]{2,1,0:T(8,128)(2,1)S(1)}, bf16[2,32,2048]{2,1,0:T(8,128)(2,1)S(1)}, u32[]{:S(2)}, u32[]{:S(2)}) collective-permute-start(bf16[2,32,2048]{2,1,0:T(8,128)(2,1)S(1)} %collective-permute-done.9.refs_10_), channel_id=1, source_target_pairs={{0,1},{1,0},{2,3},{3,2},{4,5},{5,4},{6,7},{7,6},{8,9},{9,8},{10,11... | collective-permute-start | bytes 786440 | tf_op jit(solution)/shard_map/ppermute | solution.py:253
  39.8 1.8 %copy-start.2 = (s32[16]{0:T(128)S(1)}, s32[16]{0:T(128)}, u32[]{:S(2)}) copy-start(s32[16]{0:T(128)} %labels.1) | copy-start | bytes 196
  41.1 11.8 %copy-start.3 = (s32[8]{0:T(128)S(1)}, s32[8]{0:T(128)}, u32[]{:S(2)}) copy-start(s32[8]{0:T(128)} %constant.52.clone) | copy-start | bytes 100
  41.1 8.4 %collective-permute-start.16 = (bf16[2,512,128]{2,1,0:T(8,128)(2,1)S(1)}, bf16[2,512,128]{2,1,0:T(8,128)(2,1)S(1)}, u32[]{:S(2)}, u32[]{:S(2)}) collective-permute-start(bf16[2,512,128]{2,1,0:T(8,128)(2,1)S(1)} %form_beams.3), channel_id=1, source_target_pairs={{0,2},{1,3},{2,0},{3,1},{4,6},{5,7},{6,4},{7,5},{8,10},{9,11},{10,... | collective-permute-start | bytes 786440 | tf_op jit(solution)/shard_map/ppermute | solution.py:253
  50.4 9.8 %collective-permute-start.17 = (bf16[2,320,128]{2,1,0:T(8,128)(2,1)S(1)}, bf16[2,320,128]{2,1,0:T(8,128)(2,1)S(1)}, u32[]{:S(2)}, u32[]{:S(2)}) collective-permute-start(bf16[2,320,128]{2,1,0:T(8,128)(2,1)S(1)} %get-tuple-element.52), channel_id=1, source_target_pairs={{0,4},{1,5},{2,6},{3,7},{4,0},{5,1},{6,2},{7,3},{8,12},{9,13},{10,... | collective-permute-start | bytes 491528 | tf_op jit(solution)/shard_map/ppermute | solution.py:253
  51.1 7.6 %collective-permute-start.20 = (bf16[2,320,128]{2,1,0:T(8,128)(2,1)S(1)}, bf16[2,320,128]{2,1,0:T(8,128)(2,1)S(1)}, u32[]{:S(2)}, u32[]{:S(2)}) collective-permute-start(bf16[2,320,128]{2,1,0:T(8,128)(2,1)S(1)} %get-tuple-element.56), channel_id=1, source_target_pairs={{0,2},{1,3},{2,0},{3,1},{4,6},{5,7},{6,4},{7,5},{8,10},{9,11},{10,... | collective-permute-start | bytes 491528 | tf_op jit(solution)/shard_map/ppermute | solution.py:253
  52.9 1.4 %collective-permute-start.18 = (bf16[2,320,128]{2,1,0:T(8,128)(2,1)S(1)}, bf16[2,320,128]{2,1,0:T(8,128)(2,1)S(1)}, u32[]{:S(2)}, u32[]{:S(2)}) collective-permute-start(bf16[2,320,128]{2,1,0:T(8,128)(2,1)S(1)} %get-tuple-element.53.refs_0_), channel_id=1, source_target_pairs={{0,1},{1,0},{2,3},{3,2},{4,5},{5,4},{6,7},{7,6},{8,9},{9,8},{10,11... | collective-permute-start | bytes 491528 | tf_op jit(solution)/shard_map/ppermute | solution.py:253
  60.2 7.0 %collective-permute-start.22 = (bf16[2,320,128]{2,1,0:T(8,128)(2,1)S(1)}, bf16[2,320,128]{2,1,0:T(8,128)(2,1)S(1)}, u32[]{:S(2)}, u32[]{:S(2)}) collective-permute-start(bf16[2,320,128]{2,1,0:T(8,128)(2,1)S(1)} %collective-permute-done.17.refs_1_), channel_id=1, source_target_pairs={{0,1},{1,0},{2,3},{3,2},{4,5},{5,4},{6,7},{7,6},{8,9},{9,8},{10,11... | collective-permute-start | bytes 491528 | tf_op jit(solution)/shard_map/ppermute | solution.py:253
  60.2 7.0 %collective-permute-start.21 = (bf16[2,320,128]{2,1,0:T(8,128)(2,1)S(1)}, bf16[2,320,128]{2,1,0:T(8,128)(2,1)S(1)}, u32[]{:S(2)}, u32[]{:S(2)}) collective-permute-start(bf16[2,320,128]{2,1,0:T(8,128)(2,1)S(1)} %collective-permute-done.20.refs_0_), channel_id=1, source_target_pairs={{0,1},{1,0},{2,3},{3,2},{4,5},{5,4},{6,7},{7,6},{8,9},{9,8},{10,11... | collective-permute-start | bytes 491528 | tf_op jit(solution)/shard_map/ppermute | solution.py:253
  60.7 11.0 %collective-permute-start.19 = (bf16[2,320,128]{2,1,0:T(8,128)(2,1)S(1)}, bf16[2,320,128]{2,1,0:T(8,128)(2,1)S(1)}, u32[]{:S(2)}, u32[]{:S(2)}) collective-permute-start(bf16[2,320,128]{2,1,0:T(8,128)(2,1)S(1)} %get-tuple-element.55), channel_id=1, source_target_pairs={{0,6},{1,7},{2,4},{3,5},{4,2},{5,3},{6,0},{7,1},{8,14},{9,15},{10,... | collective-permute-start | bytes 491528 | tf_op jit(solution)/shard_map/ppermute | solution.py:253
  71.7 1.5 %collective-permute-start.23 = (bf16[2,320,128]{2,1,0:T(8,128)(2,1)S(1)}, bf16[2,320,128]{2,1,0:T(8,128)(2,1)S(1)}, u32[]{:S(2)}, u32[]{:S(2)}) collective-permute-start(bf16[2,320,128]{2,1,0:T(8,128)(2,1)S(1)} %collective-permute-done.19.refs_0_), channel_id=1, source_target_pairs={{0,1},{1,0},{2,3},{3,2},{4,5},{5,4},{6,7},{7,6},{8,9},{9,8},{10,11... | collective-permute-start | bytes 491528 | tf_op jit(solution)/shard_map/ppermute | solution.py:253

commit v7 on v6

--- a/solution.py
+++ b/solution.py
@@ -288,8 +288,9 @@
     w_xyzc = swap(w_xyz, core=1)
     pieces = [w, w_c, w_x, w_xc, w_y, w_yc, w_xy, w_xyc]
     pieces += [w_z, w_zc, w_xz, w_xzc, w_yz, w_yzc, w_xyz, w_xyzc]
-    mine = form_beams(pieces, element_signals)
-    other = form_beams(pieces, after(far, mine))
+    early = form_beams(pieces[:8], far)
+    mine = form_beams(pieces, after(element_signals, early))
+    other = [early, form_beams(pieces[8:], after(far, mine))]
     return mine, other
 
 
@@ -393,8 +394,8 @@
     mine, other = all_beams(places, element_signals, beam_weights, (select, taken, sides))
     beams = [mine]
     if other is not None:
-        beams.append(places.swap(other, z=1))
-        taken = after(taken, other)
+        beams += [places.swap(part, z=1) for part in other]
+        taken = after(taken, other[1])
     index, coefs, first, second, scale = tables(bit_labels, taken, sides, slots, tile)
     select = after(select, first, second, scale, coefs)
     ordered = list(order_beams(select, beams))

time: 78.1 us -> 75.2 us (0.963)
  waiting for transfers between devices: 27.1 us -> 22.8 us
  starting transfers between devices: 18.2 us -> 21.3 us
  local copies, waits for them, and re-layouts: 5.95 us -> 4.11 us
    ppermute x24 -> x25, waiting for transfers between devices: 27.1 us -> 22.8 us  [swap(): return lax.ppermute(value, ('tm', 'beam'), pairs)]
    ppermute x24 -> x25, starting transfers between devices: 18.2 us -> 21.3 us  [swap(): return lax.ppermute(value, ('tm', 'beam'), pairs)]
    gather x1, local copies, waits for them, and re-layouts: 1.73 us -> 0.69 us  [on_device(): taken = jnp.take(table, own[:rows], axis=0, mode='clip')]
    concatenate x1, local copies, waits for them, and re-layouts: 1.02 us -> 0.21 us  [on_device(): jnp.concatenate([neighbours.astype(jnp.float32), leakage[0].astype(jnp.fl...]
    pallas_call x2 -> x3, Pallas kernels: 2.51 us -> 2.7 us  [form_beams(): pl.pallas_call(functools.partial(beams_kernel, pieces), in_specs=[whole]...]
  transfers between devices with their start and end apart: 24 -> 25, of which waited for: 12 -> 10; matrix products, arithmetic and copies ran while one was open for 11% -> 9% of each run, Pallas kernels for 22% -> 24%
where the time goes in v7:
time: 75.2 us; the launch traced here: 74.9 us
  Pallas kernels  23.6 us (31%)
  waiting for transfers between devices  22.8 us (30%)
  starting transfers between devices  21.3 us (28%)
  local copies, waits for them, and re-layouts  4.11 us (5%)
  other arithmetic  2.82 us (4%)
    ppermute x25, waiting for transfers between devices, swap(): return lax.ppermute(value, ('tm', 'beam'), pairs)  22.8 us
    ppermute x25, starting transfers between devices, swap(): return lax.ppermute(value, ('tm', 'beam'), pairs)  21.3 us
    pallas_call x4, Pallas kernels, cancel(): pl.pallas_call(functools.partial(cancel_kernel, (blocks, rows, inner, til...  18 us
    pallas_call x3, Pallas kernels, form_beams(): pl.pallas_call(functools.partial(beams_kernel, pieces), in_specs=[whole]...  2.7 us
    pallas_call x1, Pallas kernels, tables(): pl.pallas_call(functools.partial(tables_kernel, (slots, rows, inner, tile...  2 us
  transfers between devices with their start and end apart: 25, of which 10 were waited for; matrix products, arithmetic and copies ran while one was open for 9% of the time, Pallas kernels for 24%

profile of v7, /device:TPU:0, one launch (start us, length us, event | category | flops | bytes accessed | tf_op | source)
XLA Modules:
  0.0 74.9 jit_solution(13897015824319491309)
XLA Ops:
  0.0 3.0 %collective-permute-start.2 = (bf16[2,32,2048]{2,1,0:T(8,128)(2,1)}, bf16[2,32,2048]{2,1,0:T(8,128)(2,1)S(1)}, u32[]{:S(2)}, u32[]{:S(2)}) collective-permute-start(bf16[2,32,2048]{2,1,0:T(8,128)(2,1)} %refs_0_.3), channel_id=1, source_target_pairs={{0,16},{1,17},{2,18},{3,19},{4,20},{5,21},{6,22},{7,23},{8,24},{9,... | collective-permute-start | bytes 786440 | tf_op jit(solution)/shard_map/ppermute | solution.py:253
  3.0 1.5 %collective-permute-start.1 = (bf16[2,32,2048]{2,1,0:T(8,128)(2,1)}, bf16[2,32,2048]{2,1,0:T(8,128)(2,1)S(1)}, u32[]{:S(2)}, u32[]{:S(2)}) collective-permute-start(bf16[2,32,2048]{2,1,0:T(8,128)(2,1)} %refs_0_.3), channel_id=1, source_target_pairs={{0,8},{1,9},{2,10},{3,11},{4,12},{5,13},{6,14},{7,15},{8,0},{9,1},... | collective-permute-start | bytes 786440 | tf_op jit(solution)/shard_map/ppermute | solution.py:253
  4.5 2.6 %collective-permute-start = (bf16[2,32,2048]{2,1,0:T(8,128)(2,1)}, bf16[2,32,2048]{2,1,0:T(8,128)(2,1)S(1)}, u32[]{:S(2)}, u32[]{:S(2)}) collective-permute-start(bf16[2,32,2048]{2,1,0:T(8,128)(2,1)} %refs_0_.3), channel_id=1, source_target_pairs={{0,4},{1,5},{2,6},{3,7},{4,0},{5,1},{6,2},{7,3},{8,12},{9,13},{10,... | collective-permute-start | bytes 786440 | tf_op jit(solution)/shard_map/ppermute | solution.py:253
  7.1 0.8 %pad_dynamic-slice_fusion = s32[272]{0:T(512)S(1)} fusion(s32[]{:T(128)S(6)} %select_n.18, s32[1024]{0:T(1024)} %param.12), kind=kLoop, calls=%fused_computation.11 | loop fusion | bytes 5188 | tf_op jit(solution)/shard_map/dynamic_slice | solution.py:375
  7.9 1.6 %collective-permute-start.12 = (bf16[2,2048,128]{2,1,0:T(8,128)(2,1)}, bf16[2,2048,128]{2,1,0:T(8,128)(2,1)S(1)}, u32[]{:S(2)}, u32[]{:S(2)}) collective-permute-start(bf16[2,2048,128]{2,1,0:T(8,128)(2,1)} %refs_16_), channel_id=1, source_target_pairs={{0,2},{1,3},{2,0},{3,1},{4,6},{5,7},{6,4},{7,5},{8,10},{9,11},{10,... | collective-permute-start | bytes 3145736 | tf_op jit(solution)/shard_map/ppermute | solution.py:253
  9.5 0.8 %pad_slice_fusion.1 = (s32[1024]{0:T(1024)S(1)}, s32[1024]{0:T(1024)S(1)}) fusion(s32[1024]{0:T(1024)} %param.12), kind=kLoop, calls=%fused_computation.10 | loop fusion | bytes 12288 | tf_op jit(solution)/shard_map/slice | solution.py:373
  11.1 0.8 %convert_element_type.21 = f32[1024,6]{0,1:T(8,128)S(1)} convert(s32[1024,6]{0,1:T(8,128)} %param.13) | non-fusion elementwise | flops 6144 | bytes 49152 | tf_op jit(solution)/shard_map/convert_element_type | solution.py:379
  11.8 0.9 %fusion.2 = (bf16[1,1024,6]{1,0,2:T(2,128)(2,1)S(1)}, bf16[1,1024,6]{1,0,2:T(2,128)(2,1)S(1)}) fusion(bf16[2,1024,6]{1,0,2:T(2,128)(2,1)} %param.14), kind=kLoop, calls=%fused_computation.20 | loop fusion | bytes 49152 | tf_op jit(solution)/shard_map/slice | solution.py:380
  12.7 0.7 pad_maximum_fusion
  16.1 2.7 %collective-permute-done.refs_8_.refs_0_ = bf16[2,32,2048]{2,1,0:T(8,128)(2,1)S(1)} collective-permute-done((bf16[2,32,2048]{2,1,0:T(8,128)(2,1)}, bf16[2,32,2048]{2,1,0:T(8,128)(2,1)S(1)}, u32[]{:S(2)}, u32[]{:S(2)}) %collective-permute-start) | collective-permute-done | bytes 262176 | tf_op jit(solution)/shard_map/ppermute | solution.py:253
  19.8 4.0 %collective-permute-done.3.refs_6_ = bf16[2,32,2048]{2,1,0:T(8,128)(2,1)S(1)} collective-permute-done((bf16[2,32,2048]{2,1,0:T(8,128)(2,1)S(1)}, bf16[2,32,2048]{2,1,0:T(8,128)(2,1)S(1)}, u32[]{:S(2)}, u32[]{:S(2)}) %collective-permute-start.3) | collective-permute-done | bytes 262176 | tf_op jit(solution)/shard_map/ppermute | solution.py:253
  23.8 3.9 %collective-permute-done.8.refs_12_.refs_4_ = bf16[2,32,2048]{2,1,0:T(8,128)(2,1)S(1)} collective-permute-done((bf16[2,32,2048]{2,1,0:T(8,128)(2,1)S(1)}, bf16[2,32,2048]{2,1,0:T(8,128)(2,1)S(1)}, u32[]{:S(2)}, u32[]{:S(2)}) %collective-permute-start.8) | collective-permute-done | bytes 262176 | tf_op jit(solution)/shard_map/ppermute | solution.py:253
  28.8 5.5 %collective-permute-done.10.refs_14_.refs_6_ = bf16[2,32,2048]{2,1,0:T(8,128)(2,1)S(1)} collective-permute-done((bf16[2,32,2048]{2,1,0:T(8,128)(2,1)S(1)}, bf16[2,32,2048]{2,1,0:T(8,128)(2,1)S(1)}, u32[]{:S(2)}, u32[]{:S(2)}) %collective-permute-start.10) | collective-permute-done | bytes 262176 | tf_op jit(solution)/shard_map/ppermute | solution.py:253
  35.8 0.9 %collective-permute-done.12.refs_8_ = bf16[2,2048,128]{2,1,0:T(8,128)(2,1)S(1)} collective-permute-done((bf16[2,2048,128]{2,1,0:T(8,128)(2,1)}, bf16[2,2048,128]{2,1,0:T(8,128)(2,1)S(1)}, u32[]{:S(2)}, u32[]{:S(2)}) %collective-permute-start.12) | collective-permute-done | bytes 1048608 | tf_op jit(solution)/shard_map/ppermute | solution.py:253
  36.7 0.7 form_beams.3
  37.4 0.9 %collective-permute-start.16 = (bf16[2,256,128]{2,1,0:T(8,128)(2,1)S(1)}, bf16[2,256,128]{2,1,0:T(8,128)(2,1)S(1)}, u32[]{:S(2)}, u32[]{:S(2)}) collective-permute-start(bf16[2,256,128]{2,1,0:T(8,128)(2,1)S(1)} %form_beams.3), channel_id=1, source_target_pairs={{0,2},{1,3},{2,0},{3,1},{4,6},{5,7},{6,4},{7,5},{8,10},{9,11},{10,... | collective-permute-start | bytes 393224 | tf_op jit(solution)/shard_map/ppermute | solution.py:253
  38.3 1.3 %form_beams.4.refs_1_ = bf16[2,512,128]{2,1,0:T(8,128)(2,1)S(1)} custom-call(bf16[2,32,2048]{2,1,0:T(8,128)(2,1)S(1)} %copy-done.1, bf16[2,32,2048]{2,1,0:T(8,128)(2,1)S(1)} %collective-permute-done.13.refs_1_, bf16[2,32,2048]{2,1,0:T(8,128)(2,1)S(1)} %collective-permute-done.1.refs_2_, bf16[2,32,2048]{2,1,0:T(8,128)(2,1)S(1)} %collective-permute-done.14.refs_3_, ...), custom_call_target="tpu_custom_call" | custom-call | flops 1073741824 | bytes 5242880 | tf_op jit(solution)/shard_map/form_beams/pallas_call | solution.py:46
  39.6 0.7 form_beams.5
  40.3 1.3 %collective-permute-start.17 = (bf16[2,256,128]{2,1,0:T(8,128)(2,1)S(1)}, bf16[2,256,128]{2,1,0:T(8,128)(2,1)S(1)}, u32[]{:S(2)}, u32[]{:S(2)}) collective-permute-start(bf16[2,256,128]{2,1,0:T(8,128)(2,1)S(1)} %form_beams.5), channel_id=1, source_target_pairs={{0,2},{1,3},{2,0},{3,1},{4,6},{5,7},{6,4},{7,5},{8,10},{9,11},{10,... | collective-permute-start | bytes 393224 | tf_op jit(solution)/shard_map/ppermute | solution.py:253
  41.6 2.0 %tables.1 = (s32[32]{0:T(128)S(1)}, f32[32,8,128]{2,1,0:T(8,128)S(1)}, bf16[320,512]{1,0:T(8,128)(2,1)S(1)}, bf16[256,512]{1,0:T(8,128)(2,1)S(1)}, f32[2,192,128]{2,1,0:T(8,128)S(1)}) custom-call(s32[16]{0:T(128)S(1)} %copy-done.2, f32[192,19]{1,0:T(8,128)S(1)} %gather_fusion, f32[2,256]{1,0:T(2,128)S(1)} %add_convert_fusion.own), custom_call_target="tpu_custom_call" | custom-call | flops 2949120 | bytes 786432 | tf_op jit(solution)/shard_map/tables/pallas_call | solution.py:344
  43.6 2.0 %collective-permute-done.17.refs_3_ = bf16[2,256,128]{2,1,0:T(8,128)(2,1)S(1)} collective-permute-done((bf16[2,256,128]{2,1,0:T(8,128)(2,1)S(1)}, bf16[2,256,128]{2,1,0:T(8,128)(2,1)S(1)}, u32[]{:S(2)}, u32[]{:S(2)}) %collective-permute-start.17) | collective-permute-done | bytes 131104 | tf_op jit(solution)/shard_map/ppermute | solution.py:253
  45.6 0.9 %order_beams.1 = (bf16[2,320,128]{2,1,0:T(8,128)(2,1)S(1)}, bf16[2,320,128]{2,1,0:T(8,128)(2,1)S(1)}, bf16[2,320,128]{2,1,0:T(8,128)(2,1)S(1)}, bf16[2,320,128]{2,1,0:T(8,128)(2,1)S(1)}) custom-call(bf16[4,320,1024]{2,1,0:T(8,128)(2,1)S(1)} %compare_convert_fusion.refs_0_, bf16[2,512,128]{2,1,0:T(8,128)(2,1)S(1)} %form_beams.4.refs_1_, ...), custom_call_target="tpu_custom_call" | custom-call | flops 671088640 | bytes 3276800 | tf_op jit(solution)/shard_map/order_beams/pallas_call | solution.py:78
  46.5 2.5 %collective-permute-start.18 = (bf16[2,320,128]{2,1,0:T(8,128)(2,1)S(1)}, bf16[2,320,128]{2,1,0:T(8,128)(2,1)S(1)}, u32[]{:S(2)}, u32[]{:S(2)}) collective-permute-start(bf16[2,320,128]{2,1,0:T(8,128)(2,1)S(1)} %get-tuple-element.54), channel_id=1, source_target_pairs={{0,4},{1,5},{2,6},{3,7},{4,0},{5,1},{6,2},{7,3},{8,12},{9,13},{10,... | collective-permute-start | bytes 491528 | tf_op jit(solution)/shard_map/ppermute | solution.py:253
  48.9 1.0 %collective-permute-start.21 = (bf16[2,320,128]{2,1,0:T(8,128)(2,1)S(1)}, bf16[2,320,128]{2,1,0:T(8,128)(2,1)S(1)}, u32[]{:S(2)}, u32[]{:S(2)}) collective-permute-start(bf16[2,320,128]{2,1,0:T(8,128)(2,1)S(1)} %get-tuple-element.58), channel_id=1, source_target_pairs={{0,2},{1,3},{2,0},{3,1},{4,6},{5,7},{6,4},{7,5},{8,10},{9,11},{10,... | collective-permute-start | bytes 491528 | tf_op jit(solution)/shard_map/ppermute | solution.py:253
  50.0 1.3 %collective-permute-done.19.refs_1_ = bf16[2,320,128]{2,1,0:T(8,128)(2,1)S(1)} collective-permute-done((bf16[2,320,128]{2,1,0:T(8,128)(2,1)S(1)}, bf16[2,320,128]{2,1,0:T(8,128)(2,1)S(1)}, u32[]{:S(2)}, u32[]{:S(2)}) %collective-permute-start.19) | collective-permute-done | bytes 163872 | tf_op jit(solution)/shard_map/ppermute | solution.py:253
  51.3 4.5 %cancel.4.refs_6_ = bf16[4,128,1024]{2,1,0:T(8,128)(2,1)} custom-call(s32[9]{0:T(128)S(1)} %pad_add_fusion.1.place, s32[32]{0:T(128)S(1)} %get-tuple-element.47.index, bf16[2,320,128]{2,1,0:T(8,128)(2,1)S(1)} %get-tuple-element.55.refs_0_, bf16[2,320,128]{2,1,0:T(8,128)(2,1)S(1)} %collective-permute-done.19.refs_1_, ...), custom_call_target="tpu_custom_call" | custom-call | flops 78888960 | bytes 458752 | tf_op jit(solution)/shard_map/cancel/pallas_call | solution.py:217
  55.8 0.7 collective-permute-done.21.refs_0_
  57.1 2.8 %collective-permute-start.20 = (bf16[2,320,128]{2,1,0:T(8,128)(2,1)S(1)}, bf16[2,320,128]{2,1,0:T(8,128)(2,1)S(1)}, u32[]{:S(2)}, u32[]{:S(2)}) collective-permute-start(bf16[2,320,128]{2,1,0:T(8,128)(2,1)S(1)} %get-tuple-element.57), channel_id=1, source_target_pairs={{0,6},{1,7},{2,4},{3,5},{4,2},{5,3},{6,0},{7,1},{8,14},{9,15},{10,... | collective-permute-start | bytes 491528 | tf_op jit(solution)/shard_map/ppermute | solution.py:253
  59.8 4.5 %cancel.5.refs_6_ = bf16[4,128,1024]{2,1,0:T(8,128)(2,1)} custom-call(s32[9]{0:T(128)S(1)} %pad_add_fusion.1.place, s32[32]{0:T(128)S(1)} %get-tuple-element.47.index, bf16[2,320,128]{2,1,0:T(8,128)(2,1)S(1)} %collective-permute-done.21.refs_0_, bf16[2,320,128]{2,1,0:T(8,128)(2,1)S(1)} %collective-permute-done.18.refs_1_, ...), custom_call_target="tpu_custom_call", output_to_operand_aliasing={{}: (8, {})} | custom-call | flops 78888960 | bytes 458752 | tf_op jit(solution)/shard_map/cancel/pallas_call | solution.py:217
  64.4 4.5 %cancel.6.refs_6_ = bf16[4,128,1024]{2,1,0:T(8,128)(2,1)} custom-call(s32[9]{0:T(128)S(1)} %pad_add_fusion.1.place, s32[32]{0:T(128)S(1)} %get-tuple-element.47.index, bf16[2,320,128]{2,1,0:T(8,128)(2,1)S(1)} %collective-permute-done.22.refs_0_, bf16[2,320,128]{2,1,0:T(8,128)(2,1)S(1)} %collective-permute-done.23.refs_1_, ...), custom_call_target="tpu_custom_call", output_to_operand_aliasing={{}: (8, {})} | custom-call | flops 78888960 | bytes 458752 | tf_op jit(solution)/shard_map/cancel/pallas_call | solution.py:217
  69.0 1.4 %collective-permute-done.24.refs_1_ = bf16[2,320,128]{2,1,0:T(8,128)(2,1)S(1)} collective-permute-done((bf16[2,320,128]{2,1,0:T(8,128)(2,1)S(1)}, bf16[2,320,128]{2,1,0:T(8,128)(2,1)S(1)}, u32[]{:S(2)}, u32[]{:S(2)}) %collective-permute-start.24) | collective-permute-done | bytes 163872 | tf_op jit(solution)/shard_map/ppermute | solution.py:253
  70.4 4.5 %cancel.7 = bf16[4,128,1024]{2,1,0:T(8,128)(2,1)} custom-call(s32[9]{0:T(128)S(1)} %pad_add_fusion.1.place, s32[32]{0:T(128)S(1)} %get-tuple-element.47.index, bf16[2,320,128]{2,1,0:T(8,128)(2,1)S(1)} %collective-permute-done.20.refs_0_, bf16[2,320,128]{2,1,0:T(8,128)(2,1)S(1)} %collective-permute-done.24.refs_1_, ...), custom_call_target="tpu_custom_call", output_to_operand_aliasing={{}: (8, {})} | custom-call | flops 78888960 | bytes 458752 | tf_op jit(solution)/shard_map/cancel/pallas_call | solution.py:217
  (59 shorter events, 7.8 us)
Async XLA Ops:
  0.0 28.2 %copy-start.1 = (bf16[2,32,2048]{2,1,0:T(8,128)(2,1)S(1)}, bf16[2,32,2048]{2,1,0:T(8,128)(2,1)}, u32[]{:S(2)}) copy-start(bf16[2,32,2048]{2,1,0:T(8,128)(2,1)} %refs_0_.3) | copy-start | bytes 786436
  0.0 15.1 %collective-permute-start.2 = (bf16[2,32,2048]{2,1,0:T(8,128)(2,1)}, bf16[2,32,2048]{2,1,0:T(8,128)(2,1)S(1)}, u32[]{:S(2)}, u32[]{:S(2)}) collective-permute-start(bf16[2,32,2048]{2,1,0:T(8,128)(2,1)} %refs_0_.3), channel_id=1, source_target_pairs={{0,16},{1,17},{2,18},{3,19},{4,20},{5,21},{6,22},{7,23},{8,24},{9,... | collective-permute-start | bytes 786440 | tf_op jit(solution)/shard_map/ppermute | solution.py:253
  3.0 12.1 %collective-permute-start.1 = (bf16[2,32,2048]{2,1,0:T(8,128)(2,1)}, bf16[2,32,2048]{2,1,0:T(8,128)(2,1)S(1)}, u32[]{:S(2)}, u32[]{:S(2)}) collective-permute-start(bf16[2,32,2048]{2,1,0:T(8,128)(2,1)} %refs_0_.3), channel_id=1, source_target_pairs={{0,8},{1,9},{2,10},{3,11},{4,12},{5,13},{6,14},{7,15},{8,0},{9,1},... | collective-permute-start | bytes 786440 | tf_op jit(solution)/shard_map/ppermute | solution.py:253
  4.5 14.3 %collective-permute-start = (bf16[2,32,2048]{2,1,0:T(8,128)(2,1)}, bf16[2,32,2048]{2,1,0:T(8,128)(2,1)S(1)}, u32[]{:S(2)}, u32[]{:S(2)}) collective-permute-start(bf16[2,32,2048]{2,1,0:T(8,128)(2,1)} %refs_0_.3), channel_id=1, source_target_pairs={{0,4},{1,5},{2,6},{3,7},{4,0},{5,1},{6,2},{7,3},{8,12},{9,13},{10,... | collective-permute-start | bytes 786440 | tf_op jit(solution)/shard_map/ppermute | solution.py:253
  7.9 28.8 %collective-permute-start.12 = (bf16[2,2048,128]{2,1,0:T(8,128)(2,1)}, bf16[2,2048,128]{2,1,0:T(8,128)(2,1)S(1)}, u32[]{:S(2)}, u32[]{:S(2)}) collective-permute-start(bf16[2,2048,128]{2,1,0:T(8,128)(2,1)} %refs_16_), channel_id=1, source_target_pairs={{0,2},{1,3},{2,0},{3,1},{4,6},{5,7},{6,4},{7,5},{8,10},{9,11},{10,... | collective-permute-start | bytes 3145736 | tf_op jit(solution)/shard_map/ppermute | solution.py:253
  15.0 23.2 %copy-start = (bf16[2,2048,128]{2,1,0:T(8,128)(2,1)S(1)}, bf16[2,2048,128]{2,1,0:T(8,128)(2,1)}, u32[]{:S(2)}) copy-start(bf16[2,2048,128]{2,1,0:T(8,128)(2,1)} %refs_16_) | copy-start | bytes 3145732
  15.1 8.7 %collective-permute-start.3 = (bf16[2,32,2048]{2,1,0:T(8,128)(2,1)S(1)}, bf16[2,32,2048]{2,1,0:T(8,128)(2,1)S(1)}, u32[]{:S(2)}, u32[]{:S(2)}) collective-permute-start(bf16[2,32,2048]{2,1,0:T(8,128)(2,1)S(1)} %collective-permute-done.1.refs_2_), channel_id=1, source_target_pairs={{0,16},{1,17},{2,18},{3,19},{4,20},{5,21},{6,22},{7,23},{8,24},{9,... | collective-permute-start | bytes 786440 | tf_op jit(solution)/shard_map/ppermute | solution.py:253
  18.8 8.9 %collective-permute-start.8 = (bf16[2,32,2048]{2,1,0:T(8,128)(2,1)S(1)}, bf16[2,32,2048]{2,1,0:T(8,128)(2,1)S(1)}, u32[]{:S(2)}, u32[]{:S(2)}) collective-permute-start(bf16[2,32,2048]{2,1,0:T(8,128)(2,1)S(1)} %collective-permute-done.refs_8_.refs_0_), channel_id=1, source_target_pairs={{0,16},{1,17},{2,18},{3,19},{4,20},{5,21},{6,22},{7,23},{8,24},{9,... | collective-permute-start | bytes 786440 | tf_op jit(solution)/shard_map/ppermute | solution.py:253
  19.3 8.4 %collective-permute-start.5 = (bf16[2,32,2048]{2,1,0:T(8,128)(2,1)S(1)}, bf16[2,32,2048]{2,1,0:T(8,128)(2,1)S(1)}, u32[]{:S(2)}, u32[]{:S(2)}) collective-permute-start(bf16[2,32,2048]{2,1,0:T(8,128)(2,1)S(1)} %collective-permute-done.refs_8_.refs_0_), channel_id=1, source_target_pairs={{0,8},{1,9},{2,10},{3,11},{4,12},{5,13},{6,14},{7,15},{8,0},{9,1},... | collective-permute-start | bytes 786440 | tf_op jit(solution)/shard_map/ppermute | solution.py:253
  23.8 4.4 %collective-permute-start.4 = (bf16[2,32,2048]{2,1,0:T(8,128)(2,1)S(1)}, bf16[2,32,2048]{2,1,0:T(8,128)(2,1)S(1)}, u32[]{:S(2)}, u32[]{:S(2)}) collective-permute-start(bf16[2,32,2048]{2,1,0:T(8,128)(2,1)S(1)} %collective-permute-done.refs_8_.refs_0_), channel_id=1, source_target_pairs={{0,1},{1,0},{2,3},{3,2},{4,5},{5,4},{6,7},{7,6},{8,9},{9,8},{10,11... | collective-permute-start | bytes 786440 | tf_op jit(solution)/shard_map/ppermute | solution.py:253
  27.7 6.6 %collective-permute-start.10 = (bf16[2,32,2048]{2,1,0:T(8,128)(2,1)S(1)}, bf16[2,32,2048]{2,1,0:T(8,128)(2,1)S(1)}, u32[]{:S(2)}, u32[]{:S(2)}) collective-permute-start(bf16[2,32,2048]{2,1,0:T(8,128)(2,1)S(1)} %collective-permute-done.8.refs_12_.refs_4_), channel_id=1, source_target_pairs={{0,8},{1,9},{2,10},{3,11},{4,12},{5,13},{6,14},{7,15},{8,0},{9,1},... | collective-permute-start | bytes 786440 | tf_op jit(solution)/shard_map/ppermute | solution.py:253
  28.2 6.1 %collective-permute-start.6 = (bf16[2,32,2048]{2,1,0:T(8,128)(2,1)S(1)}, bf16[2,32,2048]{2,1,0:T(8,128)(2,1)S(1)}, u32[]{:S(2)}, u32[]{:S(2)}) collective-permute-start(bf16[2,32,2048]{2,1,0:T(8,128)(2,1)S(1)} %collective-permute-done.3.refs_6_), channel_id=1, source_target_pairs={{0,1},{1,0},{2,3},{3,2},{4,5},{5,4},{6,7},{7,6},{8,9},{9,8},{10,11... | collective-permute-start | bytes 786440 | tf_op jit(solution)/shard_map/ppermute | solution.py:253
  28.2 6.6 %collective-permute-start.13 = (bf16[2,32,2048]{2,1,0:T(8,128)(2,1)S(1)}, bf16[2,32,2048]{2,1,0:T(8,128)(2,1)S(1)}, u32[]{:S(2)}, u32[]{:S(2)}) collective-permute-start(bf16[2,32,2048]{2,1,0:T(8,128)(2,1)S(1)} %copy-done.1), channel_id=1, source_target_pairs={{0,1},{1,0},{2,3},{3,2},{4,5},{5,4},{6,7},{7,6},{8,9},{9,8},{10,11... | collective-permute-start | bytes 786440 | tf_op jit(solution)/shard_map/ppermute | solution.py:253
  28.7 6.1 %collective-permute-start.14 = (bf16[2,32,2048]{2,1,0:T(8,128)(2,1)S(1)}, bf16[2,32,2048]{2,1,0:T(8,128)(2,1)S(1)}, u32[]{:S(2)}, u32[]{:S(2)}) collective-permute-start(bf16[2,32,2048]{2,1,0:T(8,128)(2,1)S(1)} %collective-permute-done.1.refs_2_), channel_id=1, source_target_pairs={{0,1},{1,0},{2,3},{3,2},{4,5},{5,4},{6,7},{7,6},{8,9},{9,8},{10,11... | collective-permute-start | bytes 786440 | tf_op jit(solution)/shard_map/ppermute | solution.py:253
  34.3 1.5 %collective-permute-start.15 = (bf16[2,32,2048]{2,1,0:T(8,128)(2,1)S(1)}, bf16[2,32,2048]{2,1,0:T(8,128)(2,1)S(1)}, u32[]{:S(2)}, u32[]{:S(2)}) collective-permute-start(bf16[2,32,2048]{2,1,0:T(8,128)(2,1)S(1)} %collective-permute-done.2.refs_4_), channel_id=1, source_target_pairs={{0,1},{1,0},{2,3},{3,2},{4,5},{5,4},{6,7},{7,6},{8,9},{9,8},{10,11... | collective-permute-start | bytes 786440 | tf_op jit(solution)/shard_map/ppermute | solution.py:253
  34.3 4.0 %collective-permute-start.11 = (bf16[2,32,2048]{2,1,0:T(8,128)(2,1)S(1)}, bf16[2,32,2048]{2,1,0:T(8,128)(2,1)S(1)}, u32[]{:S(2)}, u32[]{:S(2)}) collective-permute-start(bf16[2,32,2048]{2,1,0:T(8,128)(2,1)S(1)} %collective-permute-done.10.refs_14_.refs_6_), channel_id=1, source_target_pairs={{0,1},{1,0},{2,3},{3,2},{4,5},{5,4},{6,7},{7,6},{8,9},{9,8},{10,11... | collective-permute-start | bytes 786440 | tf_op jit(solution)/shard_map/ppermute | solution.py:253
  34.8 3.5 %collective-permute-start.9 = (bf16[2,32,2048]{2,1,0:T(8,128)(2,1)S(1)}, bf16[2,32,2048]{2,1,0:T(8,128)(2,1)S(1)}, u32[]{:S(2)}, u32[]{:S(2)}) collective-permute-start(bf16[2,32,2048]{2,1,0:T(8,128)(2,1)S(1)} %collective-permute-done.8.refs_12_.refs_4_), channel_id=1, source_target_pairs={{0,1},{1,0},{2,3},{3,2},{4,5},{5,4},{6,7},{7,6},{8,9},{9,8},{10,11... | collective-permute-start | bytes 786440 | tf_op jit(solution)/shard_map/ppermute | solution.py:253
  34.9 3.4 %collective-permute-start.7 = (bf16[2,32,2048]{2,1,0:T(8,128)(2,1)S(1)}, bf16[2,32,2048]{2,1,0:T(8,128)(2,1)S(1)}, u32[]{:S(2)}, u32[]{:S(2)}) collective-permute-start(bf16[2,32,2048]{2,1,0:T(8,128)(2,1)S(1)} %collective-permute-done.5.refs_10_.refs_2_), channel_id=1, source_target_pairs={{0,1},{1,0},{2,3},{3,2},{4,5},{5,4},{6,7},{7,6},{8,9},{9,8},{10,11... | collective-permute-start | bytes 786440 | tf_op jit(solution)/shard_map/ppermute | solution.py:253
  37.4 6.2 %collective-permute-start.16 = (bf16[2,256,128]{2,1,0:T(8,128)(2,1)S(1)}, bf16[2,256,128]{2,1,0:T(8,128)(2,1)S(1)}, u32[]{:S(2)}, u32[]{:S(2)}) collective-permute-start(bf16[2,256,128]{2,1,0:T(8,128)(2,1)S(1)} %form_beams.3), channel_id=1, source_target_pairs={{0,2},{1,3},{2,0},{3,1},{4,6},{5,7},{6,4},{7,5},{8,10},{9,11},{10,... | collective-permute-start | bytes 393224 | tf_op jit(solution)/shard_map/ppermute | solution.py:253
  39.6 2.1 %copy-start.2 = (s32[16]{0:T(128)S(1)}, s32[16]{0:T(128)}, u32[]{:S(2)}) copy-start(s32[16]{0:T(128)} %labels.1) | copy-start | bytes 196
  39.6 10.4 %copy-start.3 = (s32[8]{0:T(128)S(1)}, s32[8]{0:T(128)}, u32[]{:S(2)}) copy-start(s32[8]{0:T(128)} %constant.52.clone) | copy-start | bytes 100
  40.3 5.3 %collective-permute-start.17 = (bf16[2,256,128]{2,1,0:T(8,128)(2,1)S(1)}, bf16[2,256,128]{2,1,0:T(8,128)(2,1)S(1)}, u32[]{:S(2)}, u32[]{:S(2)}) collective-permute-start(bf16[2,256,128]{2,1,0:T(8,128)(2,1)S(1)} %form_beams.5), channel_id=1, source_target_pairs={{0,2},{1,3},{2,0},{3,1},{4,6},{5,7},{6,4},{7,5},{8,10},{9,11},{10,... | collective-permute-start | bytes 393224 | tf_op jit(solution)/shard_map/ppermute | solution.py:253
  46.5 10.1 %collective-permute-start.18 = (bf16[2,320,128]{2,1,0:T(8,128)(2,1)S(1)}, bf16[2,320,128]{2,1,0:T(8,128)(2,1)S(1)}, u32[]{:S(2)}, u32[]{:S(2)}) collective-permute-start(bf16[2,320,128]{2,1,0:T(8,128)(2,1)S(1)} %get-tuple-element.54), channel_id=1, source_target_pairs={{0,4},{1,5},{2,6},{3,7},{4,0},{5,1},{6,2},{7,3},{8,12},{9,13},{10,... | collective-permute-start | bytes 491528 | tf_op jit(solution)/shard_map/ppermute | solution.py:253
  48.9 7.6 %collective-permute-start.21 = (bf16[2,320,128]{2,1,0:T(8,128)(2,1)S(1)}, bf16[2,320,128]{2,1,0:T(8,128)(2,1)S(1)}, u32[]{:S(2)}, u32[]{:S(2)}) collective-permute-start(bf16[2,320,128]{2,1,0:T(8,128)(2,1)S(1)} %get-tuple-element.58), channel_id=1, source_target_pairs={{0,2},{1,3},{2,0},{3,1},{4,6},{5,7},{6,4},{7,5},{8,10},{9,11},{10,... | collective-permute-start | bytes 491528 | tf_op jit(solution)/shard_map/ppermute | solution.py:253
  49.9 1.4 %collective-permute-start.19 = (bf16[2,320,128]{2,1,0:T(8,128)(2,1)S(1)}, bf16[2,320,128]{2,1,0:T(8,128)(2,1)S(1)}, u32[]{:S(2)}, u32[]{:S(2)}) collective-permute-start(bf16[2,320,128]{2,1,0:T(8,128)(2,1)S(1)} %get-tuple-element.55.refs_0_), channel_id=1, source_target_pairs={{0,1},{1,0},{2,3},{3,2},{4,5},{5,4},{6,7},{7,6},{8,9},{9,8},{10,11... | collective-permute-start | bytes 491528 | tf_op jit(solution)/shard_map/ppermute | solution.py:253
  56.5 7.8 %collective-permute-start.23 = (bf16[2,320,128]{2,1,0:T(8,128)(2,1)S(1)}, bf16[2,320,128]{2,1,0:T(8,128)(2,1)S(1)}, u32[]{:S(2)}, u32[]{:S(2)}) collective-permute-start(bf16[2,320,128]{2,1,0:T(8,128)(2,1)S(1)} %collective-permute-done.18.refs_1_), channel_id=1, source_target_pairs={{0,1},{1,0},{2,3},{3,2},{4,5},{5,4},{6,7},{7,6},{8,9},{9,8},{10,11... | collective-permute-start | bytes 491528 | tf_op jit(solution)/shard_map/ppermute | solution.py:253
  56.5 7.8 %collective-permute-start.22 = (bf16[2,320,128]{2,1,0:T(8,128)(2,1)S(1)}, bf16[2,320,128]{2,1,0:T(8,128)(2,1)S(1)}, u32[]{:S(2)}, u32[]{:S(2)}) collective-permute-start(bf16[2,320,128]{2,1,0:T(8,128)(2,1)S(1)} %collective-permute-done.21.refs_0_), channel_id=1, source_target_pairs={{0,1},{1,0},{2,3},{3,2},{4,5},{5,4},{6,7},{7,6},{8,9},{9,8},{10,11... | collective-permute-start | bytes 491528 | tf_op jit(solution)/shard_map/ppermute | solution.py:253
  57.1 11.8 %collective-permute-start.20 = (bf16[2,320,128]{2,1,0:T(8,128)(2,1)S(1)}, bf16[2,320,128]{2,1,0:T(8,128)(2,1)S(1)}, u32[]{:S(2)}, u32[]{:S(2)}) collective-permute-start(bf16[2,320,128]{2,1,0:T(8,128)(2,1)S(1)} %get-tuple-element.57), channel_id=1, source_target_pairs={{0,6},{1,7},{2,4},{3,5},{4,2},{5,3},{6,0},{7,1},{8,14},{9,15},{10,... | collective-permute-start | bytes 491528 | tf_op jit(solution)/shard_map/ppermute | solution.py:253
  68.9 1.5 %collective-permute-start.24 = (bf16[2,320,128]{2,1,0:T(8,128)(2,1)S(1)}, bf16[2,320,128]{2,1,0:T(8,128)(2,1)S(1)}, u32[]{:S(2)}, u32[]{:S(2)}) collective-permute-start(bf16[2,320,128]{2,1,0:T(8,128)(2,1)S(1)} %collective-permute-done.20.refs_0_), channel_id=1, source_target_pairs={{0,1},{1,0},{2,3},{3,2},{4,5},{5,4},{6,7},{7,6},{8,9},{9,8},{10,11... | collective-permute-start | bytes 491528 | tf_op jit(solution)/shard_map/ppermute | solution.py:253
